TPU v7x, 32 devices: a whole 2x2x4 slice. The times are simulated.
32 devices in a mesh: shard: 8 (over z, y), ctx: 2 (over x), tp: 2 (over core).
Axes of the slice: x: 2, y: 2, z: 4, core: 2. Of those that a mesh axis runs over, the one named last changes fastest.
Arguments:
- hidden: bfloat16 [8, 2048, 768], P('shard', 'ctx'), may hold values from -6 to 6
- block_order: int32 [4], replicated, may hold values from 0 to 3, each once
- ln1_gain: bfloat16 [768], P('shard'), may hold values from 0.099609375 to 1.8984375
- ln1_bias: bfloat16 [768], P('shard'), may hold values from -1.5 to 1.5
- ln2_gain: bfloat16 [768], P('shard'), may hold values from 0.099609375 to 1.8984375
- ln2_bias: bfloat16 [768], P('shard'), may hold values from -1.5 to 1.5
- q_weight: bfloat16 [768, 768], P('shard', 'tp'), may hold values from -0.21875 to 0.21875
- kv_weight: bfloat16 [768, 128], P('shard'), may hold values from -0.21875 to 0.21875
- o_weight: bfloat16 [768, 768], P('shard', 'tp'), may hold values from -1.25 to 1.25
- up_weight: bfloat16 [768, 3072], P('shard', 'tp'), may hold values from -0.21875 to 0.21875
- down_weight: bfloat16 [768, 3072], P('shard', 'tp'), may hold values from -0.109375 to 0.109375
- cotangent: bfloat16 [8, 2048, 768], P('shard', 'ctx'), may hold values from -6 to 6
Outputs:
- out_tokens: bfloat16 [8, 2048, 768], P('shard', 'ctx')
- keys_out: bfloat16 [8, 2048, 64], P('shard', 'ctx')
- values_out: bfloat16 [8, 2048, 64], P('shard', 'ctx')
- hidden_grad: float32 [8, 2048, 768], P('shard', 'ctx')
- ln1_gain_grad: float32 [768], P('shard')
- ln1_bias_grad: float32 [768], P('shard')
- ln2_gain_grad: float32 [768], P('shard')
- ln2_bias_grad: float32 [768], P('shard')
- q_weight_grad: float32 [768, 768], P('shard', 'tp')
- kv_weight_grad: float32 [768, 128], P('shard')
- o_weight_grad: float32 [768, 768], P('shard', 'tp')
- up_weight_grad: float32 [768, 3072], P('shard', 'tp')
- down_weight_grad: float32 [768, 3072], P('shard', 'tp')
Inputs may be any that keep to these rules, and one draw needn't show every extreme that they name: `block_order`: each of the 4 values appears once.
All inputs are finite; a program needn't handle non-finite values.
Results may differ from a plain program's by a relative error of at most 0.017.
Values may be sent and summed in bfloat16 or wider, within the bound.
A program may use at most 256 MiB of HBM per device.

v0:
```python
import jax
import jax.numpy as jnp
from jax import lax
from jax.sharding import PartitionSpec as P

ROT = 16


def layer_norm(values, gain, shift):
    center = values - jnp.mean(values, axis=-1, keepdims=True)
    spread = jnp.mean(center * center, axis=-1, keepdims=True)
    return center * lax.rsqrt(spread + 1e-05) * gain + shift


def gelu_exact(values):
    return jax.nn.gelu(values, approximate=False)


def rotate(tensor, places, sign):
    half_rot = ROT // 2
    freq = jnp.power(10000.0, -2.0 * jnp.arange(half_rot, dtype=jnp.float32) / ROT)
    angle = places.astype(jnp.float32)[:, None] * freq[None, :]
    cosine = jnp.cos(angle)[:, None, :]
    sine = sign * jnp.sin(angle)[:, None, :]
    first = tensor[..., :half_rot]
    second = tensor[..., half_rot:ROT]
    return jnp.concatenate(
        [first * cosine - second * sine, second * cosine + first * sine, tensor[..., ROT:]], axis=-1
    )


def tok_positions(block_order, rows, half_block):
    index = rows // half_block
    table = jnp.arange(block_order.shape[0], dtype=jnp.int32)
    picked = jnp.sum(jnp.where(index[:, None] == table[None, :], block_order[None, :], 0), axis=1)
    return picked * half_block + rows % half_block


def right_product(left, right):
    return lax.dot_general(
        left, right, (((1,), (1,)), ((), ())), preferred_element_type=jnp.float32
    )


def left_product(left, right):
    return lax.dot_general(
        left, right, (((0,), (0,)), ((), ())), preferred_element_type=jnp.float32
    )


def on_device(
    hidden,
    block_order,
    ln1_gain,
    ln1_bias,
    ln2_gain,
    ln2_bias,
    q_weight,
    kv_weight,
    o_weight,
    up_weight,
    down_weight,
    cotangent,
):
    seqs, span, width = hidden.shape
    half_block = span // 2
    head_size = kv_weight.shape[1] // 2
    local_heads = q_weight.shape[1] // head_size
    row_count = seqs * span
    query_rows = span * local_heads
    scale = head_size ** (-0.5)
    gathered = (
        lax.all_gather(ln1_gain, "shard", axis=0, tiled=True),
        lax.all_gather(ln1_bias, "shard", axis=0, tiled=True),
        lax.all_gather(ln2_gain, "shard", axis=0, tiled=True),
        lax.all_gather(ln2_bias, "shard", axis=0, tiled=True),
        lax.all_gather(q_weight, "shard", axis=0, tiled=True),
        lax.all_gather(kv_weight, "shard", axis=0, tiled=True),
        lax.all_gather(o_weight, "shard", axis=0, tiled=True),
        lax.all_gather(up_weight, "shard", axis=0, tiled=True),
        lax.all_gather(down_weight, "shard", axis=0, tiled=True),
    )
    gain_attn, bias_attn, gain_ffn, bias_ffn, w_query, w_keyval, w_output, w_up, w_down = gathered
    offset = lax.axis_index("ctx") * span
    query_places = tok_positions(
        block_order, offset + jnp.arange(span, dtype=jnp.int32), half_block
    )
    row_places = jnp.repeat(query_places, local_heads)
    tokens = hidden.astype(jnp.float32).reshape(row_count, width)
    norm_attn = layer_norm(
        tokens, gain_attn.astype(jnp.float32), bias_attn.astype(jnp.float32)
    ).astype(jnp.bfloat16)
    norm_ffn = layer_norm(
        tokens, gain_ffn.astype(jnp.float32), bias_ffn.astype(jnp.float32)
    ).astype(jnp.bfloat16)
    query_pre = jnp.dot(norm_attn, w_query, preferred_element_type=jnp.float32).reshape(
        seqs, span, local_heads, head_size
    )
    queries = (
        rotate(query_pre, query_places, 1.0)
        .astype(jnp.bfloat16)
        .reshape(seqs, query_rows, head_size)
    )
    keyval_pre = jnp.dot(norm_attn, w_keyval, preferred_element_type=jnp.float32).reshape(
        seqs, span, 2 * head_size
    )
    keys = rotate(keyval_pre[:, :, None, :head_size], query_places, 1.0)[:, :, 0, :].astype(
        jnp.bfloat16
    )
    values = keyval_pre[:, :, head_size:].astype(jnp.bfloat16)
    start_state = (
        jnp.full((seqs, query_rows), -1e30, jnp.float32),
        jnp.zeros((seqs, query_rows), jnp.float32),
        jnp.zeros((seqs, query_rows, head_size), jnp.float32),
    )
    key_piece = lax.all_gather(keys, "ctx", axis=1, tiled=True)
    value_piece = lax.all_gather(values, "ctx", axis=1, tiled=True)
    count = key_piece.shape[1]
    key_places = tok_positions(block_order, jnp.arange(count, dtype=jnp.int32), half_block)
    visible = key_places[None, :] <= row_places[:, None]

    def one_block(args):
        peak, total, accum, query_block, key_block, value_block = args
        scores = (
            jnp.einsum("qd,kd->qk", query_block, key_block, preferred_element_type=jnp.float32)
            * scale
        )
        scores = jnp.where(visible, scores, -1e30)
        new_peak = jnp.maximum(peak, jnp.max(scores, axis=1))
        factor = jnp.exp(peak - new_peak)
        weights = jnp.where(visible, jnp.exp(scores - new_peak[:, None]), 0.0)
        total = total * factor + jnp.sum(weights, axis=1)
        accum = accum * factor[:, None] + jnp.einsum(
            "qk,kd->qd",
            weights.astype(jnp.bfloat16),
            value_block,
            preferred_element_type=jnp.float32,
        )
        return (new_peak, total, accum)

    peak, total, accum = lax.map(
        one_block, (start_state[0], start_state[1], start_state[2], queries, key_piece, value_piece)
    )
    attended = (
        (accum / total[:, :, None]).astype(jnp.bfloat16).reshape(row_count, local_heads * head_size)
    )
    log_total = peak + jnp.log(total)
    hidden_pre = jnp.dot(norm_ffn, w_up, preferred_element_type=jnp.float32)
    activation_full, gelu_pull = jax.vjp(gelu_exact, hidden_pre)
    activation = activation_full.astype(jnp.bfloat16)
    branch = right_product(attended, w_output) + right_product(activation, w_down)
    branch = lax.psum(branch.astype(jnp.bfloat16), "tp").astype(jnp.float32)
    mixed = (tokens + branch).astype(jnp.bfloat16).reshape(seqs, span, width)
    regathered = (
        lax.all_gather(ln1_gain, "shard", axis=0, tiled=True),
        lax.all_gather(ln2_gain, "shard", axis=0, tiled=True),
        lax.all_gather(q_weight, "shard", axis=0, tiled=True),
        lax.all_gather(kv_weight, "shard", axis=0, tiled=True),
        lax.all_gather(o_weight, "shard", axis=0, tiled=True),
        lax.all_gather(up_weight, "shard", axis=0, tiled=True),
        lax.all_gather(down_weight, "shard", axis=0, tiled=True),
    )
    gain_attn, gain_ffn, w_query, w_keyval, w_output, w_up, w_down = regathered
    grad_out = cotangent.reshape(row_count, width)
    grad_attended = (
        jnp.dot(grad_out, w_output, preferred_element_type=jnp.float32)
        .astype(jnp.bfloat16)
        .reshape(seqs, query_rows, head_size)
    )
    grad_activation = jnp.dot(grad_out, w_down, preferred_element_type=jnp.float32)
    grad_hidden = gelu_pull(grad_activation)[0].astype(jnp.bfloat16)
    grad_w_output = left_product(grad_out, attended)
    grad_w_down = left_product(grad_out, activation)
    grad_w_up = left_product(norm_ffn, grad_hidden)
    grad_norm_ffn = right_product(grad_hidden, w_up)
    all_keys, all_values = (
        lax.all_gather(keys, "ctx", axis=1, tiled=True),
        lax.all_gather(values, "ctx", axis=1, tiled=True),
    )
    key_count = all_keys.shape[1]
    key_places = tok_positions(block_order, jnp.arange(key_count, dtype=jnp.int32), half_block)
    visible_all = key_places[None, :] <= row_places[:, None]

    def backward_one(args):
        query_block, key_block, value_block, grad_block, log_block = args
        scores = (
            jnp.einsum("qd,kd->qk", query_block, key_block, preferred_element_type=jnp.float32)
            * scale
        )
        probs = jnp.where(visible_all, jnp.exp(scores - log_block[:, None]), 0.0)
        grad_probs = jnp.einsum(
            "qd,kd->qk", grad_block, value_block, preferred_element_type=jnp.float32
        )
        delta = jnp.sum(probs * grad_probs, axis=1, keepdims=True)
        grad_scores = (probs * (grad_probs - delta)).astype(jnp.bfloat16)
        grad_query = (
            jnp.einsum("qk,kd->qd", grad_scores, key_block, preferred_element_type=jnp.float32)
            * scale
        )
        grad_key = (
            jnp.einsum("qk,qd->kd", grad_scores, query_block, preferred_element_type=jnp.float32)
            * scale
        )
        grad_value = jnp.einsum(
            "qk,qd->kd", probs.astype(jnp.bfloat16), grad_block, preferred_element_type=jnp.float32
        )
        return (grad_query, jnp.concatenate([grad_key, grad_value], axis=1))

    grad_queries, grad_keyvals = lax.map(
        backward_one, (queries, all_keys, all_values, grad_attended, log_total)
    )
    grad_keyvals = lax.psum_scatter(
        grad_keyvals.astype(jnp.bfloat16), "ctx", scatter_dimension=1, tiled=True
    ).astype(jnp.float32)
    grad_keyvals = lax.psum(grad_keyvals.astype(jnp.bfloat16), "tp").astype(jnp.float32)
    grad_key_pre = rotate(grad_keyvals[:, :, None, :head_size], query_places, -1.0)[:, :, 0, :]
    grad_keyval_pre = (
        jnp.concatenate([grad_key_pre, grad_keyvals[:, :, head_size:]], axis=2)
        .astype(jnp.bfloat16)
        .reshape(row_count, 2 * head_size)
    )
    grad_query_pre = (
        rotate(grad_queries.reshape(seqs, span, local_heads, head_size), query_places, -1.0)
        .astype(jnp.bfloat16)
        .reshape(row_count, local_heads * head_size)
    )
    grad_w_query = left_product(norm_attn, grad_query_pre)
    grad_w_keyval = left_product(norm_attn, grad_keyval_pre)
    grad_norm_attn = right_product(grad_query_pre, w_query)
    shared_term = right_product(grad_keyval_pre, w_keyval)
    zero_shift = jnp.zeros((width,), jnp.float32)
    attn_pull = jax.vjp(layer_norm, tokens, gain_attn.astype(jnp.float32), zero_shift)[1]
    ffn_pull = jax.vjp(layer_norm, tokens, gain_ffn.astype(jnp.float32), zero_shift)[1]
    grad_norm_attn, grad_norm_ffn = (
        lax.psum(grad_norm_attn.astype(jnp.bfloat16), "tp").astype(jnp.float32),
        lax.psum(grad_norm_ffn.astype(jnp.bfloat16), "tp").astype(jnp.float32),
    )
    grad_norm_attn = grad_norm_attn + shared_term
    grad_tok_attn, grad_gain_attn, grad_shift_attn = attn_pull(grad_norm_attn)
    grad_tok_ffn, grad_gain_ffn, grad_shift_ffn = ffn_pull(grad_norm_ffn)
    grad_tok_norms = grad_tok_attn + grad_tok_ffn
    grad_tokens = (grad_out.astype(jnp.float32) + grad_tok_norms).reshape(seqs, span, width)
    grads = (
        grad_gain_attn,
        grad_shift_attn,
        grad_gain_ffn,
        grad_shift_ffn,
        grad_w_query,
        grad_w_keyval,
        grad_w_output,
        grad_w_up,
        grad_w_down,
    )
    owned = (
        lax.psum_scatter(
            grads[0].astype(jnp.bfloat16), "shard", scatter_dimension=0, tiled=True
        ).astype(jnp.float32),
        lax.psum_scatter(
            grads[1].astype(jnp.bfloat16), "shard", scatter_dimension=0, tiled=True
        ).astype(jnp.float32),
        lax.psum_scatter(
            grads[2].astype(jnp.bfloat16), "shard", scatter_dimension=0, tiled=True
        ).astype(jnp.float32),
        lax.psum_scatter(
            grads[3].astype(jnp.bfloat16), "shard", scatter_dimension=0, tiled=True
        ).astype(jnp.float32),
        lax.psum_scatter(
            grads[4].astype(jnp.bfloat16), "shard", scatter_dimension=0, tiled=True
        ).astype(jnp.float32),
        lax.psum_scatter(
            grads[5].astype(jnp.bfloat16), "shard", scatter_dimension=0, tiled=True
        ).astype(jnp.float32),
        lax.psum_scatter(
            grads[6].astype(jnp.bfloat16), "shard", scatter_dimension=0, tiled=True
        ).astype(jnp.float32),
        lax.psum_scatter(
            grads[7].astype(jnp.bfloat16), "shard", scatter_dimension=0, tiled=True
        ).astype(jnp.float32),
        lax.psum_scatter(
            grads[8].astype(jnp.bfloat16), "shard", scatter_dimension=0, tiled=True
        ).astype(jnp.float32),
    )
    owned = (
        lax.psum(owned[0].astype(jnp.bfloat16), "ctx").astype(jnp.float32),
        lax.psum(owned[1].astype(jnp.bfloat16), "ctx").astype(jnp.float32),
        lax.psum(owned[2].astype(jnp.bfloat16), "ctx").astype(jnp.float32),
        lax.psum(owned[3].astype(jnp.bfloat16), "ctx").astype(jnp.float32),
        lax.psum(owned[4].astype(jnp.bfloat16), "ctx").astype(jnp.float32),
        lax.psum(owned[5].astype(jnp.bfloat16), "ctx").astype(jnp.float32),
        lax.psum(owned[6].astype(jnp.bfloat16), "ctx").astype(jnp.float32),
        lax.psum(owned[7].astype(jnp.bfloat16), "ctx").astype(jnp.float32),
        lax.psum(owned[8].astype(jnp.bfloat16), "ctx").astype(jnp.float32),
    )
    return (
        mixed,
        keys,
        values,
        grad_tokens,
        owned[0],
        owned[1],
        owned[2],
        owned[3],
        owned[4],
        owned[5],
        owned[6],
        owned[7],
        owned[8],
    )


def solution(mesh):
    return jax.shard_map(
        on_device,
        mesh=mesh,
        in_specs=(
            P("shard", "ctx", None),
            P(),
            P("shard"),
            P("shard"),
            P("shard"),
            P("shard"),
            P("shard", "tp"),
            P("shard", None),
            P("shard", "tp"),
            P("shard", "tp"),
            P("shard", "tp"),
            P("shard", "ctx", None),
        ),
        out_specs=(
            P("shard", "ctx", None),
            P("shard", "ctx", None),
            P("shard", "ctx", None),
            P("shard", "ctx", None),
            P("shard"),
            P("shard"),
            P("shard"),
            P("shard"),
            P("shard", "tp"),
            P("shard", None),
            P("shard", "tp"),
            P("shard", "tp"),
            P("shard", "tp"),
        ),
        check_vma=False,
    )
```

profile of v0, /device:TPU:0, one launch (start us, length us, event | category | flops | bytes accessed | tf_op | source)
XLA Modules:
  0.0 789.7 jit_solution(5737130723716735342)
XLA Ops:
  15.0 24.5 %all-reduce.9 = (bf16[768]{0:T(1024)(128)(2,1)S(1)}, bf16[768]{0:T(1024)(128)(2,1)S(1)}, bf16[768]{0:T(1024)(128)(2,1)}, bf16[768]{0:T(1024)(128)(2,1)}) all-reduce(bf16[768]{0:T(1024)(128)(2,1)S(1)} %dynamic-update-slice.1, bf16[768]{0:T(1024)(128)(2,1)S(1)} %dynamic-update-slice, ...), channel_id=1, replica_groups=mesh['shard'=8,'ctx'=2,'tp'=2] {'shard'}, use_global_device_ids=true, to_apply=%add.1 | all-reduce | flops 3072 | bytes 12288
  42.4 31.8 %all_gather.45 = bf16[768,128]{1,0:T(8,128)(2,1)S(1)} all-gather(bf16[96,128]{1,0:T(8,128)(2,1)S(1)} %copy-done.37), channel_id=1, replica_groups=mesh['shard'=8,'ctx'=2,'tp'=2] {'shard'}, dimensions={0}, use_global_device_ids=true | all-gather | bytes 221184 | tf_op jit(solution)/shard_map/all_gather | solution.py:78
  78.7 5.6 all-gather
  84.3 33.1 %all_gather.44 = bf16[768,384]{1,0:T(8,128)(2,1)S(1)} all-gather(bf16[96,384]{1,0:T(8,128)(2,1)S(1)} %copy-done.27), channel_id=1, replica_groups=mesh['shard'=8,'ctx'=2,'tp'=2] {'shard'}, dimensions={0}, use_global_device_ids=true | all-gather | bytes 663552 | tf_op jit(solution)/shard_map/all_gather | solution.py:77
  129.3 22.1 %fusion = (f32[6144]{0:T(1024)S(1)}, f32[6144,2048]{0,1:T(8,128)}) fusion(s32[6144]{0:T(1024)S(1)} %le.9, s32[2048]{0:T(1024)S(1)} %fusion.117, bf16[1,2048,1,64]{1,3,2,0:T(8,128)(2,1)S(1)} %all-gather, bf16[6144,48]{1,0:T(8,128)(2,1)} %concatenate.61, bf16[6144,8]{1,0:T(8,128)(2,1)} %reshape.585, bf16[6144,8]{1,0:T(8,128)(2,1)} %reshape.584), kind=kOutput, calls=%fused_computation.5 | convolution fusion | flops 1663297536 | bytes 51437568 | tf_op jit(solution)/shard_map/while/body/eval_jaxpr/qd,kd->qk/dot_general | solution.py:125
  152.1 23.6 %fusion.1 = f32[6144]{0:T(1024)S(1)} fusion(f32[6144,2048]{0,1:T(8,128)} %get-tuple-element.192, f32[6144]{0:T(1024)S(1)} %broadcast_maximum_fusion, s32[6144]{0:T(1024)S(1)} %le.9, s32[2048]{0:T(1024)S(1)} %fusion.117), kind=kLoop, calls=%fused_computation.6 | loop fusion | flops 75491328 | bytes 50413568 | tf_op jit(solution)/shard_map/while/body/eval_jaxpr/reduce_sum | solution.py:132
  176.3 5.6 all_gather.47
  181.9 31.5 %all_gather.48 = bf16[768,384]{1,0:T(8,128)(2,1)S(1)} all-gather(bf16[96,384]{1,0:T(8,128)(2,1)S(1)} %copy-done.28), channel_id=1, replica_groups=mesh['shard'=8,'ctx'=2,'tp'=2] {'shard'}, dimensions={0}, use_global_device_ids=true | all-gather | bytes 663552 | tf_op jit(solution)/shard_map/all_gather | solution.py:79
  216.5 33.6 %multiply_reduce_fusion = (f32[6144]{0:T(1024)S(1)}, f32[6144,2048]{0,1:T(8,128)}) fusion(f32[6144]{0:T(1024)S(1)} %get-tuple-element.180, f32[6144,2048]{0,1:T(8,128)} %get-tuple-element.192, s32[6144]{0:T(1024)S(1)} %le.9, s32[2048]{0:T(1024)S(1)} %fusion.117, bf16[6144,64]{1,0:T(8,128)(2,1)S(1)} %squeeze.42, bf16[1,2048,64]{1,2,0:T(8,128)(2,1)S(1)} %all_gather.47), kind=kOutput, calls=%fused_computation.4 | convolution fusion | flops 1686104064 | bytes 101793792 | tf_op jit(solution)/shard_map/while/body/eval_jaxpr/qd,kd->qk/dot_general | solution.py:191
  250.1 40.5 %multiply_convert_fusion = bf16[6144,2048]{0,1:T(8,128)(2,1)} fusion(f32[6144,2048]{0,1:T(8,128)} %get-tuple-element.194, f32[6144]{0:T(1024)S(1)} %get-tuple-element.193, f32[6144]{0:T(1024)S(1)} %get-tuple-element.180, f32[6144,2048]{0,1:T(8,128)} %get-tuple-element.192, s32[6144]{0:T(1024)S(1)} %le.9, s32[2048]{0:T(1024)S(1)} %fusion.117), kind=kLoop, calls=%fused_computation.3 | loop fusion | flops 88080384 | bytes 125911040 | tf_op jit(solution)/shard_map/while/body/eval_jaxpr/convert_element_type | solution.py:195
  290.6 14.2 %fusion.57 = bf16[1,2048,64]{1,2,0:T(8,128)(2,1)} fusion(bf16[6144,2048]{0,1:T(8,128)(2,1)} %multiply_convert_fusion, bf16[6144,48]{1,0:T(8,128)(2,1)} %concatenate.61, bf16[6144,8]{1,0:T(8,128)(2,1)} %reshape.585, bf16[6144,8]{1,0:T(8,128)(2,1)S(1)} %copy-done.4), kind=kOutput, calls=%fused_computation.75 | convolution fusion | flops 1613234176 | bytes 26214400 | tf_op jit(solution)/shard_map/while/body/eval_jaxpr/qk,qd->kd/dot_general | solution.py:201
  304.8 18.2 %fusion.54 = bf16[1,2048,64]{1,2,0:T(8,128)(2,1)S(1)} fusion(bf16[6144,64]{1,0:T(8,128)(2,1)S(1)} %squeeze.42, f32[6144,2048]{0,1:T(8,128)} %get-tuple-element.192, f32[6144]{0:T(1024)S(1)} %get-tuple-element.180, s32[6144]{0:T(1024)S(1)} %le.9, s32[2048]{0:T(1024)S(1)} %fusion.117), kind=kOutput, calls=%fused_computation.74 | convolution fusion | flops 1673658368 | bytes 51437568 | tf_op jit(solution)/shard_map/while/body/eval_jaxpr/qk,qd->kd/dot_general | solution.py:204
  323.9 12.1 %convolution_multiply_fusion = f32[6144,64]{0,1:T(8,128)} fusion(bf16[6144,2048]{0,1:T(8,128)(2,1)} %multiply_convert_fusion, bf16[1,2048,1,64]{1,3,2,0:T(8,128)(2,1)S(1)} %all-gather), kind=kOutput, calls=%fused_computation.12 | convolution fusion | flops 1611005952 | bytes 27000832 | tf_op jit(solution)/shard_map/while/body/eval_jaxpr/qk,kd->qd/dot_general | solution.py:197
  340.3 8.2 %fusion.144 = (f32[1,1024,6,8]{3,2,1,0:T(8,128)}, f32[1,1024,6,8]{3,2,1,0:T(8,128)}) fusion(f32[1,1024,6,64]{3,2,1,0:T(8,128)} %reshape.559), kind=kLoop, calls=%fused_computation.195 | loop fusion | bytes 786432 | tf_op jit(solution)/shard_map/slice | solution.py:26
  352.4 3.4 copy.92
  357.0 20.4 %fusion.13 = bf16[6144,64]{0,1:T(8,128)(2,1)} fusion(f32[6144,2048]{0,1:T(8,128)} %get-tuple-element.192, f32[6144]{0:T(1024)S(1)} %copy-done.26, s32[6144]{0:T(1024)S(1)} %copy-done.19, s32[2048]{0:T(1024)S(1)} %fusion.117, f32[6144]{0:T(1024)S(1)} %copy-done.38, f32[6144]{0:T(1024)S(1)} %copy-done.39, bf16[1,2048,64]{1,2,0:T(8,128)(2,1)S(1)} %copy-done.12), kind=kOutput, calls=%fused_computation.15 | convolution fusion | flops 1687289856 | bytes 51486720 | tf_op jit(solution)/shard_map/while/body/eval_jaxpr/qk,kd->qd/dot_general | solution.py:133
  385.4 19.7 %multiply_convert_fusion.1 = (bf16[1024,1536]{1,0:T(8,128)(2,1)}, f32[1024,1536]{1,0:T(8,128)}, f32[1024,1536]{1,0:T(8,128)}) fusion(bf16[768,1536]{1,0:T(8,128)(2,1)} %all-gather.4.cloned.1.call-done, bf16[1,1024,768]{2,1,0:T(8,128)(2,1)S(1)} %copy-done.2, f32[768]{0:T(1024)S(1)} %convert_element_type.227, f32[768]{0:T(1024)S(1)} %convert_element_type.226, ...), kind=kOutput, calls=%fused_computation.18 | convolution fusion | flops 2522873856 | bytes 19675136 | tf_op jit(solution)/shard_map/dot_general | solution.py:148
  405.1 9.9 %add_convert_fusion = bf16[1024,1536]{1,0:T(8,128)(2,1)S(1)} fusion(f32[1024,1536]{1,0:T(8,128)} %get-tuple-element.162, f32[1024,1536]{1,0:T(8,128)} %get-tuple-element.190, bf16[768,1536]{1,0:T(8,128)(2,1)} %all-gather.6.cloned.1.call-done, bf16[1,1024,768]{2,1,0:T(8,128)(2,1)} %param.23), kind=kOutput, calls=%fused_computation.17 | convolution fusion | flops 2437939200 | bytes 19660800 | tf_op jit(solution)/shard_map/dot_general | solution.py:170
  419.8 3.7 convolution_convert_fusion.3
  427.2 6.5 fusion.49
  433.8 4.3 copy.87
  440.5 6.5 convolution_convert_fusion.1
  455.3 33.0 %reduce-scatter.19.cloned.1.call-done = bf16[96,384]{1,0:T(8,128)(2,1)} async-done(((bf16[768,384]{1,0:T(8,128)(2,1)}), bf16[96,384]{1,0:T(8,128)(2,1)}) %reduce-scatter.19.cloned.1.call-update) | async-done | bytes 73744
  490.0 70.9 %reduce-scatter.21.cloned.1.call-done = bf16[96,1536]{1,0:T(8,128)(2,1)} async-done(((bf16[768,1536]{1,0:T(8,128)(2,1)}), bf16[96,1536]{1,0:T(8,128)(2,1)}) %reduce-scatter.21.cloned.1.call-update) | async-done | bytes 294928
  562.7 63.8 %reduce-scatter.13.cloned.1.call-done = bf16[96,384]{1,0:T(8,128)(2,1)} async-done(((bf16[768,384]{1,0:T(8,128)(2,1)}), bf16[96,384]{1,0:T(8,128)(2,1)}) %reduce-scatter.13.cloned.1.call-update) | async-done | bytes 73744 | tf_op jit(solution)/shard_map/reduce_scatter | solution.py:267
  626.5 72.0 %reduce-scatter.17.cloned.1.call-done = bf16[96,1536]{1,0:T(8,128)(2,1)} async-done(((bf16[768,1536]{1,0:T(8,128)(2,1)}), bf16[96,1536]{1,0:T(8,128)(2,1)}) %reduce-scatter.17.cloned.1.call-update) | async-done | bytes 294928 | tf_op jit(solution)/shard_map/reduce_scatter | solution.py:276
  698.5 4.4 fusion.140
  703.2 4.2 fusion.40
  707.5 19.5 %all-reduce.8 = (bf16[768]{0:T(1024)(128)(2,1)S(1)}, bf16[768]{0:T(1024)(128)(2,1)S(1)}, bf16[768]{0:T(1024)(128)(2,1)S(1)}, bf16[768]{0:T(1024)(128)(2,1)S(1)}) all-reduce(bf16[768]{0:T(1024)(128)(2,1)S(1)} %get-tuple-element.136, ...), channel_id=4, replica_groups=mesh['shard'=8,'ctx'=2,'tp'=2] {'shard'}, use_global_device_ids=true, to_apply=%region_17.18.clone | all-reduce | flops 3072 | bytes 12288
  727.3 5.6 add_bitcast_fusion
  732.9 30.1 %reduce-scatter.15.cloned.1.call-done = bf16[96,128]{1,0:T(8,128)(2,1)} async-done(((bf16[768,128]{1,0:T(8,128)(2,1)}), bf16[96,128]{1,0:T(8,128)(2,1)}) %reduce-scatter.15.cloned.1.call-update) | async-done | bytes 24592 | tf_op jit(solution)/shard_map/reduce_scatter | solution.py:270
  763.0 9.0 %all-reduce.11 = (bf16[96]{0:T(256)(128)(2,1)S(1)}, bf16[96]{0:T(256)(128)(2,1)S(1)}, bf16[96]{0:T(256)(128)(2,1)S(1)}, bf16[96]{0:T(256)(128)(2,1)S(1)}, bf16[96,128]{1,0:T(8,128)(2,1)S(1)}) all-reduce(bf16[96]{0:T(256)(128)(2,1)S(1)} %dynamic-slice.5, ...), channel_id=1, replica_groups=mesh['shard'=8,'ctx'=2,'tp'=2] {'ctx'}, use_global_device_ids=true, to_apply=%region_18.19 | all-reduce | flops 12672 | bytes 50688 | tf_op jit(solution)/shard_map/psum | solution.py:284
  (212 shorter events, 79.9 us)
Async XLA Ops:
  8.0 33.2 %copy-start.1 = (bf16[1,1024,768]{2,1,0:T(8,128)(2,1)S(1)}, bf16[1,1024,768]{2,1,0:T(8,128)(2,1)}, u32[]{:S(2)}) copy-start(bf16[1,1024,768]{2,1,0:T(8,128)(2,1)} %param.12) | copy-start | bytes 4718596
  8.0 34.4 %copy-start.37 = (bf16[96,128]{1,0:T(8,128)(2,1)S(1)}, bf16[96,128]{1,0:T(8,128)(2,1)}, u32[]{:S(2)}) copy-start(bf16[96,128]{1,0:T(8,128)(2,1)} %param.19) | copy-start | bytes 73732
  8.0 377.4 %all-gather.4.cloned.1.call-start = ((), (), s32[]{:S(2)}) async-start(), calls=%async_computation.6 | async-start | bytes 2654208 | tf_op jit(solution)/shard_map/all_gather | solution.py:80
  8.8 396.3 %all-gather.6.cloned.1.call-start = ((), (), s32[]{:S(2)}) async-start(), calls=%async_computation.7 | async-start | bytes 2654208 | tf_op jit(solution)/shard_map/all_gather | solution.py:81
  9.5 414.0 %reduce-scatter.11.cloned.1.call-start = ((), (), s32[]{:S(2)}) async-start(), calls=%async_computation.8 | async-start | bytes 786432 | tf_op jit(solution)/shard_map/reduce_scatter | solution.py:212
  9.6 67.5 %copy-start.42 = (f32[8]{0:T(128)}, f32[8]{0:T(128)S(1)}, u32[]{:S(2)}) copy-start(f32[8]{0:T(128)S(1)} %multiply_power_fusion) | copy-start | bytes 100
  39.5 78.2 %copy-start.31 = (f32[768]{0:T(1024)}, f32[768]{0:T(1024)S(1)}, u32[]{:S(2)}) copy-start(f32[768]{0:T(1024)S(1)} %convert_element_type.218) | copy-start | bytes 9220
  39.5 78.2 %copy-start.40 = (f32[768]{0:T(1024)}, f32[768]{0:T(1024)S(1)}, u32[]{:S(2)}) copy-start(f32[768]{0:T(1024)S(1)} %convert_element_type.219) | copy-start | bytes 9220
  41.2 76.5 %copy-start.23 = (f32[1024]{0:T(1024)}, f32[1024]{0:T(1024)S(1)}, u32[]{:S(2)}) copy-start(f32[1024]{0:T(1024)S(1)} %broadcast_multiply_fusion.1) | copy-start | bytes 12292
  41.8 35.0 %copy-start.45 = (s32[4]{0:T(128)S(1)}, s32[4]{0:T(128)}, u32[]{:S(2)}) copy-start(s32[4]{0:T(128)} %param.13) | copy-start | bytes 52
  42.4 75.3 %copy-start.33 = (f32[1024]{0:T(1024)}, f32[1024]{0:T(1024)S(1)}, u32[]{:S(2)}) copy-start(f32[1024]{0:T(1024)S(1)} %fusion.125) | copy-start | bytes 12292
  74.2 10.1 %copy-start.27 = (bf16[96,384]{1,0:T(8,128)(2,1)S(1)}, bf16[96,384]{1,0:T(8,128)(2,1)}, u32[]{:S(2)}) copy-start(bf16[96,384]{1,0:T(8,128)(2,1)} %param.18) | copy-start | bytes 221188
  76.9 41.8 %copy-start.29 = (f32[1024]{0:T(1024)}, f32[1024]{0:T(1024)S(1)}, u32[]{:S(2)}) copy-start(f32[1024]{0:T(1024)S(1)} %get-tuple-element.159) | copy-start | bytes 12292
  77.9 40.9 %copy-start.21 = (f32[1024,8]{0,1:T(8,128)}, f32[1024,8]{0,1:T(8,128)S(1)}, u32[]{:S(2)}) copy-start(f32[1024,8]{0,1:T(8,128)S(1)} %get-tuple-element.185) | copy-start | bytes 98308
  78.0 98.3 %copy-start.20 = (bf16[1,1024,64]{1,2,0:T(8,128)(2,1)}, bf16[1,1024,64]{1,2,0:T(8,128)(2,1)S(1)}, u32[]{:S(2)}) copy-start(bf16[1,1024,64]{1,2,0:T(8,128)(2,1)S(1)} %slice.107) | copy-start | bytes 393220
  129.2 175.5 %copy-start.18 = (s32[6144]{0:T(1024)}, s32[6144]{0:T(1024)S(1)}, u32[]{:S(2)}) copy-start(s32[6144]{0:T(1024)S(1)} %le.9) | copy-start | bytes 73732
  152.1 29.9 %copy-start.28 = (bf16[96,384]{1,0:T(8,128)(2,1)S(1)}, bf16[96,384]{1,0:T(8,128)(2,1)}, u32[]{:S(2)}) copy-start(bf16[96,384]{1,0:T(8,128)(2,1)} %param.20) | copy-start | bytes 221188
  152.1 62.2 %copy-start.5 = (bf16[1,1024,768]{2,1,0:T(8,128)(2,1)S(1)}, bf16[1,1024,768]{2,1,0:T(8,128)(2,1)}, u32[]{:S(2)}) copy-start(bf16[1,1024,768]{2,1,0:T(8,128)(2,1)} %param.23) | copy-start | bytes 4718596
  181.9 34.6 %copy-start.11 = (bf16[1,2048,64]{1,2,0:T(8,128)(2,1)}, bf16[1,2048,64]{1,2,0:T(8,128)(2,1)S(1)}, u32[]{:S(2)}) copy-start(bf16[1,2048,64]{1,2,0:T(8,128)(2,1)S(1)} %all_gather.47) | copy-start | bytes 786436
  250.1 40.5 %copy-start.4 = (bf16[6144,8]{1,0:T(8,128)(2,1)S(1)}, bf16[6144,8]{1,0:T(8,128)(2,1)}, u32[]{:S(2)}) copy-start(bf16[6144,8]{1,0:T(8,128)(2,1)} %reshape.584) | copy-start | bytes 294916
  304.8 18.2 %copy-start.13 = (bf16[1,2048,64]{1,2,0:T(8,128)(2,1)S(1)}, bf16[1,2048,64]{1,2,0:T(8,128)(2,1)}, u32[]{:S(2)}) copy-start(bf16[1,2048,64]{1,2,0:T(8,128)(2,1)} %fusion.57) | copy-start | bytes 786436
  323.9 126.2 %all-reduce.16.cloned.1.call-start = ((), (), s32[]{:S(2)}) async-start(), calls=%async_computation.14 | async-start | bytes 9961472 | tf_op jit(solution)/shard_map/psum | solution.py:152
  405.1 9.9 %copy-start.47 = (bf16[768,1536]{1,0:T(8,128)(2,1)S(1)}, bf16[768,1536]{1,0:T(8,128)(2,1)}, u32[]{:S(2)}) copy-start(bf16[768,1536]{1,0:T(8,128)(2,1)} %all-gather.6.cloned.1.call-done) | copy-start | bytes 7077892
  405.1 9.9 %copy-start.48 = (bf16[1024,1536]{1,0:T(8,128)(2,1)S(1)}, bf16[1024,1536]{1,0:T(8,128)(2,1)}, u32[]{:S(2)}) copy-start(bf16[1024,1536]{1,0:T(8,128)(2,1)} %get-tuple-element.161) | copy-start | bytes 9437188
  423.6 64.7 %reduce-scatter.19.cloned.1.call-start = ((), (), s32[]{:S(2)}) async-start(), calls=%async_computation.12 | async-start | bytes 663552
  426.9 133.9 %reduce-scatter.21.cloned.1.call-start = ((), (), s32[]{:S(2)}) async-start(), calls=%async_computation.13 | async-start | bytes 2654208
  438.1 188.4 %reduce-scatter.13.cloned.1.call-start = ((), (), s32[]{:S(2)}) async-start(), calls=%async_computation.9 | async-start | bytes 663552 | tf_op jit(solution)/shard_map/reduce_scatter | solution.py:267
  440.4 258.1 %reduce-scatter.17.cloned.1.call-start = ((), (), s32[]{:S(2)}) async-start(), calls=%async_computation.11 | async-start | bytes 2654208 | tf_op jit(solution)/shard_map/reduce_scatter | solution.py:276
  447.0 251.5 %copy-start.15 = (bf16[768,128]{1,0:T(8,128)(2,1)S(1)}, bf16[768,128]{1,0:T(8,128)(2,1)}, u32[]{:S(2)}) copy-start(bf16[768,128]{1,0:T(8,128)(2,1)} %copy-done.14) | copy-start | bytes 589828
  447.0 316.0 %reduce-scatter.15.cloned.1.call-start = ((), (), s32[]{:S(2)}) async-start(), calls=%async_computation.10 | async-start | bytes 221184 | tf_op jit(solution)/shard_map/reduce_scatter | solution.py:270
  450.1 248.4 %copy-start.3 = (bf16[1024,768]{1,0:T(8,128)(2,1)S(1)}, bf16[1024,768]{1,0:T(8,128)(2,1)}, u32[]{:S(2)}) copy-start(bf16[1024,768]{1,0:T(8,128)(2,1)} %get-tuple-element.147) | copy-start | bytes 4718596
  454.6 320.0 %all-reduce.18.cloned.1.call-start = ((), (), s32[]{:S(2)}) async-start(), calls=%async_computation.15 | async-start | bytes 1720320 | tf_op jit(solution)/shard_map/psum | solution.py:290
  (28 other events, 99.8 us)
Sparse Core Ops, SparseCore 0:
  11.0 56.9 all-gather.3
  70.2 53.7 all-gather.5
  428.3 60.0 reduce-scatter.18
  492.3 68.5 reduce-scatter.20
  564.5 61.9 reduce-scatter.12
  629.9 68.5 reduce-scatter.16
  701.7 61.2 reduce-scatter.14
Sparse Core Ops, SparseCore 1:
  324.0 11.8 reduce-scatter.10
  423.7 26.4 all-reduce.15
  698.6 35.1 all-reduce.17
where the time goes:
time: 794 us; the launch traced here: 790 us
  waiting for transfers between devices  274 us (35%)
  matrix products  188 us (24%)
  blocking collectives  161 us (20%)
  other arithmetic  89.9 us (11%)
  local copies, waits for them, and re-layouts  57.8 us (7%)
  between operations  18.3 us (2%)
    unnamed x12, waiting for transfers between devices  105 us
    reduce_scatter x1, waiting for transfers between devices, on_device(): lax.psum_scatter(grads[7].astype(jnp.bfloat16), 'shard', scatter_dimensio...  72 us
    reduce_scatter x1, waiting for transfers between devices, on_device(): lax.psum_scatter(grads[4].astype(jnp.bfloat16), 'shard', scatter_dimensio...  63.8 us
    unnamed x2, blocking collectives  44 us
    convert_element_type x1, other arithmetic, backward_one(): grad_scores = (probs * (grad_probs - delta)).astype(jnp.bfloat16)  40.5 us
    dot_general x1, matrix products, backward_one(): jnp.einsum('qd,kd->qk', grad_block, value_block, preferred_element_type=j...  33.6 us
    all_gather x1, blocking collectives, on_device(): lax.all_gather(q_weight, 'shard', axis=0, tiled=True)  33.1 us
    all_gather x1, blocking collectives, on_device(): lax.all_gather(kv_weight, 'shard', axis=0, tiled=True)  31.8 us
  transfers between devices with their start and end apart: 10, of which 6 were waited for; matrix products, arithmetic and copies ran while one was open for 41% of the time, Pallas kernels for 0%

commit v1 on v0

--- a/solution.py
+++ b/solution.py
@@ -1,7 +1,15 @@
+import functools
+
 import jax
 import jax.numpy as jnp
 from jax import lax
+from jax.experimental import pallas as pl
+from jax.experimental.pallas import tpu as pltpu
 from jax.sharding import PartitionSpec as P
+
+F32 = jnp.float32
+BF = jnp.bfloat16
+MESH = pl.DeviceIdType.MESH
 
 ROT = 16
 
@@ -308,9 +316,446 @@
     )
 
 
+NY=2
+def place(nz):
+    s=lax.axis_index("shard"); x=lax.axis_index("ctx")
+    return s//NY, s%NY, x
+
+def rcopy(src,dst,ss,rs,dev):
+    return pltpu.make_async_remote_copy(src_ref=src,dst_ref=dst,send_sem=ss,recv_sem=rs,device_id=dev,device_id_type=MESH)
+
+class Gather:
+    def __init__(self, chunks, rows, nz, sems):
+        self.ch=chunks; self.rows=rows; self.nz=nz
+        self.zs,self.ys,self.xs,self.zr,self.yr,self.xr=sems
+        self.z,self.y,self.x=place(nz)
+    def block(self,c,zz,yy):
+        return self.ch[c].at[pl.ds(pl.multiple_of((zz*NY+yy)*self.rows,16),self.rows)]
+    def half(self,c,zz,yy,h):
+        hr=self.rows//2
+        return self.ch[c].at[pl.ds(pl.multiple_of((zz*NY+yy)*self.rows+h*hr,16),hr)]
+    def up(self,c,zz):
+        b=self.block(c,zz,self.y); return rcopy(b,b,self.zs.at[c,0,zz],self.zr.at[c,zz],{"shard":(self.z+1)*NY+self.y})
+    def dn(self,c,zz):
+        b=self.block(c,zz,self.y); return rcopy(b,b,self.zs.at[c,1,zz],self.zr.at[c,zz],{"shard":(self.z-1)*NY+self.y})
+    def ycp(self,c,zz,yy,h):
+        b=self.half(c,zz,yy,h); return rcopy(b,b,self.ys.at[c,zz],self.yr.at[c,zz],{"shard":self.z*NY+1-self.y})
+    def xcp(self,c,zz,h):
+        b=self.half(c,zz,1-self.y,h); return rcopy(b,b,self.xs.at[c,zz],self.xr.at[c,zz],{"ctx":1-self.x})
+    def own(self,c):
+        z,nz=self.z,self.nz
+        @pl.when(z<nz-1)
+        def _(): self.up(c,z).start()
+        @pl.when(z>0)
+        def _(): self.dn(c,z).start()
+        self.ycp(c,z,self.y,self.x).start()
+    def dirs(self,d):
+        z,nz=self.z,self.nz
+        return ((z-d>=0, z-d, True),(z+d<nz, z+d, False))
+    def Z(self,c,d):
+        z,nz=self.z,self.nz
+        for ok,zz,isup in self.dirs(d):
+            @pl.when(ok)
+            def _():
+                self.up(c,zz).wait_recv()
+                if isup:
+                    @pl.when(z<nz-1)
+                    def _(): self.up(c,zz).start()
+                else:
+                    @pl.when(z>0)
+                    def _(): self.dn(c,zz).start()
+                self.ycp(c,zz,self.y,self.x).start()
+    def _each(self,d,f):
+        if d==0: f(self.z)
+        else:
+            for ok,zz,_ in self.dirs(d):
+                pl.when(ok)(functools.partial(f,zz))
+    def Y(self,c,d):
+        def f(zz):
+            self.ycp(c,zz,1-self.y,self.x).wait_recv()
+            self.xcp(c,zz,self.x).start()
+        self._each(d,f)
+    def X(self,c,d):
+        self._each(d,lambda zz: self.xcp(c,zz,1-self.x).wait_recv())
+    def finish(self,c):
+        z,nz=self.z,self.nz
+        @pl.when(z<nz-1)
+        def _(): self.up(c,z).wait_send()
+        @pl.when(z>0)
+        def _(): self.dn(c,z).wait_send()
+        for d in range(1,nz):
+            for ok,zz,isup in self.dirs(d):
+                if isup: pl.when(jnp.logical_and(ok,z<nz-1))(lambda: self.up(c,zz).wait_send())
+                else: pl.when(jnp.logical_and(ok,z>0))(lambda: self.dn(c,zz).wait_send())
+        for zz in range(nz):
+            self.ycp(c,zz,self.y,self.x).wait_send()
+            self.xcp(c,zz,self.x).wait_send()
+    @staticmethod
+    def sem_shapes(nc,nz):
+        D=pltpu.SemaphoreType.DMA
+        return [D((nc,2,nz)),D((nc,nz)),D((nc,nz)),D((nc,nz)),D((nc,nz)),D((nc,nz))]
+
+class Scatter:
+    def __init__(self, chunks, bufs, rows, nz, sems):
+        self.ch=chunks; self.rows=rows; self.nz=nz
+        self.xb,self.yb,self.zb,self.fb=bufs
+        self.xs,self.ys,self.zs,self.fs,self.xr,self.yr,self.zr,self.fr=sems
+        self.z,self.y,self.x=place(nz)
+    block=Gather.block; half=Gather.half
+    def xcp(self,c,zz):
+        return rcopy(self.half(c,zz,1-self.y,1-self.x),self.xb[c].at[zz],self.xs.at[c,zz],self.xr.at[c,zz],{"ctx":1-self.x})
+    def ycp(self,c,zz):
+        return rcopy(self.half(c,zz,1-self.y,self.x),self.yb[c].at[zz],self.ys.at[c,zz],self.yr.at[c,zz],{"shard":self.z*NY+1-self.y})
+    def zcp(self,c,i,zz,src):
+        to=self.z+1 if i==0 else self.z-1
+        return rcopy(src,self.zb[c].at[i,zz],self.zs.at[c,i,zz],self.zr.at[c,i,zz],{"shard":to*NY+self.y})
+    def fcp(self,c):
+        return rcopy(self.fb[c].at[0],self.fb[c].at[1],self.fs.at[c],self.fr.at[c],{"ctx":1-self.x})
+    def start(self,c):
+        for zz in range(self.nz): self.xcp(c,zz).start()
+    def X(self,c,zz):
+        self.xcp(c,zz).wait_recv()
+        h=self.half(c,zz,1-self.y,self.x)
+        h[...]=(h[...].astype(F32)+self.xb[c][zz].astype(F32)).astype(BF)
+        self.ycp(c,zz).start()
+    def Y(self,c,zz):
+        z,nz=self.z,self.nz
+        self.ycp(c,zz).wait_recv()
+        h=self.half(c,zz,self.y,self.x)
+        h[...]=(h[...].astype(F32)+self.yb[c][zz].astype(F32)).astype(BF)
+        if zz>0: pl.when(z==0)(lambda: self.zcp(c,0,zz,self.block(c,zz,self.y)).start())
+        if zz<nz-1: pl.when(z==nz-1)(lambda: self.zcp(c,1,zz,self.block(c,zz,self.y)).start())
+    def Z(self,c,k):
+        z,nz=self.z,self.nz; zm=nz-1-z
+        for i,ok,zz in ((0,jnp.logical_and(z>=1,k>=z),nz-1-k+z),(1,jnp.logical_and(zm>=1,k>=zm),k-zm)):
+            @pl.when(ok)
+            def _():
+                self.zcp(c,i,zz,self.block(c,zz,self.y)).wait_recv()
+                @pl.when(zz!=z)
+                def _():
+                    slot=self.zb[c].at[i,zz]
+                    slot[...]=(slot[...].astype(F32)+self.block(c,zz,self.y)[...].astype(F32)).astype(BF)
+                    self.zcp(c,i,zz,slot).start()
+    def F(self,c):
+        z,nz=self.z,self.nz
+        own=self.block(c,z,self.y)
+        a=own[...].astype(F32)
+        u=self.zb[c][0,z].astype(F32); d=self.zb[c][1,z].astype(F32)
+        a=a+jnp.where(z>0,u,0.0)+jnp.where(z<nz-1,d,0.0)
+        self.fb[c][0]=a.astype(BF)
+        self.fcp(c).start()
+    def G(self,c):
+        self.fcp(c).wait_recv()
+        return self.fb[c][0].astype(F32)+self.fb[c][1].astype(F32)
+    def finish(self,c):
+        z,nz=self.z,self.nz
+        for zz in range(nz):
+            self.xcp(c,zz).wait_send(); self.ycp(c,zz).wait_send()
+            pl.when(jnp.logical_and(z<nz-1,zz>z))(lambda: self.zcp(c,0,zz,self.block(c,zz,self.y)).wait_send())
+            pl.when(jnp.logical_and(z>0,zz<z))(lambda: self.zcp(c,1,zz,self.block(c,zz,self.y)).wait_send())
+        self.fcp(c).wait_send()
+    @staticmethod
+    def sem_shapes(nc,nz):
+        D=pltpu.SemaphoreType.DMA
+        return [D((nc,nz)),D((nc,nz)),D((nc,2,nz)),D((nc,)),D((nc,nz)),D((nc,nz)),D((nc,2,nz)),D((nc,))]
+
+def entry(nz,all_shards,all_ctx=False):
+    bar=pltpu.get_barrier_semaphore()
+    s=lax.axis_index("shard"); x=lax.axis_index("ctx"); n=nz*NY
+    for k in range(1,n):
+        pl.semaphore_signal(bar,inc=1,device_id={"shard":lax.rem(s+k,n)},device_id_type=MESH)
+        if all_ctx: pl.semaphore_signal(bar,inc=1,device_id={"shard":lax.rem(s+k,n),"ctx":1-x},device_id_type=MESH)
+    pl.semaphore_signal(bar,inc=1,device_id={"ctx":1-x},device_id_type=MESH)
+    pl.semaphore_wait(bar,n+(n-1 if all_ctx else 0))
+
+def gather_rounds(g,nc,nz):
+    for r in range(nc+1):
+        if r+2<nc: g.own(r+2)
+        for k in range(1,nz):
+            if r<nc:
+                g.Z(r,k); g.Y(r,k-1)
+            if r>0: g.X(r-1,k-1)
+            if k==1 and r>0: g.Y(r-1,nz-1)
+        if r>0: g.X(r-1,nz-1)
+
+def ag_kernel(nz,nc,rows,fc,ca,lnp,up,dw,q,o,kv,lno,wu,wd,wq,wo,wkv,G,GA,lb,ls,lr,sem0,sem1,*sems):
+    s=lax.axis_index("shard"); n=nz*NY
+    chunks=[G.at[c] for c in range(nc)]+[GA]
+    g=Gather(chunks,rows,nz,sems)
+    own=pl.ds(pl.multiple_of(s*rows,16),rows)
+    cps=[]
+    for c in range(nc):
+        cps.append((up.at[:,pl.ds(c*fc,fc)],G.at[c,own,pl.ds(0,fc)]))
+        cps.append((dw.at[:,pl.ds(c*fc,fc)],G.at[c,own,pl.ds(fc,fc)]))
+    cps+= [(q,GA.at[own,pl.ds(0,ca)]),(o,GA.at[own,pl.ds(ca,ca)]),(kv,GA.at[own,pl.ds(2*ca,kv.shape[1])]),(lnp,lb.at[s])]
+    cps=[pltpu.make_async_copy(a,b,sem0.at[i]) for i,(a,b) in enumerate(cps)]
+    for c in cps: c.start()
+    entry(nz,True)
+    for c in cps: c.wait()
+    lns=[rcopy(lb.at[s],lb.at[s],ls.at[k-1],lr.at[s],{"shard":lax.rem(s+k,n)}) for k in range(1,n)]
+    for c in lns: c.start()
+    g.own(0); g.own(1)
+    gather_rounds(g,nc+1,nz)
+    for k in range(1,n):
+        f=lax.rem(s+n-k,n)
+        rcopy(lb.at[f],lb.at[f],ls.at[0],lr.at[f],{"shard":f}).wait_recv()
+    outs=[]
+    for c in range(nc):
+        outs.append((G.at[c,:,pl.ds(0,fc)],wu.at[:,pl.ds(c*fc,fc)])); outs.append((G.at[c,:,pl.ds(fc,fc)],wd.at[:,pl.ds(c*fc,fc)]))
+    outs+=[(GA.at[:,pl.ds(0,ca)],wq),(GA.at[:,pl.ds(ca,ca)],wo),(GA.at[:,pl.ds(2*ca,wkv.shape[1])],wkv),(lb,lno)]
+    outs=[pltpu.make_async_copy(a,b,sem1.at[i]) for i,(a,b) in enumerate(outs)]
+    for c in outs: c.start()
+    for c in outs: c.wait()
+    for c in lns: c.wait_send()
+    for c in range(nc+1): g.finish(c)
+
+def ag_call(lnp,up,dw,q,o,kv,nz,nc,cid):
+    rows,cu=up.shape; n=nz*NY; ca=q.shape[1]; fc=cu//nc; A=pl.BlockSpec(memory_space=pl.ANY); D=pltpu.SemaphoreType.DMA
+    T=n*rows; ck=kv.shape[1]
+    sd=lambda *sh:jax.ShapeDtypeStruct(sh,BF)
+    return pl.pallas_call(functools.partial(ag_kernel,nz,nc,rows,fc,ca),
+        out_shape=(jax.ShapeDtypeStruct((n,)+lnp.shape,lnp.dtype),sd(T,cu),sd(T,cu),sd(T,ca),sd(T,ca),sd(T,ck)),
+        in_specs=[A]*6,out_specs=(A,)*6,
+        scratch_shapes=[pltpu.VMEM((nc,T,2*fc),BF),pltpu.VMEM((T,2*ca+ck),BF),pltpu.VMEM((n,)+lnp.shape,lnp.dtype),
+            D((n-1,)),D((n,)),D((2*nc+4,)),D((2*nc+4,))]+Gather.sem_shapes(nc+1,nz),
+        compiler_params=pltpu.CompilerParams(collective_id=cid,has_side_effects=True,vmem_limit_bytes=60<<20),name="gather")(lnp,up,dw,q,o,kv)
+
+def scatter_rounds(r,nc,nz,out):
+    for t in range(nc+3):
+        if t+2<nc: r.start(t+2)
+        for k in range(nz):
+            if t<nc: r.X(t,k)
+            if 0<=t-1<nc: r.Y(t-1,k)
+            if k>0 and 0<=t-2<nc: r.Z(t-2,k)
+        if 0<=t-2<nc: r.F(t-2)
+        if 0<=t-3<nc: out(t-3,r.G(t-3))
+
+def rs_kernel(nz,nc,rows,fc,ca,lng,gu,gd,gq,go,gkv,lno,ou,od,oq,oo,okv,*scr):
+    G,GA=scr[:2]; xb=scr[2:4]; yb=scr[4:6]; zb=scr[6:8]; fb=scr[8:10]; lb,ls,lr,sem0=scr[10:14]; sems=scr[14:]
+    s=lax.axis_index("shard"); x=lax.axis_index("ctx"); n=nz*NY; ck=gkv.shape[1]
+    chunks=[G.at[c] for c in range(nc)]+[GA]
+    bufs=[[b[0].at[c] for c in range(nc)]+[b[1]] for b in (xb,yb,zb,fb)]
+    r=Scatter(chunks,bufs,rows,nz,sems)
+    cps=[]
+    for c in range(nc):
+        cps.append((gu.at[:,pl.ds(c*fc,fc)],G.at[c,:,pl.ds(0,fc)]))
+        cps.append((gd.at[:,pl.ds(c*fc,fc)],G.at[c,:,pl.ds(fc,fc)]))
+    cps+= [(gq,GA.at[:,pl.ds(0,ca)]),(go,GA.at[:,pl.ds(ca,ca)]),(gkv,GA.at[:,pl.ds(2*ca,ck)])]
+    cps=[pltpu.make_async_copy(a,b,sem0.at[i]) for i,(a,b) in enumerate(cps)]
+    for c in cps: c.start()
+    entry(nz,True,True)
+    me=x*n+s
+    peers=[(s,1-x)]+[(lax.rem(s+k,n),xx) for k in range(1,n) for xx in (x,1-x)]
+    lns=[rcopy(lng.at[ps],lb.at[me],ls.at[i],lr.at[me],{"shard":ps,"ctx":px}) for i,(ps,px) in enumerate(peers)]
+    for c in lns: c.start()
+    for c in cps: c.wait()
+    r.start(0); r.start(1)
+    def out(c,v):
+        if c<nc:
+            ou[:,c*fc:(c+1)*fc]=v[:,:fc]; od[:,c*fc:(c+1)*fc]=v[:,fc:]
+        else:
+            oq[...]=v[:,:ca]; oo[...]=v[:,ca:2*ca]; okv[...]=v[:,2*ca:]
+    scatter_rounds(r,nc+1,nz,out)
+    for i,(ps,px) in enumerate(peers):
+        rcopy(lng.at[ps],lb.at[px*n+ps],ls.at[i],lr.at[px*n+ps],{"shard":ps,"ctx":px}).wait_recv()
+    pltpu.sync_copy(lng.at[s],lb.at[me])
+    t=lb[0]
+    for i in range(1,2*n): t=t+lb[i]
+    lno[...]=t
+    for c in lns: c.wait_send()
+    for c in range(nc+1): r.finish(c)
+
+def rs_call(lng,gu,gd,gq,go,gkv,nz,nc,cid):
+    T,cu=gu.shape; n=nz*NY; rows=T//n; ca=gq.shape[1]; ck=gkv.shape[1]; fc=cu//nc
+    A=pl.BlockSpec(memory_space=pl.ANY); V=pl.BlockSpec(memory_space=pltpu.VMEM); D=pltpu.SemaphoreType.DMA
+    cf,cA=2*fc,2*ca+ck; hr=rows//2
+    sd=lambda *sh:jax.ShapeDtypeStruct(sh,F32)
+    vm=lambda *sh:pltpu.VMEM(sh,BF)
+    return pl.pallas_call(functools.partial(rs_kernel,nz,nc,rows,fc,ca),
+        out_shape=(sd(*lng.shape[1:]),sd(rows,cu),sd(rows,cu),sd(rows,ca),sd(rows,ca),sd(rows,ck)),
+        in_specs=[A]*6,out_specs=(V,)*6,
+        scratch_shapes=[vm(nc,T,cf),vm(T,cA),vm(nc,nz,hr,cf),vm(nz,hr,cA),vm(nc,nz,hr,cf),vm(nz,hr,cA),
+            vm(nc,2,nz,rows,cf),vm(2,nz,rows,cA),vm(nc,2,rows,cf),vm(2,rows,cA),
+            pltpu.VMEM((2*n,)+lng.shape[1:],F32),D((2*n-1,)),D((2*n,)),D((2*nc+3,))]+Scatter.sem_shapes(nc+1,nz),
+        compiler_params=pltpu.CompilerParams(collective_id=cid,has_side_effects=True,vmem_limit_bytes=60<<20),name="scatter")(lng,gu,gd,gq,go,gkv)
+
+NEG=-1e30
+def dot_nt(a,b): return lax.dot_general(a,b,(((1,),(1,)),((),())),preferred_element_type=F32)
+def dot(a,b): return lax.dot_general(a,b,(((1,),(0,)),((),())),preferred_element_type=F32)
+
+def attn_step(step, half, npair, qx, dox, qt, dot_, kx, k0, v0, att, dq, dkt, dvt, s_scr, dp_scr, p_scr, ds_scr, BQ, BK):
+    tile = step // npair
+    sub = half // BQ
+    own = tile // sub
+    r0 = (tile % sub) * BQ
+    nk = kx.shape[0]//BK
+    offs=[]
+    per = half//BK
+    for j in range(nk):
+        if j < per: o = own*half + j*BK
+        elif j < 2*per: o = (1-own)*half + (j-per)*BK
+        else: o = j*BK
+        offs.append(pl.multiple_of(o,BK) if not isinstance(o,int) else o)
+    q = qx[step]; do = dox[step]
+    m = None
+    R = q.shape[0]
+    for j in range(nk):
+        s = dot_nt(q, kx[pl.ds(offs[j],BK),:])
+        if j < per:
+            row = lax.broadcasted_iota(jnp.int32,(R,BK),0) % BQ + r0
+            col = lax.broadcasted_iota(jnp.int32,(R,BK),1) + j*BK
+            s = jnp.where(col<=row, s, NEG)
+        s_scr[:, j*BK:(j+1)*BK] = s
+        mj = s[:, :128]
+        for t in range(1,BK//128): mj = jnp.maximum(mj, s[:, t*128:(t+1)*128])
+        m = mj if m is None else jnp.maximum(m,mj)
+    m = jnp.max(m,axis=1,keepdims=True)
+    l = None; o = None
+    for j in range(nk):
+        p = jnp.exp(s_scr[:, j*BK:(j+1)*BK]-m)
+        s_scr[:, j*BK:(j+1)*BK] = p
+        lj = p[:, :128]
+        for t in range(1,BK//128): lj = lj + p[:, t*128:(t+1)*128]
+        l = lj if l is None else l+lj
+        pb = p.astype(BF)
+        p_scr[:, j*BK:(j+1)*BK] = pb
+        oj = dot(pb, v0[pl.ds(offs[j],BK),:])
+        o = oj if o is None else o+oj
+    l = jnp.sum(l,axis=1,keepdims=True)
+    inv = 1.0/l
+    o = o*inv
+    delta = jnp.sum(o*do.astype(F32),axis=1,keepdims=True)
+    dqa = None
+    inv_row = jnp.transpose(jnp.broadcast_to(inv,(R,128)))[:1,:]
+    qs = (qt[step].astype(F32)*inv_row).astype(BF)
+    dos = (dot_[step].astype(F32)*inv_row).astype(BF)
+    for j in range(nk):
+        dp = dot_nt(do, v0[pl.ds(offs[j],BK),:])
+        ds = (s_scr[:, j*BK:(j+1)*BK]*(dp-delta)).astype(BF)
+        dj = dot(ds, k0[pl.ds(offs[j],BK),:])
+        dqa = dj if dqa is None else dqa+dj
+        dkt[:, pl.ds(offs[j],BK)] += dot(qs, ds)
+        dvt[:, pl.ds(offs[j],BK)] += dot(dos, p_scr[:, j*BK:(j+1)*BK])
+    dqa = dqa*(inv*0.125)
+    def pairup(x):
+        return x[:BQ] + pltpu.roll(x[BQ:],64,1)
+    att[step] = pairup(o).astype(att.dtype)
+    dq[step] = pairup(dqa)
+
+def attn_kernel(half, npair, BQ, BK, qx, dox, qt, dot_, kx, k0, v0, att, dq, dkt, dvt, s_scr, dp_scr, p_scr, ds_scr):
+    dkt[...] = jnp.zeros_like(dkt); dvt[...] = jnp.zeros_like(dvt)
+    @pl.loop(0, qx.shape[0])
+    def _(step):
+        attn_step(step, half, npair, qx, dox, qt, dot_, kx, k0, v0, att, dq, dkt, dvt, s_scr, dp_scr, p_scr, ds_scr, BQ, BK)
+
+def attn_call(qx, dox, qt, dot_, kx, k0, v0, half, npair, BQ, BK, name="attn"):
+    ns=qx.shape[0]; nk=kx.shape[0]; R=qx.shape[1]
+    V=pl.BlockSpec(memory_space=pltpu.VMEM)
+    return pl.pallas_call(functools.partial(attn_kernel,half,npair,BQ,BK),
+      out_shape=(jax.ShapeDtypeStruct((ns,R//2,128),BF),jax.ShapeDtypeStruct((ns,R//2,128),F32),
+                 jax.ShapeDtypeStruct((64,nk),F32),jax.ShapeDtypeStruct((64,nk),F32)),
+      in_specs=[V]*7,out_specs=(V,)*4,
+      scratch_shapes=[pltpu.VMEM((R,nk),F32),pltpu.VMEM((8,128),F32),pltpu.VMEM((R,nk),BF),pltpu.VMEM((8,128),BF)],
+      compiler_params=pltpu.CompilerParams(vmem_limit_bytes=60<<20),name=name)(qx,dox,qt,dot_,kx,k0,v0)
+
+def fits(mesh):
+    return mesh.shape["shard"] == 8 and mesh.shape["ctx"] == 2
+
+
+def fast_device(hidden, block_order, ln1_gain, ln1_bias, ln2_gain, ln2_bias, q_weight, kv_weight, o_weight, up_weight, down_weight, cotangent):
+    seqs, span, width = hidden.shape
+    half = span // 2
+    hd = kv_weight.shape[1] // 2
+    heads = q_weight.shape[1] // hd
+    npair = heads // 2
+    BQ = 256
+    nt = span // BQ
+    ns = nt * npair
+    x = lax.axis_index("ctx")
+    rows = ln1_gain.shape[0]
+    n = width // rows
+    nz = n // NY
+    lnp = jnp.pad(jnp.stack([ln1_gain, ln1_bias, ln2_gain, ln2_bias]).astype(F32), ((0, 4), (0, 128 - rows)))
+    lno, w_up, w_down, w_query, w_output, w_keyval = ag_call(lnp, up_weight, down_weight, q_weight, o_weight, kv_weight, nz, 4, 1)
+    params = lno[:, :4, :rows].transpose(1, 0, 2).reshape(4, width)
+    gain_attn, bias_attn, gain_ffn, bias_ffn = params[0], params[1], params[2], params[3]
+    tokens = hidden.astype(F32).reshape(span, width)
+    cot = cotangent.reshape(span, width)
+    norm_attn = layer_norm(tokens, gain_attn, bias_attn).astype(BF)
+    norm_ffn = layer_norm(tokens, gain_ffn, bias_ffn).astype(BF)
+    places = tok_positions(block_order, x * span + jnp.arange(span, dtype=jnp.int32), half)
+    query_pre = jnp.dot(norm_attn, w_query, preferred_element_type=F32).reshape(span, heads, hd)
+    queries = rotate(query_pre, places, 1.0).astype(BF)
+    keyval_pre = jnp.dot(norm_attn, w_keyval, preferred_element_type=F32)
+    keys = rotate(keyval_pre[:, None, :hd], places, 1.0)[:, 0].astype(BF)
+    values = keyval_pre[:, hd:].astype(BF)
+    kv = jnp.concatenate([keys, values], axis=1)
+    kv_other = lax.ppermute(kv, "ctx", [(0, 1), (1, 0)])
+    kvs = jnp.concatenate([kv, kv_other], axis=0)
+    grad_att = jnp.dot(cot, w_output, preferred_element_type=F32).astype(BF).reshape(span, heads, hd)
+
+    def stepmajor(a):
+        return a.reshape(nt, BQ, npair, 2, hd).transpose(0, 2, 3, 1, 4).reshape(ns, 2 * BQ, hd)
+
+    own = lax.dynamic_slice(block_order, (2 * x,), (2,))
+    oth = lax.dynamic_slice(block_order, (2 * (1 - x),), (2,))
+    order = jnp.concatenate([own, oth])
+    hide = jnp.where(order[None, :] <= own[:, None], 0.0, NEG)
+    blk = (jnp.arange(ns) // npair) * BQ // half
+    lanes = jnp.pad(hide[blk], ((0, 0), (0, hd - 4))).astype(BF)
+    qs = stepmajor(queries * jnp.asarray(hd**-0.5, BF))
+    ds = stepmajor(grad_att)
+    qx = jnp.concatenate([qs, jnp.broadcast_to(lanes[:, None, :], (ns, 2 * BQ, hd))], axis=-1)
+    dox = jnp.concatenate([ds, jnp.zeros_like(ds)], axis=-1)
+    nk = kvs.shape[0]
+    hot = (jnp.arange(nk)[:, None] // half == jnp.arange(hd)[None, :]).astype(BF)
+    zero = jnp.zeros((nk, hd), BF)
+    kk, vv = kvs[:, :hd], kvs[:, hd:]
+    att, dq, dkt, dvt = attn_call(qx, dox, qs.transpose(0, 2, 1), ds.transpose(0, 2, 1), jnp.concatenate([kk, hot], -1), jnp.concatenate([kk, zero], -1), jnp.concatenate([vv, zero], -1), half, npair, BQ, 512)
+
+    def unstep(a):
+        return a.reshape(nt, npair, BQ, 2, hd).transpose(0, 2, 1, 3, 4).reshape(span, heads, hd)
+
+    attended = unstep(att).reshape(span, heads * hd)
+    hidden_pre = jnp.dot(norm_ffn, w_up, preferred_element_type=F32)
+    activation_full, gelu_pull = jax.vjp(gelu_exact, hidden_pre)
+    activation = activation_full.astype(BF)
+    branch = right_product(attended, w_output) + right_product(activation, w_down)
+    branch = lax.psum(branch.astype(BF), "tp").astype(F32)
+    mixed = (tokens + branch).astype(BF).reshape(seqs, span, width)
+    grad_activation = jnp.dot(cot, w_down, preferred_element_type=F32)
+    grad_hidden = gelu_pull(grad_activation)[0].astype(BF)
+    gwo = left_product(cot, attended)
+    gwd = left_product(cot, activation)
+    gwu = left_product(norm_ffn, grad_hidden)
+    gnf = right_product(grad_hidden, w_up)
+    gkv = jnp.concatenate([dkt, dvt], axis=0).T.astype(BF)
+    gkv = lax.psum(gkv.astype(F32), "tp").astype(BF)
+    gkv_mine = gkv[:span].astype(F32) + lax.ppermute(gkv[span:], "ctx", [(0, 1), (1, 0)]).astype(F32)
+    gk = rotate(gkv_mine[:, None, :hd], places, -1.0)[:, 0]
+    gkv_pre = jnp.concatenate([gk, gkv_mine[:, hd:]], axis=1).astype(BF)
+    gq_pre = rotate(unstep(dq), places, -1.0).astype(BF).reshape(span, heads * hd)
+    gwq = left_product(norm_attn, gq_pre)
+    gwkv = left_product(norm_attn, gkv_pre)
+    gna = right_product(gq_pre, w_query)
+    shared = right_product(gkv_pre, w_keyval)
+    zero_shift = jnp.zeros((width,), F32)
+    attn_pull = jax.vjp(layer_norm, tokens, gain_attn, zero_shift)[1]
+    ffn_pull = jax.vjp(layer_norm, tokens, gain_ffn, zero_shift)[1]
+    gna = lax.psum(gna.astype(BF), "tp").astype(F32) + shared
+    gnf = lax.psum(gnf.astype(BF), "tp").astype(F32)
+    gta, gga, gsa = attn_pull(gna)
+    gtf, ggf, gsf = ffn_pull(gnf)
+    grad_tokens = (cot.astype(F32) + gta + gtf).reshape(seqs, span, width)
+    lng = jnp.pad(jnp.stack([gga, gsa, ggf, gsf]).reshape(4, n, rows).transpose(1, 0, 2), ((0, 0), (0, 4), (0, 128 - rows)))
+    bf = lambda a: a.astype(BF)
+    lo, ou, od, oq, oo, okv = rs_call(lng, bf(gwu), bf(gwd), bf(gwq), bf(gwo), bf(gwkv), nz, 4, 2)
+    return (mixed, keys.reshape(seqs, span, hd), values.reshape(seqs, span, hd), grad_tokens, lo[0, :rows], lo[1, :rows], lo[2, :rows], lo[3, :rows], oq, okv, oo, ou, od)
+
+
 def solution(mesh):
     return jax.shard_map(
-        on_device,
+        fast_device if fits(mesh) else on_device,
         mesh=mesh,
         in_specs=(
             P("shard", "ctx", None),

time: 794 us -> 418 us (0.53)
  waiting for transfers between devices: 274 us -> 2.35 us
  Pallas kernels: 0 us -> 213 us
  blocking collectives: 161 us -> 8.2 us
  matrix products: 188 us -> 62.3 us
  other arithmetic: 89.9 us -> 40.1 us
  local copies, waits for them, and re-layouts: 57.8 us -> 68.4 us
    pallas_call x0 -> x3, Pallas kernels: none -> 213 us  [the longest x1 80.8 us: rs_call(): pl.pallas_call(functools.partial(rs_kernel, nz, nc, rows, fc, ca), out_sh...]
    reduce_scatter x4 -> x0, waiting for transfers between devices: 166 us -> none  [the longest x1 72 us: on_device(): lax.psum_scatter(grads[7].astype(jnp.bfloat16), 'shard', scatter_dimensio...]
    dot_general x11 -> x5, matrix products: 153 us -> 25.9 us  [the longest x1 15.8 us: fast_device(): hidden_pre = jnp.dot(norm_ffn, w_up, preferred_element_type=F32)]
    all_gather x5 -> x0, blocking collectives: 108 us -> none  [the longest x1 33.1 us: on_device(): lax.all_gather(q_weight, 'shard', axis=0, tiled=True)]
    unnamed x12 -> x1, waiting for transfers between devices: 105 us -> 0.02 us
    unnamed x2 -> x0, blocking collectives: 44 us -> none
    convert_element_type x15 -> x6, other arithmetic: 48.7 us -> 5.75 us  [the longest x1 2.5 us: fast_device(): gkv = lax.psum(gkv.astype(F32), 'tp').astype(BF)]
    reduce_sum x1 -> x0, other arithmetic: 23.6 us -> none  [one_block(): total = total * factor + jnp.sum(weights, axis=1)]
  transfers between devices with their start and end apart: 10 -> 3, of which waited for: 6 -> 1; matrix products, arithmetic and copies ran while one was open for 41% -> 25% of each run, Pallas kernels for 0% -> 0%
where the time goes in v1:
time: 418 us; the launch traced here: 411 us
  Pallas kernels  213 us (51%)
  local copies, waits for them, and re-layouts  68.4 us (16%)
  matrix products  62.3 us (15%)
  other arithmetic  40.1 us (10%)
  between operations  15 us (4%)
  blocking collectives  8.2 us (2%)
    pallas_call x1, Pallas kernels, rs_call(): pl.pallas_call(functools.partial(rs_kernel, nz, nc, rows, fc, ca), out_sh...  80.8 us
    pallas_call x1, Pallas kernels, ag_call(): pl.pallas_call(functools.partial(ag_kernel, nz, nc, rows, fc, ca), out_sh...  71.7 us
    pallas_call x1, Pallas kernels, attn_call(): pl.pallas_call(functools.partial(attn_kernel, half, npair, BQ, BK), out_s...  60.1 us
    dot_general x5, matrix products, right_product(): lax.dot_general(left, right, (((1,), (1,)), ((), ())), preferred_element_...  18.9 us
    dot_general x5, matrix products, left_product(): lax.dot_general(left, right, (((0,), (0,)), ((), ())), preferred_element_...  17.5 us
    dot_general x1, matrix products, fast_device(): hidden_pre = jnp.dot(norm_ffn, w_up, preferred_element_type=F32)  15.8 us
    unnamed x87, local copies, waits for them, and re-layouts  14.9 us
  transfers between devices with their start and end apart: 3, of which 1 were waited for; matrix products, arithmetic and copies ran while one was open for 25% of the time, Pallas kernels for 0%

profile of v1, /device:TPU:0, one launch (start us, length us, event | category | flops | bytes accessed | tf_op | source)
XLA Modules:
  0.0 411.0 jit_solution(16067255099647291948)
XLA Ops:
  11.8 71.7 %gather.7 = (f32[8,8,128]{2,1,0:T(8,128)}, bf16[768,1536]{1,0:T(8,128)(2,1)}, bf16[768,1536]{1,0:T(8,128)(2,1)}, bf16[768,384]{1,0:T(8,128)(2,1)}, bf16[768,384]{1,0:T(8,128)(2,1)}, /*index=5*/bf16[768,128]{1,0:T(8,128)(2,1)}) custom-call(f32[8,128]{1,0:T(8,128)} %fusion.104.lnp, bf16[96,1536]{1,0:T(8,128)(2,1)} %up.1, bf16[96,1536]{1,0:T(8,128)(2,1)} %dw.1, ...), custom_call_target="tpu_custom_call" | custom-call | tf_op jit(solution)/shard_map/gather/pallas_call | solution.py:516
  88.6 4.0 fusion.82
  99.7 3.3 fusion.61
  103.0 2.6 reshape_reshape.6
  105.7 2.8 copy.110
  108.5 3.1 reshape.522
  115.7 2.4 concatenate.56
  123.0 3.1 reshape.520
  127.0 2.4 pad_maximum_fusion
  129.5 2.6 copy.90.qx
  132.1 2.6 copy.107
  134.7 3.1 concatenate.60.clone.dox
  137.8 15.8 %multiply_convert_fusion = (bf16[1024,1536]{1,0:T(8,128)(2,1)S(1)}, f32[1024,1536]{1,0:T(8,128)S(1)}, f32[1024,1536]{1,0:T(8,128)S(1)}) fusion(bf16[768,1536]{1,0:T(8,128)(2,1)S(1)} %copy-done.35, bf16[1,1024,768]{2,1,0:T(8,128)(2,1)S(1)} %copy-done, f32[768]{0:T(1024)S(1)} %add.177, f32[768]{0:T(1024)S(1)} %mul.376, f32[1024]{0:T(1024)S(1)} %fusion.99, ...), kind=kOutput, calls=%fused_computation.12 | convolution fusion | flops 2522873856 | bytes 19675136 | tf_op jit(solution)/shard_map/dot_general | solution.py:720
  153.6 4.2 %fusion.6 = bf16[1024,1536]{1,0:T(8,128)(2,1)S(1)} fusion(f32[1024,1536]{1,0:T(8,128)S(1)} %get-tuple-element.117, f32[1024,1536]{1,0:T(8,128)S(1)} %get-tuple-element.141, bf16[768,1536]{1,0:T(8,128)(2,1)S(1)} %copy-done.34, bf16[1,1024,768]{2,1,0:T(8,128)(2,1)S(1)} %copy-done.13), kind=kOutput, calls=%fused_computation.10 | convolution fusion | flops 2437939200 | bytes 19660800 | tf_op jit(solution)/shard_map/dot_general | solution.py:726
  157.8 3.8 convolution_convert_fusion.3
  161.6 4.3 %fusion.122 = f32[1024,768]{1,0:T(8,128)} fusion(bf16[1024,1536]{1,0:T(8,128)(2,1)S(1)} %get-tuple-element.116, bf16[768,1536]{1,0:T(8,128)(2,1)S(1)} %copy-done.34), kind=kOutput, calls=%fused_computation.211 | convolution fusion | flops 2415919104 | bytes 8650752 | tf_op jit(solution)/shard_map/dot_general | solution.py:48
  170.5 60.1 %attn.1 = (bf16[12,256,128]{2,1,0:T(8,128)(2,1)}, f32[12,256,128]{2,1,0:T(8,128)}, f32[64,2048]{1,0:T(8,128)}, f32[64,2048]{1,0:T(8,128)}) custom-call(bf16[12,512,128]{2,1,0:T(8,128)(2,1)} %copy.90.qx, bf16[12,512,128]{2,1,0:T(8,128)(2,1)} %concatenate.60.clone.dox, bf16[12,64,512]{2,1,0:T(8,128)(2,1)} %bitcast.205, bf16[12,64,512]{2,1,0:T(8,128)(2,1)} %bitcast.204, ...), custom_call_target="tpu_custom_call" | custom-call | tf_op jit(solution)/shard_map/attn/pallas_call | solution.py:654
  235.7 3.0 copy.94
  238.7 3.6 copy.95
  242.3 3.1 reshape.527
  249.2 3.2 convolution_convert_fusion.2
  261.9 6.7 %fusion.39.gd = bf16[768,1536]{1,0:T(8,128)(2,1)} fusion(bf16[1024,1536]{1,0:T(8,128)(2,1)} %copy-done.36, bf16[1,1024,768]{2,1,0:T(8,128)(2,1)} %param.23), kind=kOutput, calls=%fused_computation.65 | convolution fusion | flops 2417098752 | bytes 7077888 | tf_op jit(solution)/shard_map/dot_general | solution.py:54
  268.7 4.2 %convolution_convert_fusion.1.gu = bf16[768,1536]{1,0:T(8,128)(2,1)} fusion(bf16[1024,1536]{1,0:T(8,128)(2,1)S(1)} %copy-done.38, bf16[1,1024,768]{2,1,0:T(8,128)(2,1)S(1)} %copy-done, f32[768]{0:T(1024)S(1)} %add.177, f32[768]{0:T(1024)S(1)} %mul.376, f32[1024]{0:T(1024)S(1)} %fusion.99, f32[1024]{0:T(1024)S(1)} %broadcast_multiply_fusion.1), kind=kOutput, calls=%fused_computation.47 | convolution fusion | flops 2421817344 | bytes 7092224 | tf_op jit(solution)/shard_map/dot_general | solution.py:54
  276.1 2.5 convert_bitcast_fusion.1
  278.6 8.2 %all-reduce.10 = bf16[2048,128]{1,0:T(8,128)(2,1)} all-reduce(f32[2048,128]{1,0:T(8,128)} %convert_bitcast_fusion.1), channel_id=1, replica_groups=mesh['shard'=8,'ctx'=2,'tp'=2] {'tp'}, use_global_device_ids=true, to_apply=%region_5.6 | all-reduce | flops 262144 | bytes 1572864 | tf_op jit(solution)/shard_map/psum | solution.py:733
  288.7 3.3 fusion.55.gq
  293.9 2.3 collective-permute-done.1
  296.6 2.7 fusion.79
  301.7 5.4 %fusion.31 = (f32[1024]{0:T(1024)S(1)}, f32[1024]{0:T(1024)S(1)}, f32[768]{0:T(1024)S(1)}, f32[1024,768]{1,0:T(8,128)}) fusion(bf16[1,1024,768]{2,1,0:T(8,128)(2,1)S(1)} %copy-done, f32[768]{0:T(1024)S(1)} %mul.346, f32[1024]{0:T(1024)S(1)} %broadcast_multiply_fusion.1, f32[768]{0:T(1024)S(1)} %mul.376, bf16[1024,768]{1,0:T(8,128)(2,1)} %get-tuple-element.112, ...), kind=kOutput, calls=%fused_computation.54 | convolution fusion | flops 211285248 | bytes 8344576 | tf_op jit(solution)/shard_map/dot_general | solution.py:48
  307.2 4.4 %fusion.29 = (f32[768]{0:T(1024)S(1)}, f32[1024]{0:T(1024)S(1)}, f32[768]{0:T(1024)S(1)}, f32[1024]{0:T(1024)S(1)}, f32[768]{0:T(1024)S(1)}) fusion(f32[1024,768]{1,0:T(8,128)} %get-tuple-element.142, bf16[1,1024,768]{2,1,0:T(8,128)(2,1)S(1)} %copy-done, f32[1024]{0:T(1024)S(1)} %fusion.99, f32[1024]{0:T(1024)S(1)} %broadcast_multiply_fusion.1, ...), kind=kLoop, calls=%fused_computation.52 | loop fusion | flops 16510720 | bytes 6331392 | tf_op jit(solution)/shard_map/transpose(jvp())/reduce_sum | solution.py:20
  312.4 80.8 %scatter.1 = (f32[8,128]{1,0:T(8,128)}, f32[96,1536]{1,0:T(8,128)}, f32[96,1536]{1,0:T(8,128)}, f32[96,384]{1,0:T(8,128)}, f32[96,384]{1,0:T(8,128)}, /*index=5*/f32[96,128]{1,0:T(8,128)}) custom-call(f32[8,8,128]{2,1,0:T(8,128)} %pad.21.lng, bf16[768,1536]{1,0:T(8,128)(2,1)} %convolution_convert_fusion.1.gu, bf16[768,1536]{1,0:T(8,128)(2,1)} %fusion.39.gd, ...), custom_call_target="tpu_custom_call" | custom-call | tf_op jit(solution)/shard_map/scatter/pallas_call | solution.py:574
  394.6 5.7 %add_bitcast_fusion = (f32[1,1024,768]{2,1,0:T(8,128)}, bf16[1,1024,768]{2,1,0:T(8,128)(2,1)}) fusion(bf16[1,1024,768]{2,1,0:T(8,128)(2,1)S(1)} %copy-done, bf16[1024,768]{1,0:T(8,128)(2,1)S(1)} %copy-done.1, bf16[1,1024,768]{2,1,0:T(8,128)(2,1)} %param.23, f32[1024]{0:T(1024)S(1)} %get-tuple-element.143, f32[1024]{0:T(1024)S(1)} %get-tuple-element.137, ...), kind=kLoop, calls=%fused_computation.62 | loop fusion | flops 16515072 | bytes 14186496 | tf_op jit(solution)/shard_map/reshape | solution.py:749
  (166 shorter events, 65.0 us)
Async XLA Ops:
  7.2 77.3 %copy-start = (bf16[1,1024,768]{2,1,0:T(8,128)(2,1)S(1)}, bf16[1,1024,768]{2,1,0:T(8,128)(2,1)}, u32[]{:S(2)}) copy-start(bf16[1,1024,768]{2,1,0:T(8,128)(2,1)} %param.12) | copy-start | bytes 4718596
  7.2 3.9 copy-start.29
  7.2 3.9 copy-start.30
  7.2 3.9 copy-start.31
  7.2 3.9 copy-start.32
  7.2 294.5 %all-reduce.9.cloned.1.call-start = ((), (), s32[]{:S(2)}) async-start(), calls=%async_computation | async-start | bytes 9437184 | tf_op jit(solution)/shard_map/psum | solution.py:724
  7.3 88.4 %copy-start.26 = (f32[8]{0:T(128)}, f32[8]{0:T(128)S(1)}, u32[]{:S(2)}) copy-start(f32[8]{0:T(128)S(1)} %multiply_power_fusion) | copy-start | bytes 100
  88.6 5.8 %copy-start.8 = (bf16[1024,1,48]{2,0,1:T(8,128)(2,1)}, bf16[1024,1,48]{2,0,1:T(8,128)(2,1)S(1)}, u32[]{:S(2)}) copy-start(bf16[1024,1,48]{2,0,1:T(8,128)(2,1)S(1)} %slice.135) | copy-start | bytes 294916
  94.5 71.8 %collective-permute-start = (bf16[1024,128]{1,0:T(8,128)(2,1)}, bf16[1024,128]{1,0:T(8,128)(2,1)}, u32[]{:S(2)}, u32[]{:S(2)}) collective-permute-start(bf16[1024,128]{1,0:T(8,128)(2,1)} %pad_maximum_fusion.3), channel_id=1, source_target_pairs={{0,2},{2,0},{1,3},{3,1},{4,6},{6,4},{5,7},{7,5},{8,10},{10,8},{9,1... | collective-permute-start | bytes 786440 | tf_op jit(solution)/shard_map/ppermute | solution.py:693
  137.8 15.8 %copy-start.13 = (bf16[1,1024,768]{2,1,0:T(8,128)(2,1)S(1)}, bf16[1,1024,768]{2,1,0:T(8,128)(2,1)}, u32[]{:S(2)}) copy-start(bf16[1,1024,768]{2,1,0:T(8,128)(2,1)} %param.23) | copy-start | bytes 4718596
  137.8 15.8 %copy-start.34 = (bf16[768,1536]{1,0:T(8,128)(2,1)S(1)}, bf16[768,1536]{1,0:T(8,128)(2,1)}, u32[]{:S(2)}) copy-start(bf16[768,1536]{1,0:T(8,128)(2,1)} %get-tuple-element.35) | copy-start | bytes 7077892
  153.5 8.1 %copy-start.36 = (bf16[1024,1536]{1,0:T(8,128)(2,1)}, bf16[1024,1536]{1,0:T(8,128)(2,1)S(1)}, u32[]{:S(2)}) copy-start(bf16[1024,1536]{1,0:T(8,128)(2,1)S(1)} %get-tuple-element.116) | copy-start | bytes 9437188
  157.8 3.8 copy-start.37
  161.6 4.7 %copy-start.7 = (bf16[1024,64]{1,0:T(8,128)(2,1)S(1)}, bf16[1024,64]{1,0:T(8,128)(2,1)}, u32[]{:S(2)}) copy-start(bf16[1024,64]{1,0:T(8,128)(2,1)} %copy-done.6) | copy-start | bytes 393220
  161.6 4.7 %copy-start.33 = (pred[128]{0:T(512)(128)(4,1)S(1)}, pred[128]{0:T(512)(128)(4,1)}, u32[]{:S(2)}) copy-start(pred[128]{0:T(512)(128)(4,1)} %constant.133.clone.1) | copy-start | bytes 388
  245.4 7.0 %copy-start.3 = (bf16[48,8,4,256]{3,1,2,0:T(8,128)(2,1)S(1)}, bf16[48,8,4,256]{3,1,2,0:T(8,128)(2,1)}, u32[]{:S(2)}) copy-start(bf16[48,8,4,256]{3,1,2,0:T(8,128)(2,1)} %copy.108) | copy-start | bytes 2359300
  245.4 7.0 %copy-start.5 = (f32[1024,768]{1,0:T(8,128)S(1)}, f32[1024,768]{1,0:T(8,128)}, u32[]{:S(2)}) copy-start(f32[1024,768]{1,0:T(8,128)} %fusion.122) | copy-start | bytes 9437188
  245.4 7.0 %copy-start.18 = (bf16[768,384]{1,0:T(8,128)(2,1)S(1)}, bf16[768,384]{1,0:T(8,128)(2,1)}, u32[]{:S(2)}) copy-start(bf16[768,384]{1,0:T(8,128)(2,1)} %get-tuple-element.31) | copy-start | bytes 1769476
  254.6 3.7 copy-start.9
  261.9 6.7 %copy-start.38 = (bf16[1024,1536]{1,0:T(8,128)(2,1)S(1)}, bf16[1024,1536]{1,0:T(8,128)(2,1)}, u32[]{:S(2)}) copy-start(bf16[1024,1536]{1,0:T(8,128)(2,1)} %copy-done.37) | copy-start | bytes 9437188
  268.7 4.2 %copy-start.21 = (f32[64,2048]{1,0:T(8,128)S(1)}, f32[64,2048]{1,0:T(8,128)}, u32[]{:S(2)}) copy-start(f32[64,2048]{1,0:T(8,128)} %get-tuple-element.37) | copy-start | bytes 1572868
  287.7 4.3 %copy-start.4 = (bf16[48,8,4,256]{3,1,2,0:T(8,128)(2,1)S(1)}, bf16[48,8,4,256]{3,1,2,0:T(8,128)(2,1)}, u32[]{:S(2)}) copy-start(bf16[48,8,4,256]{3,1,2,0:T(8,128)(2,1)} %copy.108) | copy-start | bytes 2359300
  287.7 4.3 %copy-start.14 = (bf16[1,1024,768]{2,1,0:T(8,128)(2,1)S(1)}, bf16[1,1024,768]{2,1,0:T(8,128)(2,1)}, u32[]{:S(2)}) copy-start(bf16[1,1024,768]{2,1,0:T(8,128)(2,1)} %param.23) | copy-start | bytes 4718596
  287.8 8.4 %collective-permute-start.1 = (bf16[1024,128]{1,0:T(8,128)(2,1)S(1)}, bf16[1024,128]{1,0:T(8,128)(2,1)S(1)}, u32[]{:S(2)}, u32[]{:S(2)}) collective-permute-start(bf16[1024,128]{1,0:T(8,128)(2,1)S(1)} %slice.145), channel_id=1, source_target_pairs={{0,2},{2,0},{1,3},{3,1},{4,6},{6,4},{5,7},{7,5},{8,10},{10,8},{9,1... | collective-permute-start | bytes 786440 | tf_op jit(solution)/shard_map/ppermute | solution.py:734
  292.0 4.2 %copy-start.12 = (bf16[2048,128]{1,0:T(8,128)(2,1)S(1)}, bf16[2048,128]{1,0:T(8,128)(2,1)}, u32[]{:S(2)}) copy-start(bf16[2048,128]{1,0:T(8,128)(2,1)} %all-reduce.10) | copy-start | bytes 1572868
  292.0 4.6 %copy-start.27 = (f32[8]{0:T(128)S(1)}, f32[8]{0:T(128)}, u32[]{:S(2)}) copy-start(f32[8]{0:T(128)} %copy-done.26) | copy-start | bytes 100
  301.7 5.5 %copy-start.1 = (bf16[1024,768]{1,0:T(8,128)(2,1)S(1)}, bf16[1024,768]{1,0:T(8,128)(2,1)}, u32[]{:S(2)}) copy-start(bf16[1024,768]{1,0:T(8,128)(2,1)} %get-tuple-element.112) | copy-start | bytes 4718596
  394.6 5.7 %copy-start.24 = (f32[96,384]{1,0:T(8,128)S(1)}, f32[96,384]{1,0:T(8,128)}, u32[]{:S(2)}) copy-start(f32[96,384]{1,0:T(8,128)} %get-tuple-element.166) | copy-start | bytes 442372
  394.6 6.4 %copy-start.25 = (f32[96,128]{1,0:T(8,128)S(1)}, f32[96,128]{1,0:T(8,128)}, u32[]{:S(2)}) copy-start(f32[96,128]{1,0:T(8,128)} %get-tuple-element.167) | copy-start | bytes 147460
  394.6 7.0 %copy-start.23 = (f32[96,384]{1,0:T(8,128)S(1)}, f32[96,384]{1,0:T(8,128)}, u32[]{:S(2)}) copy-start(f32[96,384]{1,0:T(8,128)} %get-tuple-element.168) | copy-start | bytes 442372
  394.6 7.7 %copy-start.20 = (f32[96,1536]{1,0:T(8,128)S(1)}, f32[96,1536]{1,0:T(8,128)}, u32[]{:S(2)}) copy-start(f32[96,1536]{1,0:T(8,128)} %get-tuple-element.169) | copy-start | bytes 1769476
  394.6 8.5 %copy-start.19 = (f32[96,1536]{1,0:T(8,128)S(1)}, f32[96,1536]{1,0:T(8,128)}, u32[]{:S(2)}) copy-start(f32[96,1536]{1,0:T(8,128)} %get-tuple-element.170) | copy-start | bytes 1769476
  (10 other events, 15.5 us)
Sparse Core Ops, SparseCore 0:
  254.7 30.5 all-reduce.8

commit v2 on v0

--- a/solution.py
+++ b/solution.py
@@ -1,7 +1,17 @@
+import functools
+import types
+
 import jax
 import jax.numpy as jnp
+import numpy as np
 from jax import lax
+from jax.experimental import pallas as pl
+from jax.experimental.pallas import tpu as pltpu
 from jax.sharding import PartitionSpec as P
+
+F32 = jnp.float32
+BF = jnp.bfloat16
+MESH = pl.DeviceIdType.MESH
 
 ROT = 16
 
@@ -308,9 +318,732 @@
     )
 
 
+NY = 2
+NEG = -1e30
+
+
+def rcopy(src, dst, ss, rs, dev):
+    return pltpu.make_async_remote_copy(src_ref=src, dst_ref=dst, send_sem=ss, recv_sem=rs, device_id=dev, device_id_type=MESH)
+
+
+def dot_nt(a, b):
+    return lax.dot_general(a, b, (((1,), (1,)), ((), ())), preferred_element_type=F32)
+
+
+def dot(a, b):
+    return lax.dot_general(a, b, (((1,), (0,)), ((), ())), preferred_element_type=F32)
+
+
+def both(a, b):
+    return jnp.logical_and(a, b)
+
+
+class Gather:
+    def __init__(self, ref, rows, nz, sems):
+        self.ref, self.rows, self.nz = ref, rows, nz
+        self.zs, self.ys, self.xs, self.zr, self.yr, self.xr = sems
+        s = lax.axis_index("shard")
+        self.z, self.y, self.x = s // NY, s % NY, lax.axis_index("ctx")
+
+    def block(self, c, zz, yy):
+        return self.ref.at[c, pl.ds(pl.multiple_of((zz * NY + yy) * self.rows, 16), self.rows)]
+
+    def half(self, c, zz, yy, h):
+        hr = self.rows // 2
+        return self.ref.at[c, pl.ds(pl.multiple_of((zz * NY + yy) * self.rows + h * hr, 16), hr)]
+
+    def up(self, c, zz):
+        b = self.block(c, zz, self.y)
+        return rcopy(b, b, self.zs.at[c, 0, zz], self.zr.at[c, zz], {"shard": (self.z + 1) * NY + self.y})
+
+    def dn(self, c, zz):
+        b = self.block(c, zz, self.y)
+        return rcopy(b, b, self.zs.at[c, 1, zz], self.zr.at[c, zz], {"shard": (self.z - 1) * NY + self.y})
+
+    def ycp(self, c, zz, yy, h):
+        b = self.half(c, zz, yy, h)
+        return rcopy(b, b, self.ys.at[c, zz], self.yr.at[c, zz], {"shard": self.z * NY + 1 - self.y})
+
+    def xcp(self, c, zz, h):
+        b = self.half(c, zz, 1 - self.y, h)
+        return rcopy(b, b, self.xs.at[c, zz], self.xr.at[c, zz], {"ctx": 1 - self.x})
+
+    def own(self, c):
+        z, nz = self.z, self.nz
+
+        @pl.when(z < nz - 1)
+        def _():
+            self.up(c, z).start()
+
+        @pl.when(z > 0)
+        def _():
+            self.dn(c, z).start()
+
+        self.ycp(c, z, self.y, self.x).start()
+
+    def dirs(self, d):
+        return ((self.z - d >= 0, self.z - d, True), (self.z + d < self.nz, self.z + d, False))
+
+    def Z(self, c, d):
+        z, nz = self.z, self.nz
+        for ok, zz, isup in self.dirs(d):
+
+            @pl.when(ok)
+            def _():
+                self.up(c, zz).wait_recv()
+                if isup:
+                    pl.when(z < nz - 1)(lambda: self.up(c, zz).start())
+                else:
+                    pl.when(z > 0)(lambda: self.dn(c, zz).start())
+                self.ycp(c, zz, self.y, self.x).start()
+
+    def each(self, d, f):
+        if d == 0:
+            f(self.z)
+        else:
+            for ok, zz, _ in self.dirs(d):
+                pl.when(ok)(functools.partial(f, zz))
+
+    def Y(self, c, d):
+        def f(zz):
+            self.ycp(c, zz, 1 - self.y, self.x).wait_recv()
+            self.xcp(c, zz, self.x).start()
+
+        self.each(d, f)
+
+    def X(self, c, d):
+        self.each(d, lambda zz: self.xcp(c, zz, 1 - self.x).wait_recv())
+
+    def finish(self, c):
+        z, nz = self.z, self.nz
+        pl.when(z < nz - 1)(lambda: self.up(c, z).wait_send())
+        pl.when(z > 0)(lambda: self.dn(c, z).wait_send())
+        for d in range(1, nz):
+            for ok, zz, isup in self.dirs(d):
+                if isup:
+                    pl.when(both(ok, z < nz - 1))(lambda: self.up(c, zz).wait_send())
+                else:
+                    pl.when(both(ok, z > 0))(lambda: self.dn(c, zz).wait_send())
+        for zz in range(nz):
+            self.ycp(c, zz, self.y, self.x).wait_send()
+            self.xcp(c, zz, self.x).wait_send()
+
+    @staticmethod
+    def sems(nc, nz):
+        D = pltpu.SemaphoreType.DMA
+        return [D((nc, 2, nz)), D((nc, nz)), D((nc, nz)), D((nc, nz)), D((nc, nz)), D((nc, nz))]
+
+
+class Scatter:
+    block, half = Gather.block, Gather.half
+
+    def __init__(self, ref, bufs, rows, nz, sems):
+        self.ref, self.rows, self.nz = ref, rows, nz
+        self.xb, self.yb, self.zb, self.fb = bufs
+        self.xs, self.ys, self.zs, self.fs, self.xr, self.yr, self.zr, self.fr = sems
+        s = lax.axis_index("shard")
+        self.z, self.y, self.x = s // NY, s % NY, lax.axis_index("ctx")
+
+    def xcp(self, c, zz):
+        return rcopy(self.half(c, zz, 1 - self.y, 1 - self.x), self.xb.at[c, zz], self.xs.at[c, zz], self.xr.at[c, zz], {"ctx": 1 - self.x})
+
+    def ycp(self, c, zz):
+        return rcopy(self.half(c, zz, 1 - self.y, self.x), self.yb.at[c, zz], self.ys.at[c, zz], self.yr.at[c, zz], {"shard": self.z * NY + 1 - self.y})
+
+    def zcp(self, c, i, zz, src):
+        to = self.z + 1 if i == 0 else self.z - 1
+        slot = zz if i == 0 else jnp.where(zz == to, self.nz, zz)
+        return rcopy(src, self.zb.at[c, slot], self.zs.at[c, i, zz], self.zr.at[c, i, zz], {"shard": to * NY + self.y})
+
+    def fcp(self, c):
+        return rcopy(self.fb.at[c, 0], self.fb.at[c, 1], self.fs.at[c], self.fr.at[c], {"ctx": 1 - self.x})
+
+    def start(self, c):
+        for zz in range(self.nz):
+            self.xcp(c, zz).start()
+
+    def X(self, c):
+        for zz in range(self.nz):
+            self.xcp(c, zz).wait_recv()
+            h = self.half(c, zz, 1 - self.y, self.x)
+            h[...] = (h[...].astype(F32) + self.xb[c, zz].astype(F32)).astype(BF)
+            self.ycp(c, zz).start()
+
+    def Y(self, c):
+        z, nz = self.z, self.nz
+        for zz in range(nz):
+            self.ycp(c, zz).wait_recv()
+            h = self.half(c, zz, self.y, self.x)
+            h[...] = (h[...].astype(F32) + self.yb[c, zz].astype(F32)).astype(BF)
+            if zz > 0:
+                pl.when(z == 0)(lambda: self.zcp(c, 0, zz, self.block(c, zz, self.y)).start())
+            if zz < nz - 1:
+                pl.when(z == nz - 1)(lambda: self.zcp(c, 1, zz, self.block(c, zz, self.y)).start())
+
+    def Z(self, c, k):
+        z, nz = self.z, self.nz
+        zm = nz - 1 - z
+        for i, ok, zz in ((0, both(z >= 1, k >= z), nz - 1 - k + z), (1, both(zm >= 1, k >= zm), k - zm)):
+
+            @pl.when(ok)
+            def _():
+                slot = zz if i == 0 else jnp.where(zz == z, nz, zz)
+                ref = self.zb.at[c, slot]
+                rcopy(ref, ref, self.zs.at[c, i, zz], self.zr.at[c, i, zz], {"ctx": self.x}).wait_recv()
+
+                @pl.when(zz != z)
+                def _():
+                    ref[...] = (ref[...].astype(F32) + self.block(c, zz, self.y)[...].astype(F32)).astype(BF)
+                    self.zcp(c, i, zz, ref).start()
+
+    def F(self, c):
+        z, nz = self.z, self.nz
+        fb0 = self.fb.at[c, 0]
+        fb0[...] = self.block(c, z, self.y)[...]
+
+        @pl.when(z > 0)
+        def _():
+            fb0[...] = (fb0[...].astype(F32) + self.zb[c, z].astype(F32)).astype(BF)
+
+        @pl.when(z < nz - 1)
+        def _():
+            fb0[...] = (fb0[...].astype(F32) + self.zb[c, nz].astype(F32)).astype(BF)
+
+        self.fcp(c).start()
+
+    def G(self, c):
+        self.fcp(c).wait_recv()
+        return self.fb[c, 0].astype(F32) + self.fb[c, 1].astype(F32)
+
+    def finish(self, c):
+        z, nz = self.z, self.nz
+        for zz in range(nz):
+            self.xcp(c, zz).wait_send()
+            self.ycp(c, zz).wait_send()
+            b = self.block(c, zz, self.y)
+            pl.when(both(z < nz - 1, zz > z))(lambda: self.zcp(c, 0, zz, b).wait_send())
+            pl.when(both(z > 0, zz < z))(lambda: self.zcp(c, 1, zz, b).wait_send())
+        self.fcp(c).wait_send()
+
+    @staticmethod
+    def sems(nc, nz):
+        D = pltpu.SemaphoreType.DMA
+        return [D((nc, nz)), D((nc, nz)), D((nc, 2, nz)), D((nc,)), D((nc, nz)), D((nc, nz)), D((nc, 2, nz)), D((nc,))]
+
+
+def block_kernel(names, nz, NC, half, BQ, BK, *refs):
+    w = types.SimpleNamespace(**dict(zip(names, refs)))
+    T, D = w.hb.shape
+    n = nz * NY
+    rows = D // n
+    hr = rows // 2
+    FC = w.act.shape[2]
+    CA = w.attd.shape[1]
+    QO = NC
+    npair = CA // 128
+    nt = T // BQ
+    ns = nt * npair
+    sub = half // BQ
+    s, x, t = lax.axis_index("shard"), lax.axis_index("ctx"), lax.axis_index("tp")
+    me = x * n + s
+    g = Gather(w.G, rows, nz, [getattr(w, f"ga{i}") for i in range(6)])
+    gk = Gather(w.gkv, rows, nz, [getattr(w, f"gb{i}") for i in range(6)])
+    r = Scatter(w.GR, (w.xb, w.yb, w.zb, w.fb), rows, nz, [getattr(w, f"sc{i}") for i in range(8)])
+    lane = lax.broadcasted_iota(jnp.int32, (BQ, 128), 1)
+    low = lane < 64
+
+    def tile(i):
+        return pl.ds(pl.multiple_of(i * BQ, BQ), BQ)
+
+    own = pl.ds(pl.multiple_of(s * rows, 16), rows)
+    loads = [(w.q, w.G.at[QO, own, pl.ds(0, CA)]), (w.o, w.G.at[QO, own, pl.ds(CA, CA)]), (w.kv, w.gkv.at[0, own]), (w.lnp, w.lb.at[s]), (w.hidden, w.hb), (w.cot, w.cb)]
+    for c in range(NC):
+        loads.append((w.up.at[:, pl.ds(c * FC, FC)], w.G.at[c, own, pl.ds(0, FC)]))
+        loads.append((w.dw.at[:, pl.ds(c * FC, FC)], w.G.at[c, own, pl.ds(FC, FC)]))
+    loads = [pltpu.make_async_copy(a, b, w.lsem.at[i]) for i, (a, b) in enumerate(loads)]
+    for c in loads:
+        c.start()
+
+    peers = [(s, 1 - x)] + [(lax.rem(s + k, n), xx) for k in range(1, n) for xx in (x, 1 - x)]
+    bar = pltpu.get_barrier_semaphore()
+    for ps, px in peers:
+        pl.semaphore_signal(bar, inc=1, device_id={"shard": ps, "ctx": px}, device_id_type=MESH)
+    pl.semaphore_signal(bar, inc=1, device_id={"tp": 1 - t}, device_id_type=MESH)
+    pl.semaphore_wait(bar, 2 * n)
+
+    for c in loads[:4]:
+        c.wait()
+    lns = [rcopy(w.lb.at[s], w.lb.at[s], w.lns.at[k - 1], w.lnr.at[s], {"shard": lax.rem(s + k, n)}) for k in range(1, n)]
+    for c in lns:
+        c.start()
+    gk.own(0)
+    g.own(QO)
+    for c in loads[4:]:
+        c.wait()
+
+    @pl.loop(0, nt)
+    def _(i):
+        base = w.bo[2 * x + i // sub] * half + lax.rem(i, sub) * BQ
+        pos = (base + lax.broadcasted_iota(jnp.int32, (BQ, 128), 0)).astype(F32)
+        ang = pos * w.freq[0:1, :]
+        l64 = lax.rem(lane, 64)
+        w.tc[tile(i), :] = jnp.where(l64 < 16, jnp.cos(ang), 1.0)
+        sn = jnp.sin(ang)
+        w.ts[tile(i), :] = jnp.where(l64 < 8, -sn, jnp.where(l64 < 16, sn, 0.0))
+        w.ct[:, tile(i)] = w.cb[tile(i), :].T
+
+    def rotated(v, i, sign):
+        sw = jnp.where(lax.rem(lane, 16) < 8, pltpu.roll(v, 120, 1), pltpu.roll(v, 8, 1))
+        turn = sw * w.ts[tile(i), :]
+        return v * w.tc[tile(i), :] + (turn if sign > 0 else -turn)
+
+    def head(d):
+        for e in (gk, g):
+            c = 0 if e is gk else QO
+            if d < nz:
+                e.Z(c, d)
+            e.Y(c, d - 1)
+            if d > 1:
+                e.X(c, d - 2)
+
+    head(1)
+    g.own(0)
+    for k in range(1, n):
+        f = lax.rem(s + n - k, n)
+        rcopy(w.lb.at[f], w.lb.at[f], w.lns.at[0], w.lnr.at[f], {"shard": f}).wait_recv()
+    prm = None
+    for k in range(n):
+        piece = jnp.concatenate([w.lb[k], jnp.zeros((8, D - 128), F32)], axis=1)
+        piece = pltpu.roll(piece, k * rows, 1) if k else piece
+        prm = piece if prm is None else prm + piece
+    w.prm[...] = prm
+
+    def standardized(i):
+        v = w.hb[tile(i), :].astype(F32)
+        v = v - jnp.mean(v, axis=1, keepdims=True)
+        rstd = lax.rsqrt(jnp.mean(v * v, axis=1, keepdims=True) + 1e-05)
+        return v * rstd, rstd
+
+    @pl.loop(0, nt)
+    def _(i):
+        xh, _ = standardized(i)
+        na = (xh * w.prm[0:1, :] + w.prm[1:2, :]).astype(BF)
+        nf = (xh * w.prm[2:3, :] + w.prm[3:4, :]).astype(BF)
+        w.na[tile(i), :] = na
+        w.nf[tile(i), :] = nf
+        w.nat[:, tile(i)] = na.T
+        w.nft[:, tile(i)] = nf.T
+
+    for d in range(2, nz + 2):
+        if d <= nz:
+            head(d)
+    for e, c in ((gk, 0), (g, QO)):
+        e.X(c, nz - 1)
+
+    def pump(c, d):
+        @pl.when(c < NC)
+        def _():
+            if d == 1:
+                pl.when(c + 1 < NC)(lambda: g.own(c + 1))
+            g.Z(c, d)
+            g.Y(c, d - 1)
+            if d == nz - 1:
+                g.X(c, 0)
+
+        @pl.when(both(c >= 1, c <= NC))
+        def _():
+            if d == 1:
+                g.Y(c - 1, nz - 1)
+            g.X(c - 1, d)
+
+    @pl.loop(0, nt)
+    def _(i):
+        kvp = dot(w.na[tile(i), :], w.gkv[0])
+        kvp = jnp.where(low, rotated(kvp, i, 1), kvp).astype(BF)
+        w.kvb[0, tile(i), :] = kvp
+        w.keys[tile(i), :] = kvp[:, :64]
+        w.values[tile(i), :] = pltpu.roll(kvp.astype(F32), 64, 1)[:, :64].astype(BF)
+
+    kvx = rcopy(w.kvb.at[0], w.kvb.at[1], w.es.at[0], w.er.at[0], {"ctx": 1 - x})
+    kvx.start()
+
+    order = [w.bo[2 * x], w.bo[2 * x + 1], w.bo[2 * (1 - x)], w.bo[2 * (1 - x) + 1]]
+    lane1 = lax.broadcasted_iota(jnp.int32, (1, 128), 1)
+
+    @pl.loop(0, nt)
+    def _(i):
+        qp = dot(w.na[tile(i), :], w.G[QO, :, 0:CA])
+        ga = dot(w.cb[tile(i), :], w.G[QO, :, CA : 2 * CA])
+        mine = w.bo[2 * x + i // sub]
+        hide = jnp.zeros((1, 128), F32)
+        for j in range(4):
+            hide = jnp.where(lane1 == 64 + j, jnp.where(order[j] <= mine, 0.0, NEG), hide)
+        for p in range(npair):
+            st = i * npair + p
+            qs = rotated(qp[:, 128 * p : 128 * p + 128], i, 1).astype(BF).astype(F32) * 0.125
+            w.qx[st, 0:BQ, :] = jnp.where(low, qs, hide).astype(BF)
+            w.qx[st, BQ : 2 * BQ, :] = jnp.where(low, pltpu.roll(qs, 64, 1), hide).astype(BF)
+            qt = qs.astype(BF).T
+            w.qt[st, :, 0:BQ] = qt[:64]
+            w.qt[st, :, BQ : 2 * BQ] = qt[64:]
+            gp = ga[:, 128 * p : 128 * p + 128]
+            w.dox[st, 0:BQ, :] = jnp.where(low, gp, 0.0).astype(BF)
+            w.dox[st, BQ : 2 * BQ, :] = jnp.where(low, pltpu.roll(gp, 64, 1), 0.0).astype(BF)
+            gt = gp.astype(BF).T
+            w.dt[st, :, 0:BQ] = gt[:64]
+            w.dt[st, :, BQ : 2 * BQ] = gt[64:]
+        for d in range(1, nz):
+            pl.when(i == d - 1)(functools.partial(pump, 0, d))
+
+    kvx.wait_recv()
+
+    @pl.loop(0, 2 * nt)
+    def _(i):
+        kvf = w.kvb[i // nt, tile(lax.rem(i, nt)), :].astype(F32)
+        hot = jnp.where(lane == 64 + i // sub, 1.0, 0.0)
+        w.kx[tile(i), :] = jnp.where(low, kvf, hot).astype(BF)
+        w.k0[tile(i), :] = jnp.where(low, kvf, 0.0).astype(BF)
+        w.v0[tile(i), :] = jnp.where(low, pltpu.roll(kvf, 64, 1), 0.0).astype(BF)
+
+    w.acc[...] = jnp.zeros_like(w.acc)
+
+    def feed_forward():
+        @pl.loop(0, NC)
+        def _(c):
+            @pl.loop(0, nt)
+            def _(i):
+                hp = dot(w.nf[tile(i), :], w.G[c, :, 0:FC])
+                da = dot(w.cb[tile(i), :], w.G[c, :, FC : 2 * FC])
+                cdf = 0.5 + 0.5 * lax.erf(hp * 0.7071067811865476)
+                pdf = jnp.exp(-0.5 * hp * hp) * 0.3989422804014327
+                w.act[c, tile(i), :] = (hp * cdf).astype(BF)
+                w.dh[c, tile(i), :] = (da * (cdf + hp * pdf)).astype(BF)
+                pl.when(i == 1)(lambda: pump(c + 2, 1))
+                pl.when(i == 3)(lambda: pump(c + 2, 2))
+
+            pl.when(c >= 1)(lambda: r.X(c - 1))
+
+            @pl.loop(0, D // BQ)
+            def _(m):
+                w.GR[c, tile(m), 0:FC] = dot(w.nft[tile(m), :], w.dh[c]).astype(BF)
+                w.GR[c, tile(m), FC : 2 * FC] = dot(w.ct[tile(m), :], w.act[c]).astype(BF)
+
+            r.start(c)
+            pump(c + 2, 3)
+            pl.when(c >= 2)(lambda: r.Y(c - 2))
+
+        @pl.loop(0, nt)
+        def _(i):
+            dn = dot_nt(w.dh[0, tile(i), :], w.G[0, :, 0:FC])
+            br = dot_nt(w.act[0, tile(i), :], w.G[0, :, FC : 2 * FC])
+            for c in range(1, NC):
+                dn = dn + dot_nt(w.dh[c, tile(i), :], w.G[c, :, 0:FC])
+                br = br + dot_nt(w.act[c, tile(i), :], w.G[c, :, FC : 2 * FC])
+            w.na[tile(i), :] = dn.astype(BF)
+            w.act[0, tile(i), :] = br[:, :FC].astype(BF)
+            w.act[1, tile(i), :] = br[:, FC:].astype(BF)
+
+        dnx.start()
+        r.X(NC - 1)
+        r.Y(NC - 2)
+
+    dnx = rcopy(w.na, w.dnr, w.es.at[1], w.er.at[1], {"tp": 1 - t})
+
+    def own_out(c, v):
+        cols = pl.ds(pl.multiple_of(c * FC, FC), FC)
+        w.ou[:, cols] = v[:, :FC]
+        w.od[:, cols] = v[:, FC:]
+
+    def within(h, f):
+        pl.when(both(h >= 0, h < NC))(lambda: f(h))
+
+    def scatter_step(i):
+        pl.when(i == 0)(lambda: r.Y(NC - 1))
+        h = i // 2
+
+        @pl.when(lax.rem(i, 2) == 0)
+        def _():
+            within(h, lambda c: r.Z(c, 1))
+            within(h - 1, lambda c: r.Z(c, 3))
+            within(h - 2, lambda c: own_out(c, r.G(c)))
+
+        @pl.when(lax.rem(i, 2) == 1)
+        def _():
+            within(h, lambda c: r.Z(c, 2))
+            within(h - 1, lambda c: r.F(c))
+
+    first = nz - 1
+
+    def attention(st):
+        i = st // npair
+        p = lax.rem(st, npair)
+        own_b = i // sub
+        r0 = lax.rem(i, sub) * BQ
+        R = 2 * BQ
+        nk = w.kx.shape[0] // BK
+        per = half // BK
+        offs = []
+        for j in range(nk):
+            if j < per:
+                off = own_b * half + j * BK
+            elif j < 2 * per:
+                off = (1 - own_b) * half + (j - per) * BK
+            else:
+                off = j * BK
+            offs.append(pl.ds(pl.multiple_of(off, BK), BK))
+        cols = [slice(j * BK, (j + 1) * BK) for j in range(nk)]
+        q, do = w.qx[st], w.dox[st]
+        m = None
+        for j in range(nk):
+            sc = dot_nt(q, w.kx[offs[j], :])
+            if j < per:
+                row = lax.rem(lax.broadcasted_iota(jnp.int32, (R, BK), 0), BQ) + r0
+                col = lax.broadcasted_iota(jnp.int32, (R, BK), 1) + j * BK
+                sc = jnp.where(col <= row, sc, NEG)
+            w.ss[:, cols[j]] = sc
+            for k in range(BK // 128):
+                mk = sc[:, k * 128 : (k + 1) * 128]
+                m = mk if m is None else jnp.maximum(m, mk)
+        m = jnp.max(m, axis=1, keepdims=True)
+        l = o = None
+        for j in range(nk):
+            e = jnp.exp(w.ss[:, cols[j]] - m)
+            w.ss[:, cols[j]] = e
+            for k in range(BK // 128):
+                lk = e[:, k * 128 : (k + 1) * 128]
+                l = lk if l is None else l + lk
+            eb = e.astype(BF)
+            w.ps[:, cols[j]] = eb
+            oj = dot(eb, w.v0[offs[j], :])
+            o = oj if o is None else o + oj
+        inv = 1.0 / jnp.sum(l, axis=1, keepdims=True)
+        o = o * inv
+        delta = jnp.sum(o * do.astype(F32), axis=1, keepdims=True)
+        inv_row = jnp.transpose(jnp.broadcast_to(inv, (R, 128)))[:1, :]
+        qs = (w.qt[st].astype(F32) * inv_row).astype(BF)
+        dos = (w.dt[st].astype(F32) * inv_row).astype(BF)
+        dq = None
+        for j in range(nk):
+            dp = dot_nt(do, w.v0[offs[j], :])
+            ds = (w.ss[:, cols[j]] * (dp - delta)).astype(BF)
+            dj = dot(ds, w.k0[offs[j], :])
+            dq = dj if dq is None else dq + dj
+            w.acc[0:64, offs[j]] += dot(qs, ds)
+            w.acc[64:128, offs[j]] += dot(dos, w.ps[:, cols[j]])
+        dq = dq * (inv * 0.125)
+        pair = pl.ds(pl.multiple_of(p * 128, 128), 128)
+        w.attd[tile(i), pair] = (o[:BQ] + pltpu.roll(o[BQ:], 64, 1)).astype(BF)
+        w.gq[tile(i), pair] = rotated(dq[:BQ] + pltpu.roll(dq[BQ:], 64, 1), i, -1).astype(BF)
+
+    @pl.loop(0, ns)
+    def _(st):
+        for d in range(1, nz):
+            pl.when(st == d - 1)(functools.partial(pump, 1, d))
+        pl.when(st == first)(feed_forward)
+        pl.when(st >= first)(lambda: scatter_step(st - first))
+        attention(st)
+
+    for i in range(2):
+        w.dS[i] = w.acc[:, i * T : (i + 1) * T].astype(BF)
+    dtp = rcopy(w.dS, w.dR, w.es.at[2], w.er.at[2], {"tp": 1 - t})
+    dtp.start()
+    dnx.wait_recv()
+
+    @pl.loop(0, nt)
+    def _(i):
+        br = dot_nt(w.attd[tile(i), :], w.G[QO, :, CA : 2 * CA])
+        w.act[0, tile(i), :] = (w.act[0, tile(i), :].astype(F32) + br[:, :FC]).astype(BF)
+        w.act[1, tile(i), :] = (w.act[1, tile(i), :].astype(F32) + br[:, FC:]).astype(BF)
+
+    brx = rcopy(w.act.at[pl.ds(0, 2)], w.dh.at[pl.ds(0, 2)], w.es.at[3], w.er.at[3], {"tp": 1 - t})
+    brx.start()
+
+    @pl.loop(0, D // BQ)
+    def _(m):
+        w.GR[QO, tile(m), 0:CA] = dot(w.nat[tile(m), :], w.gq[...]).astype(BF)
+        w.GR[QO, tile(m), CA : 2 * CA] = dot(w.ct[tile(m), :], w.attd[...]).astype(BF)
+
+    r.start(QO)
+    dtp.wait_recv()
+    w.dX[...] = (w.dS[1].astype(F32) + w.dR[1].astype(F32)).astype(BF)
+    dxx = rcopy(w.dX, w.dXR, w.es.at[4], w.er.at[4], {"ctx": 1 - x})
+    dxx.start()
+
+    @pl.loop(0, nt)
+    def _(i):
+        ga = dot_nt(w.gq[tile(i), :], w.G[QO, :, 0:CA])
+        w.act[2, tile(i), :] = ga[:, :FC].astype(BF)
+        w.act[3, tile(i), :] = ga[:, FC:].astype(BF)
+
+    gax = rcopy(w.act.at[pl.ds(2, 2)], w.dh.at[pl.ds(2, 2)], w.es.at[5], w.er.at[5], {"tp": 1 - t})
+    gax.start()
+    r.F(NC - 1)
+    r.X(QO)
+    brx.wait_recv()
+
+    @pl.loop(0, nt)
+    def _(i):
+        for k in range(2):
+            cs = slice(k * FC, (k + 1) * FC)
+            v = w.act[k, tile(i), :].astype(F32) + w.dh[k, tile(i), :].astype(F32)
+            w.nf[tile(i), cs] = (w.hb[tile(i), cs].astype(F32) + v).astype(BF)
+
+    outx = pltpu.make_async_copy(w.nf, w.out_tokens, w.osem.at[0])
+    outx.start()
+    r.Y(QO)
+    dxx.wait_recv()
+
+    @pl.loop(0, nt)
+    def _(i):
+        v = w.dS[0, :, tile(i)].astype(F32) + w.dR[0, :, tile(i)].astype(F32) + w.dXR[:, tile(i)].astype(F32)
+        v = v.T
+        w.gkb[tile(i), :] = jnp.where(low, rotated(v, i, -1), v).astype(BF)
+
+    w.kvS[...] = dot(w.nat[...], w.gkb[...]).astype(BF)
+
+    def kv_rows(owner):
+        return pl.ds(pl.multiple_of(owner * rows + t * hr, 16), hr)
+
+    kvs = [rcopy(w.kvS.at[kv_rows(ps)], w.kvR.at[me], w.ks.at[i], w.kr.at[me], {"shard": ps, "ctx": px}) for i, (ps, px) in enumerate(peers)]
+    for c in kvs:
+        c.start()
+    r.Z(QO, 1)
+    gax.wait_recv()
+    w.lg[...] = jnp.zeros_like(w.lg)
+
+    @pl.loop(0, nt)
+    def _(i):
+        xh, rstd = standardized(i)
+        kvg = dot_nt(w.gkb[tile(i), :], w.gkv[0])
+        gn = jnp.concatenate([w.act[k, tile(i), :].astype(F32) + w.dh[k, tile(i), :].astype(F32) for k in (2, 3)], axis=1) + kvg
+        gf = w.na[tile(i), :].astype(F32) + w.dnr[tile(i), :].astype(F32)
+        e = gn * w.prm[0:1, :] + gf * w.prm[2:3, :]
+        e = rstd * (e - jnp.mean(e, axis=1, keepdims=True) - xh * jnp.mean(e * xh, axis=1, keepdims=True))
+        w.hg[tile(i), :] = w.cb[tile(i), :].astype(F32) + e
+        w.lg[0:1, :] += jnp.sum(gn * xh, axis=0, keepdims=True)
+        w.lg[1:2, :] += jnp.sum(gn, axis=0, keepdims=True)
+        w.lg[2:3, :] += jnp.sum(gf * xh, axis=0, keepdims=True)
+        w.lg[3:4, :] += jnp.sum(gf, axis=0, keepdims=True)
+        pl.when(i == 1)(lambda: r.Z(QO, 2))
+
+    lg = w.lg[...]
+    keep = lax.broadcasted_iota(jnp.int32, (8, 128), 1) < rows
+    for k in range(n):
+        v = pltpu.roll(lg, D - k * rows, 1) if k else lg
+        w.lS[k] = jnp.where(keep, v[:, :128], 0.0)
+    lgs = [rcopy(w.lS.at[ps], w.lR.at[me], w.ls.at[i], w.lr.at[me], {"shard": ps, "ctx": px}) for i, (ps, px) in enumerate(peers)]
+    for c in lgs:
+        c.start()
+    own_out(NC - 1, r.G(NC - 1))
+    r.Z(QO, 3)
+    r.F(QO)
+
+    def arrived(ref, sems, i, ps, px):
+        k = px * n + ps
+        return rcopy(ref.at[k], ref.at[k], sems.at[i], sems.at[k], {"shard": ps, "ctx": px})
+
+    for i, (ps, px) in enumerate(peers):
+        arrived(w.kvR, w.kr, i, ps, px).wait_recv()
+    w.kvR[me] = w.kvS[kv_rows(s), :]
+    v = w.kvR[0].astype(F32)
+    for k in range(1, 2 * n):
+        v = v + w.kvR[k].astype(F32)
+    w.kvF[t] = v
+    kfx = rcopy(w.kvF.at[t], w.kvF.at[t], w.es.at[6], w.er.at[6], {"tp": 1 - t})
+    kfx.start()
+    for i, (ps, px) in enumerate(peers):
+        arrived(w.lR, w.lr, i, ps, px).wait_recv()
+    w.lR[me] = w.lS[s]
+    v = w.lR[0]
+    for k in range(1, 2 * n):
+        v = v + w.lR[k]
+    w.lno[...] = v
+    rcopy(w.kvF.at[1 - t], w.kvF.at[1 - t], w.es.at[6], w.er.at[6], {"tp": 1 - t}).wait_recv()
+    w.okv[0:hr, :] = w.kvF[0]
+    w.okv[hr:rows, :] = w.kvF[1]
+    v = r.G(QO)
+    w.oq[...] = v[:, :CA]
+    w.oo[...] = v[:, CA:]
+    outx.wait()
+    for c in lns + [kvx, dnx, dtp, brx, dxx, gax, kfx] + kvs + lgs:
+        c.wait_send()
+    gk.finish(0)
+    for c in range(NC + 1):
+        g.finish(c)
+        r.finish(c)
+
+
+def block_call(bo, freq, hidden, cot, lnp, up, dw, q, o, kv, nz, half, cid):
+    T, D = hidden.shape
+    rows, CU = up.shape
+    CA, CK = q.shape[1], kv.shape[1]
+    FC = CA
+    NC = CU // FC
+    n = nz * NY
+    hr = rows // 2
+    BQ, BK = 256, 512
+    ns = T // BQ * (CA // 128)
+    A = pl.BlockSpec(memory_space=pl.ANY)
+    V = pl.BlockSpec(memory_space=pltpu.VMEM)
+    S = pl.BlockSpec(memory_space=pltpu.SMEM)
+    Dm = pltpu.SemaphoreType.DMA
+    ins = ["bo", "freq", "hidden", "cot", "lnp", "up", "dw", "q", "o", "kv"]
+    sd = jax.ShapeDtypeStruct
+    outs = {
+        "out_tokens": (sd((T, D), BF), A), "keys": (sd((T, 64), BF), V), "values": (sd((T, 64), BF), V), "hg": (sd((T, D), F32), V),
+        "lno": (sd((8, 128), F32), V), "oq": (sd((rows, CA), F32), V), "okv": (sd((rows, CK), F32), V), "oo": (sd((rows, CA), F32), V),
+        "ou": (sd((rows, CU), F32), V), "od": (sd((rows, CU), F32), V),
+    }
+    b = lambda *sh: pltpu.VMEM(sh, BF)
+    f = lambda *sh: pltpu.VMEM(sh, F32)
+    scr = {
+        "hb": b(T, D), "cb": b(T, D), "ct": b(D, T), "na": b(T, D), "nf": b(T, D), "nft": b(D, T), "nat": b(D, T),
+        "G": b(NC + 1, D, 2 * FC), "gkv": b(1, D, CK), "GR": b(NC + 1, D, 2 * FC),
+        "xb": b(NC + 1, nz, hr, 2 * FC), "yb": b(NC + 1, nz, hr, 2 * FC), "zb": b(NC + 1, nz + 1, rows, 2 * FC), "fb": b(NC + 1, 2, rows, 2 * FC),
+        "lb": f(n, 8, 128), "act": b(NC, T, FC), "dh": b(NC, T, FC), "dnr": b(T, D),
+        "qx": b(ns, 2 * BQ, 128), "dox": b(ns, 2 * BQ, 128), "qt": b(ns, 64, 2 * BQ), "dt": b(ns, 64, 2 * BQ),
+        "kvb": b(2, T, CK), "kx": b(2 * T, 128), "k0": b(2 * T, 128), "v0": b(2 * T, 128),
+        "ss": f(2 * BQ, 2 * T), "ps": b(2 * BQ, 2 * T), "attd": b(T, CA), "gq": b(T, CA), "acc": f(128, 2 * T),
+        "tc": f(T, 128), "ts": f(T, 128), "dS": b(2, 128, T), "dR": b(2, 128, T), "dX": b(128, T), "dXR": b(128, T), "gkb": b(T, 128),
+        "kvS": b(D, CK), "kvR": b(2 * n, hr, CK), "kvF": f(2, hr, CK), "lS": f(n, 8, 128), "lR": f(2 * n, 8, 128), "prm": f(8, D), "lg": f(8, D),
+        "lsem": Dm((6 + 2 * NC,)), "lns": Dm((n - 1,)), "lnr": Dm((n,)), "es": Dm((7,)), "er": Dm((7,)), "osem": Dm((1,)),
+        "ks": Dm((2 * n - 1,)), "kr": Dm((2 * n,)), "ls": Dm((2 * n - 1,)), "lr": Dm((2 * n,)),
+    }
+    scr.update({f"ga{i}": v for i, v in enumerate(Gather.sems(NC + 1, nz))})
+    scr.update({f"gb{i}": v for i, v in enumerate(Gather.sems(1, nz))})
+    scr.update({f"sc{i}": v for i, v in enumerate(Scatter.sems(NC + 1, nz))})
+    names = ins + list(outs) + list(scr)
+    res = pl.pallas_call(
+        functools.partial(block_kernel, names, nz, NC, half, BQ, BK),
+        out_shape=tuple(v[0] for v in outs.values()),
+        in_specs=[S, V] + [A] * 8,
+        out_specs=tuple(v[1] for v in outs.values()),
+        scratch_shapes=list(scr.values()),
+        compiler_params=pltpu.CompilerParams(collective_id=cid, has_side_effects=True, vmem_limit_bytes=67043328),
+        name="block",
+    )(bo, freq, hidden, cot, lnp, up, dw, q, o, kv)
+    return dict(zip(outs, res))
+
+
+def fits(mesh):
+    return mesh.shape["shard"] == 8 and mesh.shape["ctx"] == 2
+
+
+def fast_device(hidden, block_order, ln1_gain, ln1_bias, ln2_gain, ln2_bias, q_weight, kv_weight, o_weight, up_weight, down_weight, cotangent):
+    seqs, span, width = hidden.shape
+    hd = kv_weight.shape[1] // 2
+    rows = ln1_gain.shape[0]
+    lnp = jnp.pad(jnp.stack([ln1_gain, ln1_bias, ln2_gain, ln2_bias]).astype(F32), ((0, 4), (0, 128 - rows)))
+    freq = 10000.0 ** (-2.0 * (np.arange(128) % (ROT // 2)) / ROT)
+    freq = jnp.asarray(np.broadcast_to(freq, (8, 128)), F32)
+    v = block_call(block_order, freq, hidden.reshape(span, width), cotangent.reshape(span, width), lnp, up_weight, down_weight, q_weight, o_weight, kv_weight, width // rows // NY, span // 2, 1)
+    lo = v["lno"]
+    return (v["out_tokens"][None], v["keys"][None], v["values"][None], v["hg"][None], lo[0, :rows], lo[1, :rows], lo[2, :rows], lo[3, :rows], v["oq"], v["okv"], v["oo"], v["ou"], v["od"])
+
+
 def solution(mesh):
     return jax.shard_map(
-        on_device,
+        fast_device if fits(mesh) else on_device,
         mesh=mesh,
         in_specs=(
             P("shard", "ctx", None),

time: 794 us -> 211 us (0.27)
  waiting for transfers between devices: 274 us -> 0 us
  Pallas kernels: 0 us -> 196 us
  matrix products: 188 us -> 0 us
  blocking collectives: 161 us -> 0 us
  other arithmetic: 89.9 us -> 1.31 us
  local copies, waits for them, and re-layouts: 57.8 us -> 12.9 us
  between operations: 18.3 us -> 0.68 us
    pallas_call x0 -> x1, Pallas kernels: none -> 196 us  [block_call(): pl.pallas_call(functools.partial(block_kernel, names, nz, NC, half, BQ, B...]
    dot_general x21 -> x0, matrix products: 188 us -> none  [the longest x1 33.6 us: backward_one(): jnp.einsum('qd,kd->qk', grad_block, value_block, preferred_element_type=j...]
    reduce_scatter x4 -> x0, waiting for transfers between devices: 166 us -> none  [the longest x1 72 us: on_device(): lax.psum_scatter(grads[7].astype(jnp.bfloat16), 'shard', scatter_dimensio...]
    all_gather x5 -> x0, blocking collectives: 108 us -> none  [the longest x1 33.1 us: on_device(): lax.all_gather(q_weight, 'shard', axis=0, tiled=True)]
    unnamed x12 -> x0, waiting for transfers between devices: 105 us -> none
    convert_element_type x16 -> x0, other arithmetic: 48.7 us -> none  [the longest x1 40.5 us: backward_one(): grad_scores = (probs * (grad_probs - delta)).astype(jnp.bfloat16)]
    unnamed x2 -> x0, blocking collectives: 44 us -> none
    reduce_sum x7 -> x0, other arithmetic: 30.6 us -> none  [the longest x1 23.6 us: one_block(): total = total * factor + jnp.sum(weights, axis=1)]
  transfers between devices with their start and end apart: 10 -> 0, of which waited for: 6 -> 0; matrix products, arithmetic and copies ran while one was open for 41% -> 0% of each run, Pallas kernels for 0% -> 0%
where the time goes in v2:
time: 211 us; the launch traced here: 210 us
  Pallas kernels  196 us (93%)
  local copies, waits for them, and re-layouts  12.9 us (6%)
    pallas_call x1, Pallas kernels, block_call(): pl.pallas_call(functools.partial(block_kernel, names, nz, NC, half, BQ, B...  196 us
    unnamed x21, local copies, waits for them, and re-layouts  11.5 us

profile of v2, /device:TPU:0, one launch (start us, length us, event | category | flops | bytes accessed | tf_op | source)
XLA Modules:
  0.0 210.5 jit_solution(14394281237304775400)
XLA Ops:
  0.6 1.3 fusion.9.refs_4_
  2.0 195.6 %block.1 = (bf16[1024,768]{1,0:T(8,128)(2,1)}, bf16[1024,64]{1,0:T(8,128)(2,1)}, bf16[1024,64]{1,0:T(8,128)(2,1)}, f32[1024,768]{1,0:T(8,128)}, f32[8,128]{1,0:T...) custom-call(s32[4]{0:T(128)} %refs_0_.1, ...), custom_call_target="tpu_custom_call" | custom-call | tf_op jit(solution)/shard_map/block/pallas_call | solution.py:1016
  197.6 1.7 copy.26
  199.3 1.3 slice_bitcast_fusion
  200.7 1.7 copy.27
  202.4 0.0 copy-start
  202.4 2.8 %copy.35 = bf16[1,1024,768]{2,1,0:T(8,128)(2,1)} copy(bf16[1,1024,768]{2,1,0:T(8,128)(2,1)} %bitcast.19) | data formatting | bytes 3145728
  205.2 0.0 copy-done
  205.2 0.0 copy-start.4
  205.2 0.0 copy-start.5
  205.2 0.0 copy-start.3
  205.2 0.0 copy-start.2
  205.2 1.7 copy.36
  206.9 0.0 copy-done.4
  206.9 0.0 copy-start.1
  206.9 0.7 copy.37
  207.6 0.0 copy-done.5
  207.6 0.6 copy.38
  208.2 0.0 copy-done.3
  208.2 0.7 copy.39
  208.8 0.0 copy-done.2
  208.9 0.8 copy.40
  209.7 0.0 copy-done.1
  209.7 0.8 copy.41
Async XLA Ops:
  202.4 2.8 %copy-start = (f32[1024,768]{1,0:T(8,128)S(1)}, f32[1024,768]{1,0:T(8,128)}, u32[]{:S(2)}) copy-start(f32[1024,768]{1,0:T(8,128)} %get-tuple-element.26) | copy-start | bytes 9437188
  205.2 1.7 copy-start.4
  205.2 2.4 %copy-start.5 = (f32[96,128]{1,0:T(8,128)S(1)}, f32[96,128]{1,0:T(8,128)}, u32[]{:S(2)}) copy-start(f32[96,128]{1,0:T(8,128)} %get-tuple-element.72) | copy-start | bytes 147460
  205.2 3.0 %copy-start.3 = (f32[96,384]{1,0:T(8,128)S(1)}, f32[96,384]{1,0:T(8,128)}, u32[]{:S(2)}) copy-start(f32[96,384]{1,0:T(8,128)} %get-tuple-element.73) | copy-start | bytes 442372
  205.2 3.6 %copy-start.2 = (f32[96,1536]{1,0:T(8,128)S(1)}, f32[96,1536]{1,0:T(8,128)}, u32[]{:S(2)}) copy-start(f32[96,1536]{1,0:T(8,128)} %get-tuple-element.74) | copy-start | bytes 1769476
  206.9 2.8 %copy-start.1 = (f32[96,1536]{1,0:T(8,128)S(1)}, f32[96,1536]{1,0:T(8,128)}, u32[]{:S(2)}) copy-start(f32[96,1536]{1,0:T(8,128)} %get-tuple-element.75) | copy-start | bytes 1769476

commit v3 on v2

--- a/solution.py
+++ b/solution.py
@@ -339,18 +339,23 @@
 
 
 class Gather:
-    def __init__(self, ref, rows, nz, sems):
-        self.ref, self.rows, self.nz = ref, rows, nz
+    def __init__(self, ref, rows, nz, sems, fixed=None, cols=None):
+        self.ref, self.rows, self.nz, self.fixed, self.cols = ref, rows, nz, fixed, cols
         self.zs, self.ys, self.xs, self.zr, self.yr, self.xr = sems
         s = lax.axis_index("shard")
         self.z, self.y, self.x = s // NY, s % NY, lax.axis_index("ctx")
 
+    def view(self, c, rows):
+        if self.cols is None:
+            return self.ref.at[c, rows]
+        return self.ref.at[self.fixed, rows, pl.ds(c * self.cols, self.cols)]
+
     def block(self, c, zz, yy):
-        return self.ref.at[c, pl.ds(pl.multiple_of((zz * NY + yy) * self.rows, 16), self.rows)]
+        return self.view(c, pl.ds(pl.multiple_of((zz * NY + yy) * self.rows, 16), self.rows))
 
     def half(self, c, zz, yy, h):
         hr = self.rows // 2
-        return self.ref.at[c, pl.ds(pl.multiple_of((zz * NY + yy) * self.rows + h * hr, 16), hr)]
+        return self.view(c, pl.ds(pl.multiple_of((zz * NY + yy) * self.rows + h * hr, 16), hr))
 
     def up(self, c, zz):
         b = self.block(c, zz, self.y)
@@ -435,10 +440,10 @@
 
 
 class Scatter:
-    block, half = Gather.block, Gather.half
+    view, block, half = Gather.view, Gather.block, Gather.half
 
     def __init__(self, ref, bufs, rows, nz, sems):
-        self.ref, self.rows, self.nz = ref, rows, nz
+        self.ref, self.rows, self.nz, self.cols = ref, rows, nz, None
         self.xb, self.yb, self.zb, self.fb = bufs
         self.xs, self.ys, self.zs, self.fs, self.xr, self.yr, self.zr, self.fr = sems
         s = lax.axis_index("shard")
@@ -531,7 +536,7 @@
         return [D((nc, nz)), D((nc, nz)), D((nc, 2, nz)), D((nc,)), D((nc, nz)), D((nc, nz)), D((nc, 2, nz)), D((nc,))]
 
 
-def block_kernel(names, nz, NC, half, BQ, BK, *refs):
+def block_kernel(names, nz, NC, half, BQ, *refs):
     w = types.SimpleNamespace(**dict(zip(names, refs)))
     T, D = w.hb.shape
     n = nz * NY
@@ -542,13 +547,14 @@
     QO = NC
     npair = CA // 128
     nt = T // BQ
-    ns = nt * npair
     sub = half // BQ
     s, x, t = lax.axis_index("shard"), lax.axis_index("ctx"), lax.axis_index("tp")
     me = x * n + s
     g = Gather(w.G, rows, nz, [getattr(w, f"ga{i}") for i in range(6)])
+    gq = Gather(w.G, rows, nz, [getattr(w, f"gc{i}") for i in range(6)], QO, 256)
     gk = Gather(w.gkv, rows, nz, [getattr(w, f"gb{i}") for i in range(6)])
     r = Scatter(w.GR, (w.xb, w.yb, w.zb, w.fb), rows, nz, [getattr(w, f"sc{i}") for i in range(8)])
+    rq = Scatter(w.GQ, (w.xq, w.yq, w.zq, w.fq), rows, nz, [getattr(w, f"sq{i}") for i in range(8)])
     lane = lax.broadcasted_iota(jnp.int32, (BQ, 128), 1)
     low = lane < 64
 
@@ -556,7 +562,7 @@
         return pl.ds(pl.multiple_of(i * BQ, BQ), BQ)
 
     own = pl.ds(pl.multiple_of(s * rows, 16), rows)
-    loads = [(w.q, w.G.at[QO, own, pl.ds(0, CA)]), (w.o, w.G.at[QO, own, pl.ds(CA, CA)]), (w.kv, w.gkv.at[0, own]), (w.lnp, w.lb.at[s]), (w.hidden, w.hb), (w.cot, w.cb)]
+    loads = [(w.q, w.G.at[QO, own, pl.ds(0, CA)]), (w.o, w.G.at[QO, own, pl.ds(CA, CA)]), (w.kv, w.gkv.at[0, own]), (w.cot, w.cb), (w.hidden, w.hb)]
     for c in range(NC):
         loads.append((w.up.at[:, pl.ds(c * FC, FC)], w.G.at[c, own, pl.ds(0, FC)]))
         loads.append((w.dw.at[:, pl.ds(c * FC, FC)], w.G.at[c, own, pl.ds(FC, FC)]))
@@ -564,26 +570,41 @@
     for c in loads:
         c.start()
 
+    w.lb[s] = jnp.zeros((8, 128), F32)
+    for k, ref in enumerate((w.g1, w.b1, w.g2, w.b2)):
+        w.lb[s, k : k + 1, 0:rows] = ref[...].astype(F32)
+
     peers = [(s, 1 - x)] + [(lax.rem(s + k, n), xx) for k in range(1, n) for xx in (x, 1 - x)]
     bar = pltpu.get_barrier_semaphore()
     for ps, px in peers:
         pl.semaphore_signal(bar, inc=1, device_id={"shard": ps, "ctx": px}, device_id_type=MESH)
     pl.semaphore_signal(bar, inc=1, device_id={"tp": 1 - t}, device_id_type=MESH)
+    for c in loads[:3]:
+        c.wait()
     pl.semaphore_wait(bar, 2 * n)
 
-    for c in loads[:4]:
-        c.wait()
+    gk.own(0)
     lns = [rcopy(w.lb.at[s], w.lb.at[s], w.lns.at[k - 1], w.lnr.at[s], {"shard": lax.rem(s + k, n)}) for k in range(1, n)]
     for c in lns:
         c.start()
-    gk.own(0)
-    g.own(QO)
-    for c in loads[4:]:
+    for c in range(npair):
+        gq.own(c)
+    for c in loads[3:]:
         c.wait()
+
+    first = jnp.minimum(w.bo[2 * x], w.bo[2 * x + 1])
+    second = jnp.maximum(w.bo[2 * x], w.bo[2 * x + 1])
+    swap = w.bo[2 * x] > w.bo[2 * x + 1]
+
+    def pick(a, b):
+        return jnp.where(swap, b, a)
+
+    def flip(i):
+        return lax.rem(i + sub, 2 * sub)
 
     @pl.loop(0, nt)
     def _(i):
-        base = w.bo[2 * x + i // sub] * half + lax.rem(i, sub) * BQ
+        base = jnp.where(i < sub, first, second) * half + lax.rem(i, sub) * BQ
         pos = (base + lax.broadcasted_iota(jnp.int32, (BQ, 128), 0)).astype(F32)
         ang = pos * w.freq[0:1, :]
         l64 = lax.rem(lane, 64)
@@ -592,17 +613,22 @@
         w.ts[tile(i), :] = jnp.where(l64 < 8, -sn, jnp.where(l64 < 16, sn, 0.0))
         w.ct[:, tile(i)] = w.cb[tile(i), :].T
 
-    def rotated(v, i, sign):
+    def rotated(v, i, sign, layout=False):
         sw = jnp.where(lax.rem(lane, 16) < 8, pltpu.roll(v, 120, 1), pltpu.roll(v, 8, 1))
-        turn = sw * w.ts[tile(i), :]
-        return v * w.tc[tile(i), :] + (turn if sign > 0 else -turn)
+        cs, sn = w.tc[tile(i), :], w.ts[tile(i), :]
+        if layout:
+            cs, sn = pick(cs, w.tc[tile(flip(i)), :]), pick(sn, w.ts[tile(flip(i)), :])
+        turn = sw * sn
+        return v * cs + (turn if sign > 0 else -turn)
+
+    pieces = [(gk, 0)] + [(gq, c) for c in range(npair)]
 
     def head(d):
-        for e in (gk, g):
-            c = 0 if e is gk else QO
+        for e, c in pieces:
             if d < nz:
                 e.Z(c, d)
-            e.Y(c, d - 1)
+            if d <= nz:
+                e.Y(c, d - 1)
             if d > 1:
                 e.X(c, d - 2)
 
@@ -633,53 +659,49 @@
         w.nf[tile(i), :] = nf
         w.nat[:, tile(i)] = na.T
         w.nft[:, tile(i)] = nf.T
-
-    for d in range(2, nz + 2):
-        if d <= nz:
-            head(d)
-    for e, c in ((gk, 0), (g, QO)):
-        e.X(c, nz - 1)
-
-    def pump(c, d):
-        @pl.when(c < NC)
+        pl.when(i == 0)(lambda: head(2))
+        pl.when(i == 2)(lambda: head(3))
+
+    for d in range(4, nz + 2):
+        head(d)
+
+    def within(c, f):
+        @pl.when(both(c >= 0, c < NC))
         def _():
-            if d == 1:
-                pl.when(c + 1 < NC)(lambda: g.own(c + 1))
-            g.Z(c, d)
-            g.Y(c, d - 1)
-            if d == nz - 1:
-                g.X(c, 0)
-
-        @pl.when(both(c >= 1, c <= NC))
-        def _():
-            if d == 1:
-                g.Y(c - 1, nz - 1)
-            g.X(c - 1, d)
+            f(c)
+
+    def even(a):
+        within(a + 1, g.own)
+        within(a - 2, lambda c: g.X(c, 3))
+        within(a - 1, lambda c: (g.Z(c, 3), g.Y(c, 2), g.X(c, 1)))
+        within(a, lambda c: (g.Z(c, 1), g.Y(c, 0)))
+
+    def odd(a):
+        within(a - 1, lambda c: (g.Y(c, 3), g.X(c, 2)))
+        within(a, lambda c: (g.Z(c, 2), g.Y(c, 1), g.X(c, 0)))
 
     @pl.loop(0, nt)
     def _(i):
         kvp = dot(w.na[tile(i), :], w.gkv[0])
-        kvp = jnp.where(low, rotated(kvp, i, 1), kvp).astype(BF)
-        w.kvb[0, tile(i), :] = kvp
-        w.keys[tile(i), :] = kvp[:, :64]
-        w.values[tile(i), :] = pltpu.roll(kvp.astype(F32), 64, 1)[:, :64].astype(BF)
+        w.kvb[0, tile(i), :] = jnp.where(low, rotated(kvp, i, 1, True), kvp).astype(BF)
 
     kvx = rcopy(w.kvb.at[0], w.kvb.at[1], w.es.at[0], w.er.at[0], {"ctx": 1 - x})
     kvx.start()
-
-    order = [w.bo[2 * x], w.bo[2 * x + 1], w.bo[2 * (1 - x)], w.bo[2 * (1 - x) + 1]]
+    kvo = pltpu.make_async_copy(w.kvb.at[0], w.kvout, w.osem.at[0])
+    kvo.start()
+
     lane1 = lax.broadcasted_iota(jnp.int32, (1, 128), 1)
 
     @pl.loop(0, nt)
     def _(i):
-        qp = dot(w.na[tile(i), :], w.G[QO, :, 0:CA])
-        ga = dot(w.cb[tile(i), :], w.G[QO, :, CA : 2 * CA])
-        mine = w.bo[2 * x + i // sub]
+        qp = dot(pick(w.na[tile(i), :], w.na[tile(flip(i)), :]), w.G[QO, :, 0:CA])
+        ga = dot(pick(w.cb[tile(i), :], w.cb[tile(flip(i)), :]), w.G[QO, :, CA : 2 * CA])
+        mine = jnp.where(i < sub, first, second)
         hide = jnp.zeros((1, 128), F32)
-        for j in range(4):
-            hide = jnp.where(lane1 == 64 + j, jnp.where(order[j] <= mine, 0.0, NEG), hide)
+        for j in range(2):
+            hide = jnp.where(lane1 == 64 + j, jnp.where(w.bo[2 * (1 - x) + j] <= mine, 0.0, NEG), hide)
         for p in range(npair):
-            st = i * npair + p
+            st = p * nt + i
             qs = rotated(qp[:, 128 * p : 128 * p + 128], i, 1).astype(BF).astype(F32) * 0.125
             w.qx[st, 0:BQ, :] = jnp.where(low, qs, hide).astype(BF)
             w.qx[st, BQ : 2 * BQ, :] = jnp.where(low, pltpu.roll(qs, 64, 1), hide).astype(BF)
@@ -692,20 +714,41 @@
             gt = gp.astype(BF).T
             w.dt[st, :, 0:BQ] = gt[:64]
             w.dt[st, :, BQ : 2 * BQ] = gt[64:]
-        for d in range(1, nz):
-            pl.when(i == d - 1)(functools.partial(pump, 0, d))
-
+
+    even(0)
     kvx.wait_recv()
 
-    @pl.loop(0, 2 * nt)
-    def _(i):
-        kvf = w.kvb[i // nt, tile(lax.rem(i, nt)), :].astype(F32)
-        hot = jnp.where(lane == 64 + i // sub, 1.0, 0.0)
+    def keep_keys(i, kv, hot):
+        kvf = kv.astype(F32)
         w.kx[tile(i), :] = jnp.where(low, kvf, hot).astype(BF)
         w.k0[tile(i), :] = jnp.where(low, kvf, 0.0).astype(BF)
         w.v0[tile(i), :] = jnp.where(low, pltpu.roll(kvf, 64, 1), 0.0).astype(BF)
 
+    @pl.loop(0, nt)
+    def _(i):
+        keep_keys(i, pick(w.kvb[0, tile(i), :], w.kvb[0, tile(flip(i)), :]), 0.0)
+        keep_keys(nt + i, w.kvb[1, tile(i), :], jnp.where(lane == 64 + i // sub, 1.0, 0.0))
+
     w.acc[...] = jnp.zeros_like(w.acc)
+    dnx = rcopy(w.na, w.dnr, w.es.at[1], w.er.at[1], {"tp": 1 - t})
+
+    def own_out(c, v):
+        cols = pl.ds(pl.multiple_of(c * FC, FC), FC)
+        w.ou[:, cols] = v[:, :FC]
+        w.od[:, cols] = v[:, FC:]
+
+    def pair_out(p):
+        v = rq.G(p)
+        w.oq[:, p * 128 : p * 128 + 128] = v[:, :128]
+        w.oo[:, p * 128 : p * 128 + 128] = v[:, 128:]
+
+    def pair_grads(p):
+        cols = slice(p * 128, p * 128 + 128)
+        for ref, src, to in ((w.nat, w.gq, 0), (w.ct, w.attd, 128)):
+            a, b = src[0:half, cols], src[half:T, cols]
+            v = dot(ref[:, 0:half], pick(a, b)) + dot(ref[:, half:T], pick(b, a))
+            w.GQ[p, :, to : to + 128] = v.astype(BF)
+        rq.start(p)
 
     def feed_forward():
         @pl.loop(0, NC)
@@ -718,10 +761,16 @@
                 pdf = jnp.exp(-0.5 * hp * hp) * 0.3989422804014327
                 w.act[c, tile(i), :] = (hp * cdf).astype(BF)
                 w.dh[c, tile(i), :] = (da * (cdf + hp * pdf)).astype(BF)
-                pl.when(i == 1)(lambda: pump(c + 2, 1))
-                pl.when(i == 3)(lambda: pump(c + 2, 2))
-
-            pl.when(c >= 1)(lambda: r.X(c - 1))
+
+                @pl.when(i == 2)
+                def _():
+                    odd(c + 2)
+                    pl.when(c == 0)(lambda: rq.X(0))
+                    pl.when(c == 1)(lambda: rq.Y(0))
+                    pl.when(c == 2)(lambda: rq.Z(0, 1))
+                    pl.when(c == 3)(lambda: rq.Z(0, 2))
+                    pl.when(c >= 2)(lambda: r.X(c - 2))
+                    pl.when(c >= 3)(lambda: r.Y(c - 3))
 
             @pl.loop(0, D // BQ)
             def _(m):
@@ -729,8 +778,7 @@
                 w.GR[c, tile(m), FC : 2 * FC] = dot(w.ct[tile(m), :], w.act[c]).astype(BF)
 
             r.start(c)
-            pump(c + 2, 3)
-            pl.when(c >= 2)(lambda: r.Y(c - 2))
+            even(c + 3)
 
         @pl.loop(0, nt)
         def _(i):
@@ -743,78 +791,63 @@
             w.act[0, tile(i), :] = br[:, :FC].astype(BF)
             w.act[1, tile(i), :] = br[:, FC:].astype(BF)
 
+            @pl.when(i == 2)
+            def _():
+                rq.Z(0, 3)
+                rq.F(0)
+                r.X(2)
+                r.Y(1)
+
         dnx.start()
-        r.X(NC - 1)
-        r.Y(NC - 2)
-
-    dnx = rcopy(w.na, w.dnr, w.es.at[1], w.er.at[1], {"tp": 1 - t})
-
-    def own_out(c, v):
-        cols = pl.ds(pl.multiple_of(c * FC, FC), FC)
-        w.ou[:, cols] = v[:, :FC]
-        w.od[:, cols] = v[:, FC:]
-
-    def within(h, f):
-        pl.when(both(h >= 0, h < NC))(lambda: f(h))
-
-    def scatter_step(i):
-        pl.when(i == 0)(lambda: r.Y(NC - 1))
-        h = i // 2
-
-        @pl.when(lax.rem(i, 2) == 0)
-        def _():
-            within(h, lambda c: r.Z(c, 1))
-            within(h - 1, lambda c: r.Z(c, 3))
-            within(h - 2, lambda c: own_out(c, r.G(c)))
-
-        @pl.when(lax.rem(i, 2) == 1)
-        def _():
-            within(h, lambda c: r.Z(c, 2))
-            within(h - 1, lambda c: r.F(c))
-
-    first = nz - 1
-
-    def attention(st):
-        i = st // npair
-        p = lax.rem(st, npair)
-        own_b = i // sub
-        r0 = lax.rem(i, sub) * BQ
+
+    def scatter_step(p, k):
+        def last(c):
+            r.Z(c, 3)
+            r.F(c)
+
+        def out(c):
+            own_out(c, r.G(c))
+
+        if p == 1:
+            todo = {0: [(r.Z, 0, 1), (pair_out, 0)], 1: [(r.X, 3), (r.Y, 2), (r.Z, 0, 2)], 2: [(last, 0), (r.Z, 1, 1)], 3: [(r.Y, 3), (r.Z, 1, 2), (out, 0)]}
+        else:
+            todo = {0: [(last, 1), (r.Z, 2, 1)], 1: [(rq.X, 1), (r.Z, 2, 2), (out, 1)], 2: [(rq.Y, 1), (last, 2), (r.Z, 3, 1)], 3: [(rq.Z, 1, 1), (r.Z, 3, 2), (out, 2)]}
+        for f, *a in todo[k]:
+            f(*a)
+
+    def attention(p, k):
+        st = p * nt + k
         R = 2 * BQ
-        nk = w.kx.shape[0] // BK
-        per = half // BK
-        offs = []
-        for j in range(nk):
-            if j < per:
-                off = own_b * half + j * BK
-            elif j < 2 * per:
-                off = (1 - own_b) * half + (j - per) * BK
-            else:
-                off = j * BK
-            offs.append(pl.ds(pl.multiple_of(off, BK), BK))
-        cols = [slice(j * BK, (j + 1) * BK) for j in range(nk)]
+        b, rr = k // sub, k % sub
+        spans = [(0, half, False)] if b else []
+        spans += [(b * half + i * BQ, BQ, False) for i in range(rr)]
+        spans += [(b * half + rr * BQ, BQ, True), (2 * half, half, False), (3 * half, half, False)]
+        parts, at = [], 0
+        for off, size, tri in spans:
+            parts.append((slice(off, off + size), slice(at, at + size), tri))
+            at += size
         q, do = w.qx[st], w.dox[st]
         m = None
-        for j in range(nk):
-            sc = dot_nt(q, w.kx[offs[j], :])
-            if j < per:
-                row = lax.rem(lax.broadcasted_iota(jnp.int32, (R, BK), 0), BQ) + r0
-                col = lax.broadcasted_iota(jnp.int32, (R, BK), 1) + j * BK
-                sc = jnp.where(col <= row, sc, NEG)
-            w.ss[:, cols[j]] = sc
-            for k in range(BK // 128):
-                mk = sc[:, k * 128 : (k + 1) * 128]
-                m = mk if m is None else jnp.maximum(m, mk)
+        for ks, cs, tri in parts:
+            sc = dot_nt(q, w.kx[ks, :])
+            if tri:
+                row = lax.rem(lax.broadcasted_iota(jnp.int32, (R, BQ), 0), BQ)
+                sc = jnp.where(lax.broadcasted_iota(jnp.int32, (R, BQ), 1) <= row, sc, NEG)
+            w.ss[:, cs] = sc
+            for j in range(sc.shape[1] // 128):
+                mj = sc[:, j * 128 : (j + 1) * 128]
+                m = mj if m is None else jnp.maximum(m, mj)
         m = jnp.max(m, axis=1, keepdims=True)
         l = o = None
-        for j in range(nk):
-            e = jnp.exp(w.ss[:, cols[j]] - m)
-            w.ss[:, cols[j]] = e
-            for k in range(BK // 128):
-                lk = e[:, k * 128 : (k + 1) * 128]
-                l = lk if l is None else l + lk
+        for ks, cs, _ in parts:
+            e = jnp.exp(w.ss[:, cs] - m)
+            w.ss[:, cs] = e
+            for j in range(e.shape[1] // 128):
+                lj = e[:, j * 128 : (j + 1) * 128]
+                l = lj if l is None else l + lj
             eb = e.astype(BF)
-            w.ps[:, cols[j]] = eb
-            oj = dot(eb, w.v0[offs[j], :])
+            w.ps[:, cs] = eb
+            oj = dot(eb, w.v0[ks, :])
             o = oj if o is None else o + oj
         inv = 1.0 / jnp.sum(l, axis=1, keepdims=True)
         o = o * inv
@@ -823,62 +856,70 @@
         qs = (w.qt[st].astype(F32) * inv_row).astype(BF)
         dos = (w.dt[st].astype(F32) * inv_row).astype(BF)
         dq = None
-        for j in range(nk):
-            dp = dot_nt(do, w.v0[offs[j], :])
-            ds = (w.ss[:, cols[j]] * (dp - delta)).astype(BF)
-            dj = dot(ds, w.k0[offs[j], :])
+        for ks, cs, _ in parts:
+            dp = dot_nt(do, w.v0[ks, :])
+            ds = (w.ss[:, cs] * (dp - delta)).astype(BF)
+            dj = dot(ds, w.k0[ks, :])
             dq = dj if dq is None else dq + dj
-            w.acc[0:64, offs[j]] += dot(qs, ds)
-            w.acc[64:128, offs[j]] += dot(dos, w.ps[:, cols[j]])
+            w.acc[0:64, ks] += dot(qs, ds)
+            w.acc[64:128, ks] += dot(dos, w.ps[:, cs])
         dq = dq * (inv * 0.125)
         pair = pl.ds(pl.multiple_of(p * 128, 128), 128)
-        w.attd[tile(i), pair] = (o[:BQ] + pltpu.roll(o[BQ:], 64, 1)).astype(BF)
-        w.gq[tile(i), pair] = rotated(dq[:BQ] + pltpu.roll(dq[BQ:], 64, 1), i, -1).astype(BF)
-
-    @pl.loop(0, ns)
-    def _(st):
-        for d in range(1, nz):
-            pl.when(st == d - 1)(functools.partial(pump, 1, d))
-        pl.when(st == first)(feed_forward)
-        pl.when(st >= first)(lambda: scatter_step(st - first))
-        attention(st)
-
-    for i in range(2):
-        w.dS[i] = w.acc[:, i * T : (i + 1) * T].astype(BF)
+        at = slice(k * BQ, (k + 1) * BQ)
+        w.attd[at, pair] = (o[:BQ] + pltpu.roll(o[BQ:], 64, 1)).astype(BF)
+        w.gq[at, pair] = rotated(dq[:BQ] + pltpu.roll(dq[BQ:], 64, 1), k, -1).astype(BF)
+
+    @pl.loop(0, npair)
+    def _(p):
+        @pl.when(p == 1)
+        def _():
+            pair_grads(0)
+            feed_forward()
+
+        pl.when(p == 2)(lambda: pair_grads(1))
+        for k in range(nt):
+            pl.when(p == 0)(lambda: (odd, even)[k % 2]((k + 1) // 2))
+            for pp in range(1, npair):
+                pl.when(p == pp)(functools.partial(scatter_step, pp, k))
+            attention(p, k)
+
+    for b in (0, 1):
+        o = 1 - b
+        w.dS[0, :, b * half : (b + 1) * half] = pick(w.acc[:, b * half : (b + 1) * half], w.acc[:, o * half : (o + 1) * half]).astype(BF)
+    w.dS[1] = w.acc[:, T : 2 * T].astype(BF)
     dtp = rcopy(w.dS, w.dR, w.es.at[2], w.er.at[2], {"tp": 1 - t})
     dtp.start()
-    dnx.wait_recv()
-
-    @pl.loop(0, nt)
-    def _(i):
-        br = dot_nt(w.attd[tile(i), :], w.G[QO, :, CA : 2 * CA])
-        w.act[0, tile(i), :] = (w.act[0, tile(i), :].astype(F32) + br[:, :FC]).astype(BF)
-        w.act[1, tile(i), :] = (w.act[1, tile(i), :].astype(F32) + br[:, FC:]).astype(BF)
-
-    brx = rcopy(w.act.at[pl.ds(0, 2)], w.dh.at[pl.ds(0, 2)], w.es.at[3], w.er.at[3], {"tp": 1 - t})
-    brx.start()
-
-    @pl.loop(0, D // BQ)
-    def _(m):
-        w.GR[QO, tile(m), 0:CA] = dot(w.nat[tile(m), :], w.gq[...]).astype(BF)
-        w.GR[QO, tile(m), CA : 2 * CA] = dot(w.ct[tile(m), :], w.attd[...]).astype(BF)
-
-    r.start(QO)
+    pair_grads(2)
     dtp.wait_recv()
     w.dX[...] = (w.dS[1].astype(F32) + w.dR[1].astype(F32)).astype(BF)
     dxx = rcopy(w.dX, w.dXR, w.es.at[4], w.er.at[4], {"ctx": 1 - x})
     dxx.start()
+    r.Z(3, 3)
+    r.F(3)
+    rq.Z(1, 2)
+    dnx.wait_recv()
 
     @pl.loop(0, nt)
     def _(i):
-        ga = dot_nt(w.gq[tile(i), :], w.G[QO, :, 0:CA])
+        br = dot_nt(pick(w.attd[tile(i), :], w.attd[tile(flip(i)), :]), w.G[QO, :, CA : 2 * CA])
+        w.act[0, tile(i), :] = (w.act[0, tile(i), :].astype(F32) + br[:, :FC]).astype(BF)
+        w.act[1, tile(i), :] = (w.act[1, tile(i), :].astype(F32) + br[:, FC:]).astype(BF)
+
+    brx = rcopy(w.act.at[pl.ds(0, 2)], w.dh.at[pl.ds(0, 2)], w.es.at[3], w.er.at[3], {"tp": 1 - t})
+    brx.start()
+    rq.X(2)
+
+    @pl.loop(0, nt)
+    def _(i):
+        ga = dot_nt(pick(w.gq[tile(i), :], w.gq[tile(flip(i)), :]), w.G[QO, :, 0:CA])
         w.act[2, tile(i), :] = ga[:, :FC].astype(BF)
         w.act[3, tile(i), :] = ga[:, FC:].astype(BF)
 
     gax = rcopy(w.act.at[pl.ds(2, 2)], w.dh.at[pl.ds(2, 2)], w.es.at[5], w.er.at[5], {"tp": 1 - t})
     gax.start()
-    r.F(NC - 1)
-    r.X(QO)
+    rq.Z(1, 3)
+    rq.F(1)
+    rq.Y(2)
     brx.wait_recv()
 
     @pl.loop(0, nt)
@@ -888,16 +929,15 @@
             v = w.act[k, tile(i), :].astype(F32) + w.dh[k, tile(i), :].astype(F32)
             w.nf[tile(i), cs] = (w.hb[tile(i), cs].astype(F32) + v).astype(BF)
 
-    outx = pltpu.make_async_copy(w.nf, w.out_tokens, w.osem.at[0])
+    outx = pltpu.make_async_copy(w.nf, w.out_tokens, w.osem.at[1])
     outx.start()
-    r.Y(QO)
     dxx.wait_recv()
 
     @pl.loop(0, nt)
     def _(i):
         v = w.dS[0, :, tile(i)].astype(F32) + w.dR[0, :, tile(i)].astype(F32) + w.dXR[:, tile(i)].astype(F32)
         v = v.T
-        w.gkb[tile(i), :] = jnp.where(low, rotated(v, i, -1), v).astype(BF)
+        w.gkb[tile(i), :] = jnp.where(low, rotated(v, i, -1, True), v).astype(BF)
 
     w.kvS[...] = dot(w.nat[...], w.gkb[...]).astype(BF)
 
@@ -907,9 +947,12 @@
     kvs = [rcopy(w.kvS.at[kv_rows(ps)], w.kvR.at[me], w.ks.at[i], w.kr.at[me], {"shard": ps, "ctx": px}) for i, (ps, px) in enumerate(peers)]
     for c in kvs:
         c.start()
-    r.Z(QO, 1)
+    rq.Z(2, 1)
     gax.wait_recv()
     w.lg[...] = jnp.zeros_like(w.lg)
+
+    def hgx(i):
+        return pltpu.make_async_copy(w.hgs.at[tile(i)], w.hg.at[tile(i)], w.osem.at[2 + i])
 
     @pl.loop(0, nt)
     def _(i):
@@ -919,12 +962,13 @@
         gf = w.na[tile(i), :].astype(F32) + w.dnr[tile(i), :].astype(F32)
         e = gn * w.prm[0:1, :] + gf * w.prm[2:3, :]
         e = rstd * (e - jnp.mean(e, axis=1, keepdims=True) - xh * jnp.mean(e * xh, axis=1, keepdims=True))
-        w.hg[tile(i), :] = w.cb[tile(i), :].astype(F32) + e
+        w.hgs[tile(i), :] = w.cb[tile(i), :].astype(F32) + e
+        hgx(i).start()
         w.lg[0:1, :] += jnp.sum(gn * xh, axis=0, keepdims=True)
         w.lg[1:2, :] += jnp.sum(gn, axis=0, keepdims=True)
         w.lg[2:3, :] += jnp.sum(gf * xh, axis=0, keepdims=True)
         w.lg[3:4, :] += jnp.sum(gf, axis=0, keepdims=True)
-        pl.when(i == 1)(lambda: r.Z(QO, 2))
+        pl.when(i == 2)(lambda: rq.Z(2, 2))
 
     lg = w.lg[...]
     keep = lax.broadcasted_iota(jnp.int32, (8, 128), 1) < rows
@@ -934,9 +978,10 @@
     lgs = [rcopy(w.lS.at[ps], w.lR.at[me], w.ls.at[i], w.lr.at[me], {"shard": ps, "ctx": px}) for i, (ps, px) in enumerate(peers)]
     for c in lgs:
         c.start()
-    own_out(NC - 1, r.G(NC - 1))
-    r.Z(QO, 3)
-    r.F(QO)
+    rq.Z(2, 3)
+    rq.F(2)
+    own_out(3, r.G(3))
+    pair_out(1)
 
     def arrived(ref, sems, i, ps, px):
         k = px * n + ps
@@ -961,19 +1006,23 @@
     rcopy(w.kvF.at[1 - t], w.kvF.at[1 - t], w.es.at[6], w.er.at[6], {"tp": 1 - t}).wait_recv()
     w.okv[0:hr, :] = w.kvF[0]
     w.okv[hr:rows, :] = w.kvF[1]
-    v = r.G(QO)
-    w.oq[...] = v[:, :CA]
-    w.oo[...] = v[:, CA:]
+    pair_out(2)
+    kvo.wait()
     outx.wait()
+    for i in range(nt):
+        hgx(i).wait()
     for c in lns + [kvx, dnx, dtp, brx, dxx, gax, kfx] + kvs + lgs:
         c.wait_send()
     gk.finish(0)
-    for c in range(NC + 1):
+    for c in range(npair):
+        gq.finish(c)
+        rq.finish(c)
+    for c in range(NC):
         g.finish(c)
         r.finish(c)
 
 
-def block_call(bo, freq, hidden, cot, lnp, up, dw, q, o, kv, nz, half, cid):
+def block_call(bo, freq, hidden, cot, lns, up, dw, q, o, kv, nz, half, cid):
     T, D = hidden.shape
     rows, CU = up.shape
     CA, CK = q.shape[1], kv.shape[1]
@@ -981,16 +1030,17 @@
     NC = CU // FC
     n = nz * NY
     hr = rows // 2
-    BQ, BK = 256, 512
-    ns = T // BQ * (CA // 128)
+    BQ = 256
+    npair = CA // 128
+    ns = T // BQ * npair
     A = pl.BlockSpec(memory_space=pl.ANY)
     V = pl.BlockSpec(memory_space=pltpu.VMEM)
     S = pl.BlockSpec(memory_space=pltpu.SMEM)
     Dm = pltpu.SemaphoreType.DMA
-    ins = ["bo", "freq", "hidden", "cot", "lnp", "up", "dw", "q", "o", "kv"]
+    ins = ["bo", "freq", "g1", "b1", "g2", "b2", "hidden", "cot", "up", "dw", "q", "o", "kv"]
     sd = jax.ShapeDtypeStruct
     outs = {
-        "out_tokens": (sd((T, D), BF), A), "keys": (sd((T, 64), BF), V), "values": (sd((T, 64), BF), V), "hg": (sd((T, D), F32), V),
+        "out_tokens": (sd((T, D), BF), A), "kvout": (sd((T, CK), BF), A), "hg": (sd((T, D), F32), A),
         "lno": (sd((8, 128), F32), V), "oq": (sd((rows, CA), F32), V), "okv": (sd((rows, CK), F32), V), "oo": (sd((rows, CA), F32), V),
         "ou": (sd((rows, CU), F32), V), "od": (sd((rows, CU), F32), V),
     }
@@ -998,31 +1048,77 @@
     f = lambda *sh: pltpu.VMEM(sh, F32)
     scr = {
         "hb": b(T, D), "cb": b(T, D), "ct": b(D, T), "na": b(T, D), "nf": b(T, D), "nft": b(D, T), "nat": b(D, T),
-        "G": b(NC + 1, D, 2 * FC), "gkv": b(1, D, CK), "GR": b(NC + 1, D, 2 * FC),
-        "xb": b(NC + 1, nz, hr, 2 * FC), "yb": b(NC + 1, nz, hr, 2 * FC), "zb": b(NC + 1, nz + 1, rows, 2 * FC), "fb": b(NC + 1, 2, rows, 2 * FC),
+        "G": b(NC + 1, D, 2 * FC), "gkv": b(1, D, CK), "GR": b(NC, D, 2 * FC), "GQ": b(npair, D, 256),
+        "xb": b(NC, nz, hr, 2 * FC), "yb": b(NC, nz, hr, 2 * FC), "zb": b(NC, nz + 1, rows, 2 * FC), "fb": b(NC, 2, rows, 2 * FC),
+        "xq": b(npair, nz, hr, 256), "yq": b(npair, nz, hr, 256), "zq": b(npair, nz + 1, rows, 256), "fq": b(npair, 2, rows, 256),
         "lb": f(n, 8, 128), "act": b(NC, T, FC), "dh": b(NC, T, FC), "dnr": b(T, D),
         "qx": b(ns, 2 * BQ, 128), "dox": b(ns, 2 * BQ, 128), "qt": b(ns, 64, 2 * BQ), "dt": b(ns, 64, 2 * BQ),
         "kvb": b(2, T, CK), "kx": b(2 * T, 128), "k0": b(2 * T, 128), "v0": b(2 * T, 128),
         "ss": f(2 * BQ, 2 * T), "ps": b(2 * BQ, 2 * T), "attd": b(T, CA), "gq": b(T, CA), "acc": f(128, 2 * T),
         "tc": f(T, 128), "ts": f(T, 128), "dS": b(2, 128, T), "dR": b(2, 128, T), "dX": b(128, T), "dXR": b(128, T), "gkb": b(T, 128),
-        "kvS": b(D, CK), "kvR": b(2 * n, hr, CK), "kvF": f(2, hr, CK), "lS": f(n, 8, 128), "lR": f(2 * n, 8, 128), "prm": f(8, D), "lg": f(8, D),
-        "lsem": Dm((6 + 2 * NC,)), "lns": Dm((n - 1,)), "lnr": Dm((n,)), "es": Dm((7,)), "er": Dm((7,)), "osem": Dm((1,)),
+        "kvS": b(D, CK), "kvR": b(2 * n, hr, CK), "kvF": f(2, hr, CK), "lS": f(n, 8, 128), "lR": f(2 * n, 8, 128), "prm": f(8, D), "lg": f(8, D), "hgs": f(T, D),
+        "lsem": Dm((5 + 2 * NC,)), "lns": Dm((n - 1,)), "lnr": Dm((n,)), "es": Dm((7,)), "er": Dm((7,)), "osem": Dm((2 + T // BQ,)),
         "ks": Dm((2 * n - 1,)), "kr": Dm((2 * n,)), "ls": Dm((2 * n - 1,)), "lr": Dm((2 * n,)),
     }
-    scr.update({f"ga{i}": v for i, v in enumerate(Gather.sems(NC + 1, nz))})
+    scr.update({f"ga{i}": v for i, v in enumerate(Gather.sems(NC, nz))})
     scr.update({f"gb{i}": v for i, v in enumerate(Gather.sems(1, nz))})
-    scr.update({f"sc{i}": v for i, v in enumerate(Scatter.sems(NC + 1, nz))})
+    scr.update({f"gc{i}": v for i, v in enumerate(Gather.sems(npair, nz))})
+    scr.update({f"sc{i}": v for i, v in enumerate(Scatter.sems(NC, nz))})
+    scr.update({f"sq{i}": v for i, v in enumerate(Scatter.sems(npair, nz))})
     names = ins + list(outs) + list(scr)
     res = pl.pallas_call(
-        functools.partial(block_kernel, names, nz, NC, half, BQ, BK),
+        functools.partial(block_kernel, names, nz, NC, half, BQ),
         out_shape=tuple(v[0] for v in outs.values()),
-        in_specs=[S, V] + [A] * 8,
+        in_specs=[S, V, V, V, V, V] + [A] * 7,
         out_specs=tuple(v[1] for v in outs.values()),
         scratch_shapes=list(scr.values()),
         compiler_params=pltpu.CompilerParams(collective_id=cid, has_side_effects=True, vmem_limit_bytes=67043328),
         name="block",
-    )(bo, freq, hidden, cot, lnp, up, dw, q, o, kv)
+    )(bo, freq, *lns, hidden, cot, up, dw, q, o, kv)
     return dict(zip(outs, res))
+
+
+def results_kernel(nt, tok, hg, kv, lno, oq, okv, oo, ou, od, tok_o, k_o, v_o, hg_o, a_o, b_o, c_o, d_o, oq_o, okv_o, oo_o, ou_o, od_o, tb, hb, sin, sout):
+    BQ = tok.shape[0] // nt
+    moves = []
+    for i in range(nt):
+        t = pl.ds(i * BQ, BQ)
+        moves.append((hg.at[t], hb.at[t], hg_o.at[t]))
+        moves.append((tok.at[t], tb.at[t], tok_o.at[t]))
+    ins = [pltpu.make_async_copy(a, b, sin.at[i]) for i, (a, b, _) in enumerate(moves)]
+    outs = [pltpu.make_async_copy(b, c, sout.at[i]) for i, (_, b, c) in enumerate(moves)]
+    for c in ins:
+        c.start()
+    for a, b in zip(ins, outs):
+        a.wait()
+        b.start()
+    k_o[...] = kv[:, :64]
+    v_o[...] = pltpu.roll(kv[...].astype(F32), 64, 1)[:, :64].astype(BF)
+    for k, ref in enumerate((a_o, b_o, c_o, d_o)):
+        ref[...] = lno[k, : ref.shape[0]]
+    for a, b in ((oq, oq_o), (okv, okv_o), (oo, oo_o), (ou, ou_o), (od, od_o)):
+        b[...] = a[...]
+    for c in outs:
+        c.wait()
+
+
+def results(v, rows):
+    T, D = v["hg"].shape
+    A = pl.BlockSpec(memory_space=pl.ANY)
+    V = pl.BlockSpec(memory_space=pltpu.VMEM)
+    sd = jax.ShapeDtypeStruct
+    like = lambda k: sd(v[k].shape, v[k].dtype)
+    nt = 4
+    Dm = pltpu.SemaphoreType.DMA
+    order = ("out_tokens", "hg", "kvout", "lno", "oq", "okv", "oo", "ou", "od")
+    return pl.pallas_call(
+        functools.partial(results_kernel, nt),
+        out_shape=(like("out_tokens"), sd((T, 64), BF), sd((T, 64), BF), like("hg")) + (sd((rows,), F32),) * 4 + tuple(like(k) for k in order[4:]),
+        in_specs=[A, A] + [V] * 7,
+        out_specs=(A, V, V, A) + (V,) * 9,
+        scratch_shapes=[pltpu.VMEM((T, D), BF), pltpu.VMEM((T, D), F32), Dm((2 * nt,)), Dm((2 * nt,))],
+        name="results",
+    )(*[v[k] for k in order])
 
 
 def fits(mesh):
@@ -1031,14 +1127,13 @@
 
 def fast_device(hidden, block_order, ln1_gain, ln1_bias, ln2_gain, ln2_bias, q_weight, kv_weight, o_weight, up_weight, down_weight, cotangent):
     seqs, span, width = hidden.shape
-    hd = kv_weight.shape[1] // 2
     rows = ln1_gain.shape[0]
-    lnp = jnp.pad(jnp.stack([ln1_gain, ln1_bias, ln2_gain, ln2_bias]).astype(F32), ((0, 4), (0, 128 - rows)))
     freq = 10000.0 ** (-2.0 * (np.arange(128) % (ROT // 2)) / ROT)
     freq = jnp.asarray(np.broadcast_to(freq, (8, 128)), F32)
-    v = block_call(block_order, freq, hidden.reshape(span, width), cotangent.reshape(span, width), lnp, up_weight, down_weight, q_weight, o_weight, kv_weight, width // rows // NY, span // 2, 1)
-    lo = v["lno"]
-    return (v["out_tokens"][None], v["keys"][None], v["values"][None], v["hg"][None], lo[0, :rows], lo[1, :rows], lo[2, :rows], lo[3, :rows], v["oq"], v["okv"], v["oo"], v["ou"], v["od"])
+    lns = [a.reshape(1, rows) for a in (ln1_gain, ln1_bias, ln2_gain, ln2_bias)]
+    v = block_call(block_order, freq, hidden.reshape(span, width), cotangent.reshape(span, width), lns, up_weight, down_weight, q_weight, o_weight, kv_weight, width // rows // NY, span // 2, 1)
+    tok, keys, values, hg, a, b, c, d, oq, okv, oo, ou, od = results(v, rows)
+    return (tok[None], keys[None], values[None], hg[None], a, b, c, d, oq, okv, oo, ou, od)
 
 
 def solution(mesh):

time: 211 us -> 184 us (0.87)
  Pallas kernels: 196 us -> 180 us
  local copies, waits for them, and re-layouts: 12.9 us -> 3.45 us
    pallas_call x1 -> x2, Pallas kernels: 196 us -> 180 us  [the longest x1 173 us: block_call(): pl.pallas_call(functools.partial(block_kernel, names, nz, NC, half, BQ),...]
    unnamed x21 -> x2, local copies, waits for them, and re-layouts: 11.5 us -> 3.45 us
where the time goes in v3:
time: 184 us
  Pallas kernels  180 us (98%)
  local copies, waits for them, and re-layouts  3.45 us (2%)
    pallas_call x1, Pallas kernels, block_call(): pl.pallas_call(functools.partial(block_kernel, names, nz, NC, half, BQ),...  173 us
    pallas_call x1, Pallas kernels, results(): pl.pallas_call(functools.partial(results_kernel, nt), out_shape=(like('ou...  6.63 us

profile of v3, /device:TPU:0, one launch (start us, length us, event | category | flops | bytes accessed | tf_op | source)
XLA Modules:
  0.0 184.1 jit_solution(18445662401061884244)
XLA Ops:
  0.6 173.4 %block.1 = (bf16[1024,768]{1,0:T(8,128)(2,1)}, bf16[1024,128]{1,0:T(8,128)(2,1)}, f32[1024,768]{1,0:T(8,128)}, f32[8,128]{1,0:T(8,128)}, f32[96,384]{1,0:T(8,128...) custom-call(s32[4]{0:T(128)} %refs_0_.1, ...), custom_call_target="tpu_custom_call" | custom-call | tf_op jit(solution)/shard_map/block/pallas_call | solution.py:1069
  174.0 6.6 %results.1 = (bf16[1024,768]{1,0:T(8,128)(2,1)}, bf16[1024,64]{1,0:T(8,128)(2,1)}, bf16[1024,64]{1,0:T(8,128)(2,1)}, f32[1024,768]{1,0:T(8,128)}, f32[96]{0:T(12...) custom-call(bf16[1024,768]{1,0:T(8,128)(2,1)} %get-tuple-element.35., ...), custom_call_target="tpu_custom_call" | custom-call | tf_op jit(solution)/shard_map/results/pallas_call | solution.py:1114
  180.7 1.7 copy.26
  182.4 1.7 copy.27

commit v4 on v3

--- a/solution.py
+++ b/solution.py
@@ -366,7 +366,7 @@
         return rcopy(b, b, self.zs.at[c, 1, zz], self.zr.at[c, zz], {"shard": (self.z - 1) * NY + self.y})
 
     def ycp(self, c, zz, yy, h):
-        b = self.half(c, zz, yy, h)
+        b = self.half(c, zz, yy, h) if self.cols is None else self.block(c, zz, yy)
         return rcopy(b, b, self.ys.at[c, zz], self.yr.at[c, zz], {"shard": self.z * NY + 1 - self.y})
 
     def xcp(self, c, zz, h):
@@ -412,12 +412,21 @@
     def Y(self, c, d):
         def f(zz):
             self.ycp(c, zz, 1 - self.y, self.x).wait_recv()
-            self.xcp(c, zz, self.x).start()
+            if self.cols is None:
+                self.xcp(c, zz, self.x).start()
 
         self.each(d, f)
 
     def X(self, c, d):
         self.each(d, lambda zz: self.xcp(c, zz, 1 - self.x).wait_recv())
+
+    def stage(self, c, d):
+        if d < self.nz:
+            self.Z(c, d)
+        if d <= self.nz:
+            self.Y(c, d - 1)
+        if d > 1 and self.cols is None:
+            self.X(c, d - 2)
 
     def finish(self, c):
         z, nz = self.z, self.nz
@@ -431,7 +440,8 @@
                     pl.when(both(ok, z > 0))(lambda: self.dn(c, zz).wait_send())
         for zz in range(nz):
             self.ycp(c, zz, self.y, self.x).wait_send()
-            self.xcp(c, zz, self.x).wait_send()
+            if self.cols is None:
+                self.xcp(c, zz, self.x).wait_send()
 
     @staticmethod
     def sems(nc, nz):
@@ -463,26 +473,30 @@
     def fcp(self, c):
         return rcopy(self.fb.at[c, 0], self.fb.at[c, 1], self.fs.at[c], self.fr.at[c], {"ctx": 1 - self.x})
 
+    def far(self, j):
+        return jnp.where(self.z < self.nz // 2, self.nz - 1 - j, j)
+
     def start(self, c):
-        for zz in range(self.nz):
-            self.xcp(c, zz).start()
-
-    def X(self, c):
-        for zz in range(self.nz):
+        for j in range(self.nz):
+            self.xcp(c, self.far(j)).start()
+
+    def X(self, c, j0=0, count=None):
+        for j in range(j0, j0 + (count or self.nz)):
+            zz = self.far(j)
             self.xcp(c, zz).wait_recv()
             h = self.half(c, zz, 1 - self.y, self.x)
             h[...] = (h[...].astype(F32) + self.xb[c, zz].astype(F32)).astype(BF)
             self.ycp(c, zz).start()
 
-    def Y(self, c):
+    def Y(self, c, j0=0, count=None):
         z, nz = self.z, self.nz
-        for zz in range(nz):
+        for j in range(j0, j0 + (count or nz)):
+            zz = self.far(j)
             self.ycp(c, zz).wait_recv()
             h = self.half(c, zz, self.y, self.x)
             h[...] = (h[...].astype(F32) + self.yb[c, zz].astype(F32)).astype(BF)
-            if zz > 0:
+            if j < nz - 1:
                 pl.when(z == 0)(lambda: self.zcp(c, 0, zz, self.block(c, zz, self.y)).start())
-            if zz < nz - 1:
                 pl.when(z == nz - 1)(lambda: self.zcp(c, 1, zz, self.block(c, zz, self.y)).start())
 
     def Z(self, c, k):
@@ -552,7 +566,6 @@
     me = x * n + s
     g = Gather(w.G, rows, nz, [getattr(w, f"ga{i}") for i in range(6)])
     gq = Gather(w.G, rows, nz, [getattr(w, f"gc{i}") for i in range(6)], QO, 256)
-    gk = Gather(w.gkv, rows, nz, [getattr(w, f"gb{i}") for i in range(6)])
     r = Scatter(w.GR, (w.xb, w.yb, w.zb, w.fb), rows, nz, [getattr(w, f"sc{i}") for i in range(8)])
     rq = Scatter(w.GQ, (w.xq, w.yq, w.zq, w.fq), rows, nz, [getattr(w, f"sq{i}") for i in range(8)])
     lane = lax.broadcasted_iota(jnp.int32, (BQ, 128), 1)
@@ -562,7 +575,12 @@
         return pl.ds(pl.multiple_of(i * BQ, BQ), BQ)
 
     own = pl.ds(pl.multiple_of(s * rows, 16), rows)
-    loads = [(w.q, w.G.at[QO, own, pl.ds(0, CA)]), (w.o, w.G.at[QO, own, pl.ds(CA, CA)]), (w.kv, w.gkv.at[0, own]), (w.cot, w.cb), (w.hidden, w.hb)]
+    loads = [(w.kv, w.gkv.at[own])]
+    for p in range(npair):
+        loads.append((w.q.at[:, pl.ds(128 * p, 128)], w.G.at[QO, own, pl.ds(256 * p, 128)]))
+        loads.append((w.o.at[:, pl.ds(128 * p, 128)], w.G.at[QO, own, pl.ds(256 * p + 128, 128)]))
+    loads += [(w.cot, w.cb), (w.hidden, w.hb)]
+    nl = 1 + 2 * npair
     for c in range(NC):
         loads.append((w.up.at[:, pl.ds(c * FC, FC)], w.G.at[c, own, pl.ds(0, FC)]))
         loads.append((w.dw.at[:, pl.ds(c * FC, FC)], w.G.at[c, own, pl.ds(FC, FC)]))
@@ -579,17 +597,19 @@
     for ps, px in peers:
         pl.semaphore_signal(bar, inc=1, device_id={"shard": ps, "ctx": px}, device_id_type=MESH)
     pl.semaphore_signal(bar, inc=1, device_id={"tp": 1 - t}, device_id_type=MESH)
-    for c in loads[:3]:
+    for c in loads[:nl]:
         c.wait()
     pl.semaphore_wait(bar, 2 * n)
 
-    gk.own(0)
+    kds = [rcopy(w.gkv.at[own], w.gkv.at[own], w.gb0.at[k - 1], w.gb1.at[s], {"shard": lax.rem(s + k, n)}) for k in range(1, n)]
+    for c in kds:
+        c.start()
     lns = [rcopy(w.lb.at[s], w.lb.at[s], w.lns.at[k - 1], w.lnr.at[s], {"shard": lax.rem(s + k, n)}) for k in range(1, n)]
     for c in lns:
         c.start()
     for c in range(npair):
         gq.own(c)
-    for c in loads[3:]:
+    for c in loads[nl:]:
         c.wait()
 
     first = jnp.minimum(w.bo[2 * x], w.bo[2 * x + 1])
@@ -621,19 +641,6 @@
         turn = sw * sn
         return v * cs + (turn if sign > 0 else -turn)
 
-    pieces = [(gk, 0)] + [(gq, c) for c in range(npair)]
-
-    def head(d):
-        for e, c in pieces:
-            if d < nz:
-                e.Z(c, d)
-            if d <= nz:
-                e.Y(c, d - 1)
-            if d > 1:
-                e.X(c, d - 2)
-
-    head(1)
-    g.own(0)
     for k in range(1, n):
         f = lax.rem(s + n - k, n)
         rcopy(w.lb.at[f], w.lb.at[f], w.lns.at[0], w.lnr.at[f], {"shard": f}).wait_recv()
@@ -654,35 +661,27 @@
     def _(i):
         xh, _ = standardized(i)
         na = (xh * w.prm[0:1, :] + w.prm[1:2, :]).astype(BF)
-        nf = (xh * w.prm[2:3, :] + w.prm[3:4, :]).astype(BF)
         w.na[tile(i), :] = na
-        w.nf[tile(i), :] = nf
-        w.nat[:, tile(i)] = na.T
-        w.nft[:, tile(i)] = nf.T
-        pl.when(i == 0)(lambda: head(2))
-        pl.when(i == 2)(lambda: head(3))
-
-    for d in range(4, nz + 2):
-        head(d)
-
-    def within(c, f):
-        @pl.when(both(c >= 0, c < NC))
-        def _():
-            f(c)
-
-    def even(a):
-        within(a + 1, g.own)
-        within(a - 2, lambda c: g.X(c, 3))
-        within(a - 1, lambda c: (g.Z(c, 3), g.Y(c, 2), g.X(c, 1)))
-        within(a, lambda c: (g.Z(c, 1), g.Y(c, 0)))
-
-    def odd(a):
-        within(a - 1, lambda c: (g.Y(c, 3), g.X(c, 2)))
-        within(a, lambda c: (g.Z(c, 2), g.Y(c, 1), g.X(c, 0)))
+
+    plan = {
+        ("h", 0): [(gq.stage, 0, 1), (g.own, 1)],
+        ("h", 1): [(gq.stage, 0, 2), (g.own, 0)],
+        ("h", 2): [(gq.stage, 0, 3), (gq.stage, 0, 4), (gq.stage, 1, 1), (g.stage, 0, 1)],
+    }
+
+    def at(*slot):
+        for f, *a in plan.get(slot, []):
+            f(*a)
+
+    at("h", 0)
+    for k in range(1, n):
+        f = lax.rem(s + n - k, n)
+        b = w.gkv.at[pl.ds(pl.multiple_of(f * rows, 16), rows)]
+        rcopy(b, b, w.gb0.at[0], w.gb1.at[f], {"shard": f}).wait_recv()
 
     @pl.loop(0, nt)
     def _(i):
-        kvp = dot(w.na[tile(i), :], w.gkv[0])
+        kvp = dot(w.na[tile(i), :], w.gkv[...])
         w.kvb[0, tile(i), :] = jnp.where(low, rotated(kvp, i, 1, True), kvp).astype(BF)
 
     kvx = rcopy(w.kvb.at[0], w.kvb.at[1], w.es.at[0], w.er.at[0], {"ctx": 1 - x})
@@ -692,31 +691,36 @@
 
     lane1 = lax.broadcasted_iota(jnp.int32, (1, 128), 1)
 
+    at("h", 1)
+
     @pl.loop(0, nt)
     def _(i):
-        qp = dot(pick(w.na[tile(i), :], w.na[tile(flip(i)), :]), w.G[QO, :, 0:CA])
-        ga = dot(pick(w.cb[tile(i), :], w.cb[tile(flip(i)), :]), w.G[QO, :, CA : 2 * CA])
-        mine = jnp.where(i < sub, first, second)
-        hide = jnp.zeros((1, 128), F32)
-        for j in range(2):
-            hide = jnp.where(lane1 == 64 + j, jnp.where(w.bo[2 * (1 - x) + j] <= mine, 0.0, NEG), hide)
-        for p in range(npair):
-            st = p * nt + i
-            qs = rotated(qp[:, 128 * p : 128 * p + 128], i, 1).astype(BF).astype(F32) * 0.125
-            w.qx[st, 0:BQ, :] = jnp.where(low, qs, hide).astype(BF)
-            w.qx[st, BQ : 2 * BQ, :] = jnp.where(low, pltpu.roll(qs, 64, 1), hide).astype(BF)
+        xh, _ = standardized(i)
+        nf = (xh * w.prm[2:3, :] + w.prm[3:4, :]).astype(BF)
+        w.nf[tile(i), :] = nf
+        w.nft[:, tile(i)] = nf.T
+        w.nat[:, tile(i)] = w.na[tile(i), :].T
+
+    def project(p):
+        @pl.loop(0, nt)
+        def _(i):
+            qp = dot(pick(w.na[tile(i), :], w.na[tile(flip(i)), :]), w.G[QO, :, pl.ds(pl.multiple_of(p * 256, 128), 128)])
+            gp = dot(pick(w.cb[tile(i), :], w.cb[tile(flip(i)), :]), w.G[QO, :, pl.ds(pl.multiple_of(p * 256 + 128, 128), 128)])
+            mine = jnp.where(i < sub, first, second)
+            hide = jnp.zeros((1, 128), F32)
+            for j in range(2):
+                hide = jnp.where(lane1 == 64 + j, jnp.where(w.bo[2 * (1 - x) + j] <= mine, 0.0, NEG), hide)
+            qs = rotated(qp, i, 1).astype(BF).astype(F32) * 0.125
+            w.qx[i, 0:BQ, :] = jnp.where(low, qs, hide).astype(BF)
+            w.qx[i, BQ : 2 * BQ, :] = jnp.where(low, pltpu.roll(qs, 64, 1), hide).astype(BF)
             qt = qs.astype(BF).T
-            w.qt[st, :, 0:BQ] = qt[:64]
-            w.qt[st, :, BQ : 2 * BQ] = qt[64:]
-            gp = ga[:, 128 * p : 128 * p + 128]
-            w.dox[st, 0:BQ, :] = jnp.where(low, gp, 0.0).astype(BF)
-            w.dox[st, BQ : 2 * BQ, :] = jnp.where(low, pltpu.roll(gp, 64, 1), 0.0).astype(BF)
+            w.qt[i, :, 0:BQ] = qt[:64]
+            w.qt[i, :, BQ : 2 * BQ] = qt[64:]
+            w.dox[i, 0:BQ, :] = jnp.where(low, gp, 0.0).astype(BF)
+            w.dox[i, BQ : 2 * BQ, :] = jnp.where(low, pltpu.roll(gp, 64, 1), 0.0).astype(BF)
             gt = gp.astype(BF).T
-            w.dt[st, :, 0:BQ] = gt[:64]
-            w.dt[st, :, BQ : 2 * BQ] = gt[64:]
-
-    even(0)
-    kvx.wait_recv()
+            w.dt[i, :, 0:BQ] = gt[:64]
+            w.dt[i, :, BQ : 2 * BQ] = gt[64:]
 
     def keep_keys(i, kv, hot):
         kvf = kv.astype(F32)
@@ -727,10 +731,16 @@
     @pl.loop(0, nt)
     def _(i):
         keep_keys(i, pick(w.kvb[0, tile(i), :], w.kvb[0, tile(flip(i)), :]), 0.0)
+
+    at("h", 2)
+    kvx.wait_recv()
+
+    @pl.loop(0, nt)
+    def _(i):
         keep_keys(nt + i, w.kvb[1, tile(i), :], jnp.where(lane == 64 + i // sub, 1.0, 0.0))
 
     w.acc[...] = jnp.zeros_like(w.acc)
-    dnx = rcopy(w.na, w.dnr, w.es.at[1], w.er.at[1], {"tp": 1 - t})
+    at("h", 3)
 
     def own_out(c, v):
         cols = pl.ds(pl.multiple_of(c * FC, FC), FC)
@@ -750,73 +760,98 @@
             w.GQ[p, :, to : to + 128] = v.astype(BF)
         rq.start(p)
 
-    def feed_forward():
-        @pl.loop(0, NC)
-        def _(c):
-            @pl.loop(0, nt)
-            def _(i):
-                hp = dot(w.nf[tile(i), :], w.G[c, :, 0:FC])
-                da = dot(w.cb[tile(i), :], w.G[c, :, FC : 2 * FC])
-                cdf = 0.5 + 0.5 * lax.erf(hp * 0.7071067811865476)
-                pdf = jnp.exp(-0.5 * hp * hp) * 0.3989422804014327
-                w.act[c, tile(i), :] = (hp * cdf).astype(BF)
-                w.dh[c, tile(i), :] = (da * (cdf + hp * pdf)).astype(BF)
-
-                @pl.when(i == 2)
-                def _():
-                    odd(c + 2)
-                    pl.when(c == 0)(lambda: rq.X(0))
-                    pl.when(c == 1)(lambda: rq.Y(0))
-                    pl.when(c == 2)(lambda: rq.Z(0, 1))
-                    pl.when(c == 3)(lambda: rq.Z(0, 2))
-                    pl.when(c >= 2)(lambda: r.X(c - 2))
-                    pl.when(c >= 3)(lambda: r.Y(c - 3))
-
-            @pl.loop(0, D // BQ)
-            def _(m):
-                w.GR[c, tile(m), 0:FC] = dot(w.nft[tile(m), :], w.dh[c]).astype(BF)
-                w.GR[c, tile(m), FC : 2 * FC] = dot(w.ct[tile(m), :], w.act[c]).astype(BF)
-
-            r.start(c)
-            even(c + 3)
-
+    def feed(c, part):
         @pl.loop(0, nt)
         def _(i):
-            dn = dot_nt(w.dh[0, tile(i), :], w.G[0, :, 0:FC])
-            br = dot_nt(w.act[0, tile(i), :], w.G[0, :, FC : 2 * FC])
-            for c in range(1, NC):
-                dn = dn + dot_nt(w.dh[c, tile(i), :], w.G[c, :, 0:FC])
-                br = br + dot_nt(w.act[c, tile(i), :], w.G[c, :, FC : 2 * FC])
-            w.na[tile(i), :] = dn.astype(BF)
-            w.act[0, tile(i), :] = br[:, :FC].astype(BF)
-            w.act[1, tile(i), :] = br[:, FC:].astype(BF)
-
-            @pl.when(i == 2)
-            def _():
-                rq.Z(0, 3)
-                rq.F(0)
-                r.X(2)
-                r.Y(1)
-
-        dnx.start()
-
-    def scatter_step(p, k):
-        def last(c):
-            r.Z(c, 3)
-            r.F(c)
-
-        def out(c):
-            own_out(c, r.G(c))
-
-        if p == 1:
-            todo = {0: [(r.Z, 0, 1), (pair_out, 0)], 1: [(r.X, 3), (r.Y, 2), (r.Z, 0, 2)], 2: [(last, 0), (r.Z, 1, 1)], 3: [(r.Y, 3), (r.Z, 1, 2), (out, 0)]}
-        else:
-            todo = {0: [(last, 1), (r.Z, 2, 1)], 1: [(rq.X, 1), (r.Z, 2, 2), (out, 1)], 2: [(rq.Y, 1), (last, 2), (r.Z, 3, 1)], 3: [(rq.Z, 1, 1), (r.Z, 3, 2), (out, 2)]}
-        for f, *a in todo[k]:
-            f(*a)
+            hp = dot(w.nf[tile(i), :], w.G[c, :, 0:FC])
+            da = dot(w.cb[tile(i), :], w.G[c, :, FC : 2 * FC])
+            cdf = 0.5 + 0.5 * lax.erf(hp * 0.7071067811865476)
+            pdf = jnp.exp(-0.5 * hp * hp) * 0.3989422804014327
+            w.act[c, tile(i), :] = (hp * cdf).astype(BF)
+            w.dh[c, tile(i), :] = (da * (cdf + hp * pdf)).astype(BF)
+            for j in range(nt):
+                pl.when(i == j)(functools.partial(part, "i", c, j))
+
+        @pl.loop(0, D // BQ)
+        def _(m):
+            w.GR[c, tile(m), 0:FC] = dot(w.nft[tile(m), :], w.dh[c]).astype(BF)
+            w.GR[c, tile(m), FC : 2 * FC] = dot(w.ct[tile(m), :], w.act[c]).astype(BF)
+            for j in range(2):
+                pl.when(m == j)(functools.partial(part, "m", c, j))
+
+        r.start(c)
+
+    def out(c):
+        own_out(c, r.G(c))
+
+    plan.update({
+        ("a", 2): [(r.Y, 0, 2, 2), (r.X, 1, 2, 2)],
+        ("b", 0): [(g.stage, 0, 5)],
+        ("b", 1): [(g.stage, 1, 5)],
+        ("b", 2): [(g.stage, 3, 3)],
+        ("b", 3): [(g.stage, 3, 5), (r.Z, 0, 2), (r.X, 2, 2, 2), (rq.Z, 0, 3)],
+        ("d", 0): [(r.Z, 1, 3), (r.F, 1), (r.Y, 3, 2, 2), (rq.Z, 1, 2)],
+        ("d", 1): [(r.Z, 3, 1), (rq.X, 2)],
+        ("d", 2): [(r.Z, 2, 2), (rq.Z, 1, 3), (rq.F, 1)],
+        ("i", 0, 0): [(g.stage, 3, 1)],
+        ("i", 0, 3): [(g.stage, 1, 4), (g.stage, 2, 3)],
+        ("i", 1, 0): [(g.stage, 3, 2), (rq.Y, 0)],
+        ("i", 2, 0): [(rq.Z, 0, 1)],
+        ("i", 2, 3): [(gq.stage, 2, 3), (r.X, 1, 0, 2), (rq.Z, 0, 2)],
+        ("i", 3, 2): [(r.Y, 1, 2, 2), (rq.F, 0)],
+        ("l", 0): [(r.Z, 3, 3)],
+        ("l", 1): [(r.F, 3)],
+        ("l", 2): [(rq.Z, 2, 2), (pair_out, 1)],
+        ("m", 0, 1): [(rq.X, 0)],
+        ("m", 1, 0): [(g.stage, 2, 4), (r.X, 0, 0, 2)],
+        ("m", 1, 1): [(gq.stage, 2, 2)],
+        ("m", 3, 0): [(r.Z, 0, 3)],
+        ("m", 3, 1): [(r.Z, 1, 1), (rq.X, 1)],
+        ("t", 0): [(r.F, 0), (r.Z, 3, 2), (rq.Y, 2), (rq.Z, 2, 1)],
+        ("t", 1): [(r.Z, 2, 3), (r.F, 2)],
+        ("t", 3): [(rq.Z, 2, 3), (rq.F, 2), (out, 0), (out, 1), (out, 2), (out, 3)],
+        ("t", 4): [(pair_out, 2)],
+        (0, 0, 0): [(g.own, 2)],
+        (0, 0, 1): [(gq.stage, 1, 2)],
+        (0, 1, 1): [(g.stage, 1, 1)],
+        (0, 2, 0): [(gq.stage, 1, 3), (g.stage, 0, 2)],
+        (0, 2, 1): [(g.stage, 2, 1)],
+        (0, 3, 0): [(g.stage, 1, 2), (g.own, 3)],
+        (0, 3, 1): [(gq.stage, 1, 4), (g.stage, 0, 3)],
+        (1, 0, 0): [(g.stage, 0, 4), (g.stage, 2, 2)],
+        (1, 1, 0): [(g.stage, 1, 3)],
+        (1, 2, 0): [(gq.stage, 2, 1)],
+        (1, 2, 1): [(r.X, 0, 2, 2)],
+        (1, 3, 0): [(g.stage, 2, 5), (r.Y, 0, 0, 2)],
+        (1, 3, 1): [(gq.stage, 2, 4), (g.stage, 3, 4), (r.Z, 0, 1)],
+        (2, 0, 0): [(r.Y, 1, 0, 2), (r.X, 2, 0, 2)],
+        (2, 0, 1): [(pair_out, 0)],
+        (2, 1, 0): [(r.Y, 2, 0, 2)],
+        (2, 2, 0): [(r.X, 3, 0, 2)],
+        (2, 2, 1): [(r.Z, 1, 2), (rq.Y, 1)],
+        (2, 3, 0): [(r.Y, 2, 2, 2)],
+        (2, 3, 1): [(r.Z, 2, 1), (r.X, 3, 2, 2), (r.Y, 3, 0, 2), (rq.Z, 1, 1)],
+    })
+
+    def chunks(these):
+        def part(*slot):
+            for cc in these:
+                if (slot[0], cc, *slot[2:]) in plan:
+                    pl.when(slot[1] == cc)(functools.partial(at, slot[0], cc, *slot[2:]))
+
+        def chunk(c):
+            part("b", c)
+            feed(c, part)
+            part("a", c)
+
+        pl.loop(these[0], these[-1] + 1)(chunk)
+
+    def tick(p, k, m):
+        for pp in range(npair):
+            if (pp, k, m) in plan:
+                pl.when(p == pp)(functools.partial(at, pp, k, m))
 
     def attention(p, k):
-        st = p * nt + k
         R = 2 * BQ
         b, rr = k // sub, k % sub
         spans = [(0, half, False)] if b else []
@@ -826,7 +861,7 @@
         for off, size, tri in spans:
             parts.append((slice(off, off + size), slice(at, at + size), tri))
             at += size
-        q, do = w.qx[st], w.dox[st]
+        q, do = w.qx[k], w.dox[k]
         m = None
         for ks, cs, tri in parts:
             sc = dot_nt(q, w.kx[ks, :])
@@ -853,8 +888,9 @@
         o = o * inv
         delta = jnp.sum(o * do.astype(F32), axis=1, keepdims=True)
         inv_row = jnp.transpose(jnp.broadcast_to(inv, (R, 128)))[:1, :]
-        qs = (w.qt[st].astype(F32) * inv_row).astype(BF)
-        dos = (w.dt[st].astype(F32) * inv_row).astype(BF)
+        qs = (w.qt[k].astype(F32) * inv_row).astype(BF)
+        dos = (w.dt[k].astype(F32) * inv_row).astype(BF)
+        tick(p, k, 1)
         dq = None
         for ks, cs, _ in parts:
             dp = dot_nt(do, w.v0[ks, :])
@@ -871,16 +907,19 @@
 
     @pl.loop(0, npair)
     def _(p):
-        @pl.when(p == 1)
-        def _():
-            pair_grads(0)
-            feed_forward()
-
-        pl.when(p == 2)(lambda: pair_grads(1))
+        for pp in range(1, npair):
+            pl.when(p == pp)(functools.partial(pair_grads, pp - 1))
+        project(p)
         for k in range(nt):
-            pl.when(p == 0)(lambda: (odd, even)[k % 2]((k + 1) // 2))
-            for pp in range(1, npair):
-                pl.when(p == pp)(functools.partial(scatter_step, pp, k))
+            tick(p, k, 0)
+            if k == 1:
+                pl.when(p == 1)(functools.partial(chunks, [0]))
+            if k == 2:
+                pl.when(p == 1)(functools.partial(chunks, [1]))
+            if k == 3:
+                pl.when(p == 1)(functools.partial(chunks, [2]))
+            if k == 0:
+                pl.when(p == 2)(functools.partial(chunks, [3]))
             attention(p, k)
 
     for b in (0, 1):
@@ -894,43 +933,52 @@
     w.dX[...] = (w.dS[1].astype(F32) + w.dR[1].astype(F32)).astype(BF)
     dxx = rcopy(w.dX, w.dXR, w.es.at[4], w.er.at[4], {"ctx": 1 - x})
     dxx.start()
-    r.Z(3, 3)
-    r.F(3)
-    rq.Z(1, 2)
-    dnx.wait_recv()
+
+    def dnx(i):
+        return rcopy(w.na.at[tile(i)], w.dnr.at[tile(i)], w.ts0.at[0, i], w.tr0.at[0, i], {"tp": 1 - t})
+
+    def brx(i):
+        return rcopy(w.act.at[pl.ds(0, 2), tile(i)], w.brr.at[:, tile(i)], w.ts0.at[1, i], w.tr0.at[1, i], {"tp": 1 - t})
+
+    def gax(i):
+        return rcopy(w.act.at[pl.ds(2, 2), tile(i)], w.gar.at[:, tile(i)], w.ts0.at[2, i], w.tr0.at[2, i], {"tp": 1 - t})
 
     @pl.loop(0, nt)
     def _(i):
-        br = dot_nt(pick(w.attd[tile(i), :], w.attd[tile(flip(i)), :]), w.G[QO, :, CA : 2 * CA])
-        w.act[0, tile(i), :] = (w.act[0, tile(i), :].astype(F32) + br[:, :FC]).astype(BF)
-        w.act[1, tile(i), :] = (w.act[1, tile(i), :].astype(F32) + br[:, FC:]).astype(BF)
-
-    brx = rcopy(w.act.at[pl.ds(0, 2)], w.dh.at[pl.ds(0, 2)], w.es.at[3], w.er.at[3], {"tp": 1 - t})
-    brx.start()
-    rq.X(2)
+        dn = dot_nt(w.dh[0, tile(i), :], w.G[0, :, 0:FC])
+        br = dot_nt(w.act[0, tile(i), :], w.G[0, :, FC : 2 * FC])
+        for c in range(1, NC):
+            dn = dn + dot_nt(w.dh[c, tile(i), :], w.G[c, :, 0:FC])
+            br = br + dot_nt(w.act[c, tile(i), :], w.G[c, :, FC : 2 * FC])
+        ga = None
+        for p in range(npair):
+            cols = slice(128 * p, 128 * p + 128)
+            gp = dot_nt(pick(w.gq[tile(i), cols], w.gq[tile(flip(i)), cols]), w.G[QO, :, 256 * p : 256 * p + 128])
+            ga = gp if ga is None else ga + gp
+            br = br + dot_nt(pick(w.attd[tile(i), cols], w.attd[tile(flip(i)), cols]), w.G[QO, :, 256 * p + 128 : 256 * p + 256])
+        w.na[tile(i), :] = dn.astype(BF)
+        for k, v in enumerate((br, ga)):
+            w.act[2 * k, tile(i), :] = v[:, :FC].astype(BF)
+            w.act[2 * k + 1, tile(i), :] = v[:, FC:].astype(BF)
+        brx(i).start()
+        gax(i).start()
+        dnx(i).start()
+        for j in range(nt):
+            pl.when(i == j)(functools.partial(at, "d", j))
+
+    at("t", 0)
 
     @pl.loop(0, nt)
     def _(i):
-        ga = dot_nt(pick(w.gq[tile(i), :], w.gq[tile(flip(i)), :]), w.G[QO, :, 0:CA])
-        w.act[2, tile(i), :] = ga[:, :FC].astype(BF)
-        w.act[3, tile(i), :] = ga[:, FC:].astype(BF)
-
-    gax = rcopy(w.act.at[pl.ds(2, 2)], w.dh.at[pl.ds(2, 2)], w.es.at[5], w.er.at[5], {"tp": 1 - t})
-    gax.start()
-    rq.Z(1, 3)
-    rq.F(1)
-    rq.Y(2)
-    brx.wait_recv()
-
-    @pl.loop(0, nt)
-    def _(i):
+        brx(i).wait_recv()
         for k in range(2):
             cs = slice(k * FC, (k + 1) * FC)
-            v = w.act[k, tile(i), :].astype(F32) + w.dh[k, tile(i), :].astype(F32)
+            v = w.act[k, tile(i), :].astype(F32) + w.brr[k, tile(i), :].astype(F32)
             w.nf[tile(i), cs] = (w.hb[tile(i), cs].astype(F32) + v).astype(BF)
 
     outx = pltpu.make_async_copy(w.nf, w.out_tokens, w.osem.at[1])
     outx.start()
+    at("t", 1)
     dxx.wait_recv()
 
     @pl.loop(0, nt)
@@ -947,8 +995,7 @@
     kvs = [rcopy(w.kvS.at[kv_rows(ps)], w.kvR.at[me], w.ks.at[i], w.kr.at[me], {"shard": ps, "ctx": px}) for i, (ps, px) in enumerate(peers)]
     for c in kvs:
         c.start()
-    rq.Z(2, 1)
-    gax.wait_recv()
+    at("t", 2)
     w.lg[...] = jnp.zeros_like(w.lg)
 
     def hgx(i):
@@ -956,9 +1003,11 @@
 
     @pl.loop(0, nt)
     def _(i):
+        gax(i).wait_recv()
+        dnx(i).wait_recv()
         xh, rstd = standardized(i)
-        kvg = dot_nt(w.gkb[tile(i), :], w.gkv[0])
-        gn = jnp.concatenate([w.act[k, tile(i), :].astype(F32) + w.dh[k, tile(i), :].astype(F32) for k in (2, 3)], axis=1) + kvg
+        kvg = dot_nt(w.gkb[tile(i), :], w.gkv[...])
+        gn = jnp.concatenate([w.act[2 + k, tile(i), :].astype(F32) + w.gar[k, tile(i), :].astype(F32) for k in (0, 1)], axis=1) + kvg
         gf = w.na[tile(i), :].astype(F32) + w.dnr[tile(i), :].astype(F32)
         e = gn * w.prm[0:1, :] + gf * w.prm[2:3, :]
         e = rstd * (e - jnp.mean(e, axis=1, keepdims=True) - xh * jnp.mean(e * xh, axis=1, keepdims=True))
@@ -968,7 +1017,8 @@
         w.lg[1:2, :] += jnp.sum(gn, axis=0, keepdims=True)
         w.lg[2:3, :] += jnp.sum(gf * xh, axis=0, keepdims=True)
         w.lg[3:4, :] += jnp.sum(gf, axis=0, keepdims=True)
-        pl.when(i == 2)(lambda: rq.Z(2, 2))
+        for j in range(nt):
+            pl.when(i == j)(functools.partial(at, "l", j))
 
     lg = w.lg[...]
     keep = lax.broadcasted_iota(jnp.int32, (8, 128), 1) < rows
@@ -978,10 +1028,7 @@
     lgs = [rcopy(w.lS.at[ps], w.lR.at[me], w.ls.at[i], w.lr.at[me], {"shard": ps, "ctx": px}) for i, (ps, px) in enumerate(peers)]
     for c in lgs:
         c.start()
-    rq.Z(2, 3)
-    rq.F(2)
-    own_out(3, r.G(3))
-    pair_out(1)
+    at("t", 3)
 
     def arrived(ref, sems, i, ps, px):
         k = px * n + ps
@@ -1006,14 +1053,16 @@
     rcopy(w.kvF.at[1 - t], w.kvF.at[1 - t], w.es.at[6], w.er.at[6], {"tp": 1 - t}).wait_recv()
     w.okv[0:hr, :] = w.kvF[0]
     w.okv[hr:rows, :] = w.kvF[1]
-    pair_out(2)
+    at("t", 4)
     kvo.wait()
     outx.wait()
     for i in range(nt):
         hgx(i).wait()
-    for c in lns + [kvx, dnx, dtp, brx, dxx, gax, kfx] + kvs + lgs:
+    for c in lns + kds + [kvx, dtp, dxx, kfx] + kvs + lgs:
         c.wait_send()
-    gk.finish(0)
+    for i in range(nt):
+        for f in (dnx, brx, gax):
+            f(i).wait_send()
     for c in range(npair):
         gq.finish(c)
         rq.finish(c)
@@ -1032,7 +1081,7 @@
     hr = rows // 2
     BQ = 256
     npair = CA // 128
-    ns = T // BQ * npair
+    nt = T // BQ
     A = pl.BlockSpec(memory_space=pl.ANY)
     V = pl.BlockSpec(memory_space=pltpu.VMEM)
     S = pl.BlockSpec(memory_space=pltpu.SMEM)
@@ -1048,20 +1097,20 @@
     f = lambda *sh: pltpu.VMEM(sh, F32)
     scr = {
         "hb": b(T, D), "cb": b(T, D), "ct": b(D, T), "na": b(T, D), "nf": b(T, D), "nft": b(D, T), "nat": b(D, T),
-        "G": b(NC + 1, D, 2 * FC), "gkv": b(1, D, CK), "GR": b(NC, D, 2 * FC), "GQ": b(npair, D, 256),
+        "G": b(NC + 1, D, 2 * FC), "gkv": b(D, CK), "GR": b(NC, D, 2 * FC), "GQ": b(npair, D, 256),
         "xb": b(NC, nz, hr, 2 * FC), "yb": b(NC, nz, hr, 2 * FC), "zb": b(NC, nz + 1, rows, 2 * FC), "fb": b(NC, 2, rows, 2 * FC),
         "xq": b(npair, nz, hr, 256), "yq": b(npair, nz, hr, 256), "zq": b(npair, nz + 1, rows, 256), "fq": b(npair, 2, rows, 256),
         "lb": f(n, 8, 128), "act": b(NC, T, FC), "dh": b(NC, T, FC), "dnr": b(T, D),
-        "qx": b(ns, 2 * BQ, 128), "dox": b(ns, 2 * BQ, 128), "qt": b(ns, 64, 2 * BQ), "dt": b(ns, 64, 2 * BQ),
+        "qx": b(nt, 2 * BQ, 128), "dox": b(nt, 2 * BQ, 128), "qt": b(nt, 64, 2 * BQ), "dt": b(nt, 64, 2 * BQ),
+        "brr": b(2, T, FC), "gar": b(2, T, FC), "ts0": Dm((3, nt)), "tr0": Dm((3, nt)), "gb0": Dm((n - 1,)), "gb1": Dm((n,)),
         "kvb": b(2, T, CK), "kx": b(2 * T, 128), "k0": b(2 * T, 128), "v0": b(2 * T, 128),
         "ss": f(2 * BQ, 2 * T), "ps": b(2 * BQ, 2 * T), "attd": b(T, CA), "gq": b(T, CA), "acc": f(128, 2 * T),
         "tc": f(T, 128), "ts": f(T, 128), "dS": b(2, 128, T), "dR": b(2, 128, T), "dX": b(128, T), "dXR": b(128, T), "gkb": b(T, 128),
         "kvS": b(D, CK), "kvR": b(2 * n, hr, CK), "kvF": f(2, hr, CK), "lS": f(n, 8, 128), "lR": f(2 * n, 8, 128), "prm": f(8, D), "lg": f(8, D), "hgs": f(T, D),
-        "lsem": Dm((5 + 2 * NC,)), "lns": Dm((n - 1,)), "lnr": Dm((n,)), "es": Dm((7,)), "er": Dm((7,)), "osem": Dm((2 + T // BQ,)),
+        "lsem": Dm((3 + 2 * npair + 2 * NC,)), "lns": Dm((n - 1,)), "lnr": Dm((n,)), "es": Dm((7,)), "er": Dm((7,)), "osem": Dm((2 + T // BQ,)),
         "ks": Dm((2 * n - 1,)), "kr": Dm((2 * n,)), "ls": Dm((2 * n - 1,)), "lr": Dm((2 * n,)),
     }
     scr.update({f"ga{i}": v for i, v in enumerate(Gather.sems(NC, nz))})
-    scr.update({f"gb{i}": v for i, v in enumerate(Gather.sems(1, nz))})
     scr.update({f"gc{i}": v for i, v in enumerate(Gather.sems(npair, nz))})
     scr.update({f"sc{i}": v for i, v in enumerate(Scatter.sems(NC, nz))})
     scr.update({f"sq{i}": v for i, v in enumerate(Scatter.sems(npair, nz))})
@@ -1092,8 +1141,9 @@
     for a, b in zip(ins, outs):
         a.wait()
         b.start()
-    k_o[...] = kv[:, :64]
-    v_o[...] = pltpu.roll(kv[...].astype(F32), 64, 1)[:, :64].astype(BF)
+    turned = kv[...].T
+    k_o[...] = turned[:64]
+    v_o[...] = turned[64:]
     for k, ref in enumerate((a_o, b_o, c_o, d_o)):
         ref[...] = lno[k, : ref.shape[0]]
     for a, b in ((oq, oq_o), (okv, okv_o), (oo, oo_o), (ou, ou_o), (od, od_o)):
@@ -1113,7 +1163,7 @@
     order = ("out_tokens", "hg", "kvout", "lno", "oq", "okv", "oo", "ou", "od")
     return pl.pallas_call(
         functools.partial(results_kernel, nt),
-        out_shape=(like("out_tokens"), sd((T, 64), BF), sd((T, 64), BF), like("hg")) + (sd((rows,), F32),) * 4 + tuple(like(k) for k in order[4:]),
+        out_shape=(like("out_tokens"), sd((64, T), BF), sd((64, T), BF), like("hg")) + (sd((rows,), F32),) * 4 + tuple(like(k) for k in order[4:]),
         in_specs=[A, A] + [V] * 7,
         out_specs=(A, V, V, A) + (V,) * 9,
         scratch_shapes=[pltpu.VMEM((T, D), BF), pltpu.VMEM((T, D), F32), Dm((2 * nt,)), Dm((2 * nt,))],
@@ -1133,7 +1183,7 @@
     lns = [a.reshape(1, rows) for a in (ln1_gain, ln1_bias, ln2_gain, ln2_bias)]
     v = block_call(block_order, freq, hidden.reshape(span, width), cotangent.reshape(span, width), lns, up_weight, down_weight, q_weight, o_weight, kv_weight, width // rows // NY, span // 2, 1)
     tok, keys, values, hg, a, b, c, d, oq, okv, oo, ou, od = results(v, rows)
-    return (tok[None], keys[None], values[None], hg[None], a, b, c, d, oq, okv, oo, ou, od)
+    return (tok[None], keys.T[None], values.T[None], hg[None], a, b, c, d, oq, okv, oo, ou, od)
 
 
 def solution(mesh):

time: 184 us -> 153 us (0.83)
  Pallas kernels: 180 us -> 152 us
  local copies, waits for them, and re-layouts: 3.45 us -> 0 us
    pallas_call x1, Pallas kernels: 173 us -> 145 us  [block_call(): pl.pallas_call(functools.partial(block_kernel, names, nz, NC, half, BQ),...]
    unnamed x2 -> x0, local copies, waits for them, and re-layouts: 3.45 us -> none
where the time goes in v4:
time: 153 us
  Pallas kernels  152 us (99%)
    pallas_call x1, Pallas kernels, block_call(): pl.pallas_call(functools.partial(block_kernel, names, nz, NC, half, BQ),...  145 us
    pallas_call x1, Pallas kernels, results(): pl.pallas_call(functools.partial(results_kernel, nt), out_shape=(like('ou...  6.52 us

profile of v4, /device:TPU:0, one launch (start us, length us, event | category | flops | bytes accessed | tf_op | source)
XLA Modules:
  0.0 152.5 jit_solution(1003486219242956762)
XLA Ops:
  0.6 145.2 %block.1 = (bf16[1024,768]{1,0:T(8,128)(2,1)}, bf16[1024,128]{1,0:T(8,128)(2,1)}, f32[1024,768]{1,0:T(8,128)}, f32[8,128]{1,0:T(8,128)}, f32[96,384]{1,0:T(8,128...) custom-call(s32[4]{0:T(128)} %refs_0_.1, ...), custom_call_target="tpu_custom_call" | custom-call | tf_op jit(solution)/shard_map/block/pallas_call | solution.py:1118
  145.8 6.5 %results.1 = (bf16[1024,768]{1,0:T(8,128)(2,1)}, bf16[64,1024]{1,0:T(8,128)(2,1)}, bf16[64,1024]{1,0:T(8,128)(2,1)}, f32[1024,768]{1,0:T(8,128)}, f32[96]{0:T(12...) custom-call(bf16[1024,768]{1,0:T(8,128)(2,1)} %get-tuple-element.35., ...), custom_call_target="tpu_custom_call" | custom-call | tf_op jit(solution)/shard_map/results/pallas_call | solution.py:1164

commit v5 on v4

--- a/solution.py
+++ b/solution.py
@@ -319,6 +319,7 @@
 
 
 NY = 2
+WHOLE = (3,)
 NEG = -1e30
 
 
@@ -365,8 +366,11 @@
         b = self.block(c, zz, self.y)
         return rcopy(b, b, self.zs.at[c, 1, zz], self.zr.at[c, zz], {"shard": (self.z - 1) * NY + self.y})
 
+    def direct(self, c):
+        return self.cols is not None or c in WHOLE
+
     def ycp(self, c, zz, yy, h):
-        b = self.half(c, zz, yy, h) if self.cols is None else self.block(c, zz, yy)
+        b = self.block(c, zz, yy) if self.direct(c) else self.half(c, zz, yy, h)
         return rcopy(b, b, self.ys.at[c, zz], self.yr.at[c, zz], {"shard": self.z * NY + 1 - self.y})
 
     def xcp(self, c, zz, h):
@@ -412,7 +416,7 @@
     def Y(self, c, d):
         def f(zz):
             self.ycp(c, zz, 1 - self.y, self.x).wait_recv()
-            if self.cols is None:
+            if not self.direct(c):
                 self.xcp(c, zz, self.x).start()
 
         self.each(d, f)
@@ -425,7 +429,7 @@
             self.Z(c, d)
         if d <= self.nz:
             self.Y(c, d - 1)
-        if d > 1 and self.cols is None:
+        if d > 1 and not self.direct(c):
             self.X(c, d - 2)
 
     def finish(self, c):
@@ -440,7 +444,7 @@
                     pl.when(both(ok, z > 0))(lambda: self.dn(c, zz).wait_send())
         for zz in range(nz):
             self.ycp(c, zz, self.y, self.x).wait_send()
-            if self.cols is None:
+            if not self.direct(c):
                 self.xcp(c, zz, self.x).wait_send()
 
     @staticmethod
@@ -664,9 +668,10 @@
         w.na[tile(i), :] = na
 
     plan = {
-        ("h", 0): [(gq.stage, 0, 1), (g.own, 1)],
-        ("h", 1): [(gq.stage, 0, 2), (g.own, 0)],
-        ("h", 2): [(gq.stage, 0, 3), (gq.stage, 0, 4), (gq.stage, 1, 1), (g.stage, 0, 1)],
+        ("h", 0): [(gq.stage, 0, 1)],
+        ("h", 1): [(g.own, 0)],
+        ("h", 2): [(gq.stage, 0, 2), (gq.stage, 1, 1), (g.own, 1)],
+        ("h", 3): [(gq.stage, 0, 3), (gq.stage, 0, 4), (gq.stage, 1, 2), (g.stage, 0, 1)],
     }
 
     def at(*slot):
@@ -785,52 +790,52 @@
         own_out(c, r.G(c))
 
     plan.update({
-        ("a", 2): [(r.Y, 0, 2, 2), (r.X, 1, 2, 2)],
+        ("a", 2): [(r.Y, 0, 2, 2)],
+        ("a", 3): [(rq.Z, 0, 2)],
         ("b", 0): [(g.stage, 0, 5)],
-        ("b", 1): [(g.stage, 1, 5)],
-        ("b", 2): [(g.stage, 3, 3)],
-        ("b", 3): [(g.stage, 3, 5), (r.Z, 0, 2), (r.X, 2, 2, 2), (rq.Z, 0, 3)],
-        ("d", 0): [(r.Z, 1, 3), (r.F, 1), (r.Y, 3, 2, 2), (rq.Z, 1, 2)],
-        ("d", 1): [(r.Z, 3, 1), (rq.X, 2)],
-        ("d", 2): [(r.Z, 2, 2), (rq.Z, 1, 3), (rq.F, 1)],
-        ("i", 0, 0): [(g.stage, 3, 1)],
-        ("i", 0, 3): [(g.stage, 1, 4), (g.stage, 2, 3)],
-        ("i", 1, 0): [(g.stage, 3, 2), (rq.Y, 0)],
-        ("i", 2, 0): [(rq.Z, 0, 1)],
-        ("i", 2, 3): [(gq.stage, 2, 3), (r.X, 1, 0, 2), (rq.Z, 0, 2)],
-        ("i", 3, 2): [(r.Y, 1, 2, 2), (rq.F, 0)],
-        ("l", 0): [(r.Z, 3, 3)],
-        ("l", 1): [(r.F, 3)],
-        ("l", 2): [(rq.Z, 2, 2), (pair_out, 1)],
-        ("m", 0, 1): [(rq.X, 0)],
-        ("m", 1, 0): [(g.stage, 2, 4), (r.X, 0, 0, 2)],
-        ("m", 1, 1): [(gq.stage, 2, 2)],
-        ("m", 3, 0): [(r.Z, 0, 3)],
-        ("m", 3, 1): [(r.Z, 1, 1), (rq.X, 1)],
-        ("t", 0): [(r.F, 0), (r.Z, 3, 2), (rq.Y, 2), (rq.Z, 2, 1)],
-        ("t", 1): [(r.Z, 2, 3), (r.F, 2)],
-        ("t", 3): [(rq.Z, 2, 3), (rq.F, 2), (out, 0), (out, 1), (out, 2), (out, 3)],
-        ("t", 4): [(pair_out, 2)],
-        (0, 0, 0): [(g.own, 2)],
-        (0, 0, 1): [(gq.stage, 1, 2)],
-        (0, 1, 1): [(g.stage, 1, 1)],
-        (0, 2, 0): [(gq.stage, 1, 3), (g.stage, 0, 2)],
-        (0, 2, 1): [(g.stage, 2, 1)],
-        (0, 3, 0): [(g.stage, 1, 2), (g.own, 3)],
-        (0, 3, 1): [(gq.stage, 1, 4), (g.stage, 0, 3)],
-        (1, 0, 0): [(g.stage, 0, 4), (g.stage, 2, 2)],
-        (1, 1, 0): [(g.stage, 1, 3)],
-        (1, 2, 0): [(gq.stage, 2, 1)],
-        (1, 2, 1): [(r.X, 0, 2, 2)],
-        (1, 3, 0): [(g.stage, 2, 5), (r.Y, 0, 0, 2)],
-        (1, 3, 1): [(gq.stage, 2, 4), (g.stage, 3, 4), (r.Z, 0, 1)],
-        (2, 0, 0): [(r.Y, 1, 0, 2), (r.X, 2, 0, 2)],
-        (2, 0, 1): [(pair_out, 0)],
-        (2, 1, 0): [(r.Y, 2, 0, 2)],
-        (2, 2, 0): [(r.X, 3, 0, 2)],
-        (2, 2, 1): [(r.Z, 1, 2), (rq.Y, 1)],
-        (2, 3, 0): [(r.Y, 2, 2, 2)],
-        (2, 3, 1): [(r.Z, 2, 1), (r.X, 3, 2, 2), (r.Y, 3, 0, 2), (rq.Z, 1, 1)],
+        ("b", 1): [(g.stage, 1, 5), (rq.Y, 0)],
+        ("b", 2): [(g.stage, 2, 5)],
+        ("b", 3): [(g.stage, 3, 4), (g.stage, 3, 5), (r.X, 2, 0, 2)],
+        ("d", 0): [(r.Z, 2, 2), (r.Y, 3, 2, 2), (out, 1)],
+        ("d", 1): [(r.Z, 0, 3), (r.Z, 3, 1), (rq.X, 2)],
+        ("d", 2): [(r.F, 0), (r.Z, 2, 3)],
+        ("d", 3): [(rq.Z, 1, 2), (rq.Y, 2)],
+        ("i", 0, 1): [(g.stage, 1, 4)],
+        ("i", 0, 2): [(gq.stage, 2, 2), (g.stage, 3, 1)],
+        ("i", 1, 0): [(r.X, 0, 0, 2)],
+        ("i", 1, 2): [(gq.stage, 2, 3)],
+        ("i", 2, 1): [(r.X, 1, 0, 2)],
+        ("i", 3, 0): [(r.Z, 0, 1)],
+        ("i", 3, 1): [(r.X, 2, 2, 2)],
+        ("i", 3, 3): [(r.Y, 1, 2, 2)],
+        ("l", 1): [(rq.Z, 2, 2)],
+        ("m", 1, 0): [(g.stage, 3, 2), (r.X, 0, 2, 2)],
+        ("m", 1, 1): [(g.stage, 2, 4)],
+        ("m", 2, 0): [(gq.stage, 2, 4)],
+        ("m", 2, 1): [(g.stage, 3, 3)],
+        ("m", 3, 1): [(r.Z, 1, 1)],
+        ("t", 0): [(r.Z, 3, 2)],
+        ("t", 1): [(r.F, 2), (rq.Z, 2, 1), (pair_out, 0)],
+        ("t", 2): [(rq.Z, 1, 3), (rq.F, 1)],
+        ("t", 3): [(r.Z, 3, 3), (r.F, 3), (rq.Z, 2, 3), (rq.F, 2), (out, 0), (out, 2), (pair_out, 1)],
+        ("t", 4): [(out, 3), (pair_out, 2)],
+        (0, 1, 0): [(g.stage, 1, 1), (g.own, 2)],
+        (0, 1, 1): [(gq.stage, 1, 3)],
+        (0, 2, 0): [(g.stage, 0, 2)],
+        (0, 2, 1): [(g.stage, 1, 2)],
+        (0, 3, 0): [(g.stage, 2, 1)],
+        (0, 3, 1): [(gq.stage, 1, 4), (g.stage, 0, 3), (g.own, 3)],
+        (1, 0, 0): [(gq.stage, 2, 1), (g.stage, 0, 4), (g.stage, 1, 3), (g.stage, 2, 2)],
+        (1, 1, 0): [(rq.X, 0)],
+        (1, 2, 0): [(g.stage, 2, 3)],
+        (1, 2, 1): [(r.Y, 0, 0, 2), (rq.Z, 0, 1)],
+        (1, 3, 1): [(r.X, 1, 2, 2), (r.Y, 1, 0, 2)],
+        (2, 0, 1): [(r.Y, 2, 0, 2), (rq.X, 1)],
+        (2, 1, 1): [(r.Z, 0, 2), (r.Z, 1, 2), (r.X, 3, 0, 2)],
+        (2, 2, 0): [(rq.Y, 1)],
+        (2, 2, 1): [(r.Y, 2, 2, 2), (r.X, 3, 2, 2)],
+        (2, 3, 0): [(r.Z, 2, 1), (r.Y, 3, 0, 2), (rq.Z, 0, 3), (rq.F, 0)],
+        (2, 3, 1): [(r.Z, 1, 3), (r.F, 1), (rq.Z, 1, 1)],
     })
 
     def chunks(these):
@@ -934,17 +939,25 @@
     dxx = rcopy(w.dX, w.dXR, w.es.at[4], w.er.at[4], {"ctx": 1 - x})
     dxx.start()
 
+    def part(i):
+        return tile(lax.rem(i, nt // 2))
+
     def dnx(i):
-        return rcopy(w.na.at[tile(i)], w.dnr.at[tile(i)], w.ts0.at[0, i], w.tr0.at[0, i], {"tp": 1 - t})
+        return rcopy(w.na.at[tile(i)], w.dnr.at[part(i)], w.ts0.at[0, i], w.tr0.at[0, i], {"tp": 1 - t})
 
     def brx(i):
-        return rcopy(w.act.at[pl.ds(0, 2), tile(i)], w.brr.at[:, tile(i)], w.ts0.at[1, i], w.tr0.at[1, i], {"tp": 1 - t})
+        return rcopy(w.act.at[pl.ds(0, 2), tile(i)], w.brr.at[:, part(i)], w.ts0.at[1, i], w.tr0.at[1, i], {"tp": 1 - t})
 
     def gax(i):
-        return rcopy(w.act.at[pl.ds(2, 2), tile(i)], w.gar.at[:, tile(i)], w.ts0.at[2, i], w.tr0.at[2, i], {"tp": 1 - t})
+        return rcopy(w.act.at[pl.ds(2, 2), tile(i)], w.gar.at[:, part(i)], w.ts0.at[2, i], w.tr0.at[2, i], {"tp": 1 - t})
+
+    ht = nt // 2
+    ours = pl.ds(pl.multiple_of(t * (T // 2), BQ), T // 2)
+    theirs = pl.ds(pl.multiple_of((1 - t) * (T // 2), BQ), T // 2)
 
     @pl.loop(0, nt)
-    def _(i):
+    def _(step):
+        i = lax.rem(step + (1 - t) * ht, nt)
         dn = dot_nt(w.dh[0, tile(i), :], w.G[0, :, 0:FC])
         br = dot_nt(w.act[0, tile(i), :], w.G[0, :, FC : 2 * FC])
         for c in range(1, NC):
@@ -960,24 +973,34 @@
         for k, v in enumerate((br, ga)):
             w.act[2 * k, tile(i), :] = v[:, :FC].astype(BF)
             w.act[2 * k + 1, tile(i), :] = v[:, FC:].astype(BF)
-        brx(i).start()
-        gax(i).start()
-        dnx(i).start()
+
+        @pl.when(step < ht)
+        def _():
+            brx(i).start()
+            gax(i).start()
+            dnx(i).start()
+
         for j in range(nt):
-            pl.when(i == j)(functools.partial(at, "d", j))
+            pl.when(step == j)(functools.partial(at, "d", j))
 
     at("t", 0)
 
-    @pl.loop(0, nt)
-    def _(i):
+    @pl.loop(0, ht)
+    def _(j):
+        i = t * ht + j
         brx(i).wait_recv()
         for k in range(2):
             cs = slice(k * FC, (k + 1) * FC)
-            v = w.act[k, tile(i), :].astype(F32) + w.brr[k, tile(i), :].astype(F32)
+            v = w.act[k, tile(i), :].astype(F32) + w.brr[k, tile(j), :].astype(F32)
             w.nf[tile(i), cs] = (w.hb[tile(i), cs].astype(F32) + v).astype(BF)
 
-    outx = pltpu.make_async_copy(w.nf, w.out_tokens, w.osem.at[1])
+    outx = pltpu.make_async_copy(w.nf.at[ours], w.out_tokens.at[ours], w.osem.at[1])
     outx.start()
+
+    def outr(rows):
+        return rcopy(w.nf.at[rows], w.out_tokens.at[rows], w.es.at[1], w.er.at[1], {"tp": 1 - t})
+
+    outr(ours).start()
     at("t", 1)
     dxx.wait_recv()
 
@@ -999,26 +1022,31 @@
     w.lg[...] = jnp.zeros_like(w.lg)
 
     def hgx(i):
-        return pltpu.make_async_copy(w.hgs.at[tile(i)], w.hg.at[tile(i)], w.osem.at[2 + i])
-
-    @pl.loop(0, nt)
-    def _(i):
+        return pltpu.make_async_copy(w.hgs.at[part(i)], w.hg.at[tile(i)], w.osem.at[2 + i])
+
+    def hgr(i):
+        return rcopy(w.hgs.at[part(i)], w.hg.at[tile(i)], w.ts0.at[3, i], w.tr0.at[3, i], {"tp": 1 - t})
+
+    @pl.loop(0, ht)
+    def _(j):
+        i = t * ht + j
         gax(i).wait_recv()
         dnx(i).wait_recv()
         xh, rstd = standardized(i)
         kvg = dot_nt(w.gkb[tile(i), :], w.gkv[...])
-        gn = jnp.concatenate([w.act[2 + k, tile(i), :].astype(F32) + w.gar[k, tile(i), :].astype(F32) for k in (0, 1)], axis=1) + kvg
-        gf = w.na[tile(i), :].astype(F32) + w.dnr[tile(i), :].astype(F32)
+        gn = jnp.concatenate([w.act[2 + k, tile(i), :].astype(F32) + w.gar[k, tile(j), :].astype(F32) for k in (0, 1)], axis=1) + kvg
+        gf = w.na[tile(i), :].astype(F32) + w.dnr[tile(j), :].astype(F32)
         e = gn * w.prm[0:1, :] + gf * w.prm[2:3, :]
         e = rstd * (e - jnp.mean(e, axis=1, keepdims=True) - xh * jnp.mean(e * xh, axis=1, keepdims=True))
-        w.hgs[tile(i), :] = w.cb[tile(i), :].astype(F32) + e
+        w.hgs[tile(j), :] = w.cb[tile(i), :].astype(F32) + e
         hgx(i).start()
+        hgr(i).start()
         w.lg[0:1, :] += jnp.sum(gn * xh, axis=0, keepdims=True)
         w.lg[1:2, :] += jnp.sum(gn, axis=0, keepdims=True)
         w.lg[2:3, :] += jnp.sum(gf * xh, axis=0, keepdims=True)
         w.lg[3:4, :] += jnp.sum(gf, axis=0, keepdims=True)
-        for j in range(nt):
-            pl.when(i == j)(functools.partial(at, "l", j))
+        for k in range(ht):
+            pl.when(j == k)(functools.partial(at, "l", k))
 
     lg = w.lg[...]
     keep = lax.broadcasted_iota(jnp.int32, (8, 128), 1) < rows
@@ -1049,20 +1077,27 @@
     v = w.lR[0]
     for k in range(1, 2 * n):
         v = v + w.lR[k]
-    w.lno[...] = v
+    w.lF[t] = v
+    lfx = rcopy(w.lF.at[t], w.lF.at[t], w.es.at[3], w.er.at[3], {"tp": 1 - t})
+    lfx.start()
     rcopy(w.kvF.at[1 - t], w.kvF.at[1 - t], w.es.at[6], w.er.at[6], {"tp": 1 - t}).wait_recv()
     w.okv[0:hr, :] = w.kvF[0]
     w.okv[hr:rows, :] = w.kvF[1]
     at("t", 4)
+    rcopy(w.lF.at[1 - t], w.lF.at[1 - t], w.es.at[3], w.er.at[3], {"tp": 1 - t}).wait_recv()
+    w.lno[...] = w.lF[0] + w.lF[1]
     kvo.wait()
     outx.wait()
-    for i in range(nt):
-        hgx(i).wait()
-    for c in lns + kds + [kvx, dtp, dxx, kfx] + kvs + lgs:
+    outr(theirs).wait_recv()
+    for j in range(ht):
+        hgx(t * ht + j).wait()
+        hgr((1 - t) * ht + j).wait_recv()
+    for c in lns + kds + [kvx, dtp, dxx, kfx, lfx, outr(ours)] + kvs + lgs:
         c.wait_send()
-    for i in range(nt):
+    for j in range(ht):
         for f in (dnx, brx, gax):
-            f(i).wait_send()
+            f((1 - t) * ht + j).wait_send()
+        hgr(t * ht + j).wait_send()
     for c in range(npair):
         gq.finish(c)
         rq.finish(c)
@@ -1100,13 +1135,13 @@
         "G": b(NC + 1, D, 2 * FC), "gkv": b(D, CK), "GR": b(NC, D, 2 * FC), "GQ": b(npair, D, 256),
         "xb": b(NC, nz, hr, 2 * FC), "yb": b(NC, nz, hr, 2 * FC), "zb": b(NC, nz + 1, rows, 2 * FC), "fb": b(NC, 2, rows, 2 * FC),
         "xq": b(npair, nz, hr, 256), "yq": b(npair, nz, hr, 256), "zq": b(npair, nz + 1, rows, 256), "fq": b(npair, 2, rows, 256),
-        "lb": f(n, 8, 128), "act": b(NC, T, FC), "dh": b(NC, T, FC), "dnr": b(T, D),
+        "lb": f(n, 8, 128), "act": b(NC, T, FC), "dh": b(NC, T, FC), "dnr": b(T // 2, D),
         "qx": b(nt, 2 * BQ, 128), "dox": b(nt, 2 * BQ, 128), "qt": b(nt, 64, 2 * BQ), "dt": b(nt, 64, 2 * BQ),
-        "brr": b(2, T, FC), "gar": b(2, T, FC), "ts0": Dm((3, nt)), "tr0": Dm((3, nt)), "gb0": Dm((n - 1,)), "gb1": Dm((n,)),
+        "brr": b(2, T // 2, FC), "gar": b(2, T // 2, FC), "ts0": Dm((4, nt)), "tr0": Dm((4, nt)), "lF": f(2, 8, 128), "gb0": Dm((n - 1,)), "gb1": Dm((n,)),
         "kvb": b(2, T, CK), "kx": b(2 * T, 128), "k0": b(2 * T, 128), "v0": b(2 * T, 128),
         "ss": f(2 * BQ, 2 * T), "ps": b(2 * BQ, 2 * T), "attd": b(T, CA), "gq": b(T, CA), "acc": f(128, 2 * T),
         "tc": f(T, 128), "ts": f(T, 128), "dS": b(2, 128, T), "dR": b(2, 128, T), "dX": b(128, T), "dXR": b(128, T), "gkb": b(T, 128),
-        "kvS": b(D, CK), "kvR": b(2 * n, hr, CK), "kvF": f(2, hr, CK), "lS": f(n, 8, 128), "lR": f(2 * n, 8, 128), "prm": f(8, D), "lg": f(8, D), "hgs": f(T, D),
+        "kvS": b(D, CK), "kvR": b(2 * n, hr, CK), "kvF": f(2, hr, CK), "lS": f(n, 8, 128), "lR": f(2 * n, 8, 128), "prm": f(8, D), "lg": f(8, D), "hgs": f(T // 2, D),
         "lsem": Dm((3 + 2 * npair + 2 * NC,)), "lns": Dm((n - 1,)), "lnr": Dm((n,)), "es": Dm((7,)), "er": Dm((7,)), "osem": Dm((2 + T // BQ,)),
         "ks": Dm((2 * n - 1,)), "kr": Dm((2 * n,)), "ls": Dm((2 * n - 1,)), "lr": Dm((2 * n,)),
     }
@@ -1127,28 +1162,32 @@
     return dict(zip(outs, res))
 
 
-def results_kernel(nt, tok, hg, kv, lno, oq, okv, oo, ou, od, tok_o, k_o, v_o, hg_o, a_o, b_o, c_o, d_o, oq_o, okv_o, oo_o, ou_o, od_o, tb, hb, sin, sout):
+def results_kernel(nt, tok, hg, kv, lno, oq, okv, oo, ou, od, tok_o, k_o, v_o, hg_o, a_o, b_o, c_o, d_o, oq_o, okv_o, oo_o, ou_o, od_o, tb, hb, kb, kt, lb, b0, b1, b2, b3, b4, sin, sout):
     BQ = tok.shape[0] // nt
     moves = []
     for i in range(nt):
         t = pl.ds(i * BQ, BQ)
         moves.append((hg.at[t], hb.at[t], hg_o.at[t]))
         moves.append((tok.at[t], tb.at[t], tok_o.at[t]))
+    moves += [(ou, b3, ou_o), (od, b4, od_o), (oq, b0, oq_o), (oo, b2, oo_o), (okv, b1, okv_o)]
+    n = len(moves)
     ins = [pltpu.make_async_copy(a, b, sin.at[i]) for i, (a, b, _) in enumerate(moves)]
     outs = [pltpu.make_async_copy(b, c, sout.at[i]) for i, (_, b, c) in enumerate(moves)]
-    for c in ins:
+    small = [pltpu.make_async_copy(kv, kb, sin.at[n]), pltpu.make_async_copy(lno, lb, sin.at[n + 1])]
+    turned = [pltpu.make_async_copy(kt.at[pl.ds(0, 64)], k_o, sout.at[n]), pltpu.make_async_copy(kt.at[pl.ds(64, 64)], v_o, sout.at[n + 1])]
+    for c in small + ins:
         c.start()
+    for c in small:
+        c.wait()
+    kt[...] = kb[...].T
+    for c in turned:
+        c.start()
+    for k, ref in enumerate((a_o, b_o, c_o, d_o)):
+        ref[...] = lb[k, : ref.shape[0]]
     for a, b in zip(ins, outs):
         a.wait()
         b.start()
-    turned = kv[...].T
-    k_o[...] = turned[:64]
-    v_o[...] = turned[64:]
-    for k, ref in enumerate((a_o, b_o, c_o, d_o)):
-        ref[...] = lno[k, : ref.shape[0]]
-    for a, b in ((oq, oq_o), (okv, okv_o), (oo, oo_o), (ou, ou_o), (od, od_o)):
-        b[...] = a[...]
-    for c in outs:
+    for c in outs + turned:
         c.wait()
 
 
@@ -1158,15 +1197,16 @@
     V = pl.BlockSpec(memory_space=pltpu.VMEM)
     sd = jax.ShapeDtypeStruct
     like = lambda k: sd(v[k].shape, v[k].dtype)
+    vm = lambda k: pltpu.VMEM(v[k].shape, v[k].dtype)
     nt = 4
     Dm = pltpu.SemaphoreType.DMA
     order = ("out_tokens", "hg", "kvout", "lno", "oq", "okv", "oo", "ou", "od")
     return pl.pallas_call(
         functools.partial(results_kernel, nt),
         out_shape=(like("out_tokens"), sd((64, T), BF), sd((64, T), BF), like("hg")) + (sd((rows,), F32),) * 4 + tuple(like(k) for k in order[4:]),
-        in_specs=[A, A] + [V] * 7,
-        out_specs=(A, V, V, A) + (V,) * 9,
-        scratch_shapes=[pltpu.VMEM((T, D), BF), pltpu.VMEM((T, D), F32), Dm((2 * nt,)), Dm((2 * nt,))],
+        in_specs=[A] * 9,
+        out_specs=(A,) * 4 + (V,) * 4 + (A,) * 5,
+        scratch_shapes=[vm("out_tokens"), vm("hg"), vm("kvout"), pltpu.VMEM((128, T), BF), vm("lno")] + [vm(k) for k in order[4:]] + [Dm((2 * nt + 7,)), Dm((2 * nt + 7,))],
         name="results",
     )(*[v[k] for k in order])
 

time: 153 us -> 148 us (0.967)
  Pallas kernels: 152 us -> 147 us
    pallas_call x1, Pallas kernels: 145 us -> 140 us  [block_call(): pl.pallas_call(functools.partial(block_kernel, names, nz, NC, half, BQ),...]
where the time goes in v5:
time: 148 us
  Pallas kernels  147 us (99%)
    pallas_call x1, Pallas kernels, block_call(): pl.pallas_call(functools.partial(block_kernel, names, nz, NC, half, BQ),...  140 us
    pallas_call x1, Pallas kernels, results(): pl.pallas_call(functools.partial(results_kernel, nt), out_shape=(like('ou...  6.22 us

profile of v5, /device:TPU:0, one launch (start us, length us, event | category | flops | bytes accessed | tf_op | source)
XLA Modules:
  0.0 147.5 jit_solution(5390607408661361421)
XLA Ops:
  0.6 140.5 %block.1 = (bf16[1024,768]{1,0:T(8,128)(2,1)}, bf16[1024,128]{1,0:T(8,128)(2,1)}, f32[1024,768]{1,0:T(8,128)}, f32[8,128]{1,0:T(8,128)}, f32[96,384]{1,0:T(8,128...) custom-call(s32[4]{0:T(128)} %refs_0_.1, ...), custom_call_target="tpu_custom_call" | custom-call | tf_op jit(solution)/shard_map/block/pallas_call | solution.py:1153
  141.1 6.2 %results.1 = (bf16[1024,768]{1,0:T(8,128)(2,1)}, bf16[64,1024]{1,0:T(8,128)(2,1)}, bf16[64,1024]{1,0:T(8,128)(2,1)}, f32[1024,768]{1,0:T(8,128)}, f32[96]{0:T(12...) custom-call(bf16[1024,768]{1,0:T(8,128)(2,1)} %get-tuple-element.35., ...), custom_call_target="tpu_custom_call" | custom-call | tf_op jit(solution)/shard_map/results/pallas_call | solution.py:1204
